TPU v7x, 32 devices: a whole 2x2x4 slice. The times are simulated.
32 devices in a mesh: fsdp: 2 (over x), ctx: 4 (over z), tp: 4 (over y, core).
Axes of the slice: x: 2, y: 2, z: 4, core: 2. Of those that a mesh axis runs over, the one named last changes fastest.
Arguments:
- tokens: bfloat16 [4, 1024, 2048], P('fsdp', 'ctx'), may hold values from -36 to 36
- cotangent: bfloat16 [4, 1024, 2048], P('fsdp', 'ctx'), may hold values from -9 to 9
- lengths: int32 [4, 2], P('fsdp'), may hold values from 1 to 768, 1024 in all within a row
- deal: int32 [4, 1024], P('fsdp'), may hold values from 0 to 1023, each once within a row
- att_proj: float32 [3, 2048, 2048], P(None, ('fsdp', 'ctx'), 'tp'), may hold values from -0.125 to 0.125
- attn_out: float32 [2048, 2048], P(('fsdp', 'ctx'), 'tp'), may hold values from -0.75 to 0.75
- ff_proj: float32 [2, 2048, 8192], P(None, ('fsdp', 'ctx'), 'tp'), may hold values from -0.125 to 0.125
- ff_out: float32 [2048, 8192], P(('fsdp', 'ctx'), 'tp'), may hold values from -0.0625 to 0.0625
- att_proj_first: float32 [3, 2048, 2048], P(None, ('fsdp', 'ctx'), 'tp')
- attn_out_first: float32 [2048, 2048], P(('fsdp', 'ctx'), 'tp')
- ff_proj_first: float32 [2, 2048, 8192], P(None, ('fsdp', 'ctx'), 'tp')
- ff_out_first: float32 [2048, 8192], P(('fsdp', 'ctx'), 'tp')
- att_proj_second: float32 [3, 2048, 2048], P(None, ('fsdp', 'ctx'), 'tp'), as said below
- attn_out_second: float32 [2048, 2048], P(('fsdp', 'ctx'), 'tp'), as said below
- ff_proj_second: float32 [2, 2048, 8192], P(None, ('fsdp', 'ctx'), 'tp'), as said below
- ff_out_second: float32 [2048, 8192], P(('fsdp', 'ctx'), 'tp'), as said below
Outputs:
- block_out: bfloat16 [4, 1024, 2048], P('fsdp', 'ctx')
- input_grad: float32 [4, 1024, 2048], P('fsdp', 'ctx')
- grad_norm: float32 [1], replicated
- att_proj_grad: float32 [3, 2048, 2048], P(None, ('fsdp', 'ctx'), 'tp')
- attn_out_grad: float32 [2048, 2048], P(('fsdp', 'ctx'), 'tp')
- ff_proj_grad: float32 [2, 2048, 8192], P(None, ('fsdp', 'ctx'), 'tp')
- ff_out_grad: float32 [2048, 8192], P(('fsdp', 'ctx'), 'tp')
- att_proj_first_new: float32 [3, 2048, 2048], P(None, ('fsdp', 'ctx'), 'tp')
- attn_out_first_new: float32 [2048, 2048], P(('fsdp', 'ctx'), 'tp')
- ff_proj_first_new: float32 [2, 2048, 8192], P(None, ('fsdp', 'ctx'), 'tp')
- ff_out_first_new: float32 [2048, 8192], P(('fsdp', 'ctx'), 'tp')
- att_proj_second_new: float32 [3, 2048, 2048], P(None, ('fsdp', 'ctx'), 'tp')
- attn_out_second_new: float32 [2048, 2048], P(('fsdp', 'ctx'), 'tp')
- ff_proj_second_new: float32 [2, 2048, 8192], P(None, ('fsdp', 'ctx'), 'tp')
- ff_out_second_new: float32 [2048, 8192], P(('fsdp', 'ctx'), 'tp')
- att_proj_new: float32 [3, 2048, 2048], P(None, ('fsdp', 'ctx'), 'tp')
- attn_out_new: float32 [2048, 2048], P(('fsdp', 'ctx'), 'tp')
- ff_proj_new: float32 [2, 2048, 8192], P(None, ('fsdp', 'ctx'), 'tp')
- ff_out_new: float32 [2048, 8192], P(('fsdp', 'ctx'), 'tp')
- att_proj_low: bfloat16 [3, 2048, 2048], P(None, ('fsdp', 'ctx'), 'tp')
- attn_out_low: bfloat16 [2048, 2048], P(('fsdp', 'ctx'), 'tp')
- ff_proj_low: bfloat16 [2, 2048, 8192], P(None, ('fsdp', 'ctx'), 'tp')
- ff_out_low: bfloat16 [2048, 8192], P(('fsdp', 'ctx'), 'tp')
Inputs may be any that keep to these rules, and one draw needn't show every extreme that they name: `lengths`: each row sums to 1024 and no entry exceeds 768. `deal`: each row is a permutation of the positions of its pack. `att_proj_second`: every entry is positive. `attn_out_second`: every entry is positive. `ff_proj_second`: every entry is positive. `ff_out_second`: every entry is positive.
All inputs are finite; a program needn't handle non-finite values.
Results may differ from a plain program's by a relative error of at most 0.017.
Values may be sent and summed in bfloat16 or wider, within the bound.
A program may use at most 320 MiB of HBM per device.

v0:
```python
import jax
import jax.numpy as jnp
from jax import lax
from jax.sharding import PartitionSpec as P

D = 2048
HEAD_DIM = 128
STEP = 10


EPS_NORM = 1e-05
BETA_ONE = 0.9
BETA_TWO = 0.95
EPS_ADAM = 1e-08
DECAY = 0.1
MAX_NORM = 1.0
NEG_FILL = -1e30


def layer_norm(values):
    centre = values - jnp.mean(values, axis=-1, keepdims=True)
    spread = jnp.mean(centre * centre, axis=-1, keepdims=True)
    return centre * lax.rsqrt(spread + EPS_NORM)


def rotary(values, cos_table, sine_table):
    half_dim = values.shape[-1] // 2
    turned = jnp.concatenate([-values[..., half_dim:], values[..., :half_dim]], axis=-1)
    return values * cos_table + turned * sine_table


def rope_tables(places):
    freq_steps = jnp.arange(HEAD_DIM // 2, dtype=jnp.float32)
    inverse = jnp.power(10000.0, -2.0 * freq_steps / HEAD_DIM)
    angles = places.astype(jnp.float32)[:, None] * inverse[None, :]
    doubled = jnp.concatenate([angles, angles], axis=1)
    return (jnp.cos(doubled)[:, None, :], jnp.sin(doubled)[:, None, :])


def first_positions(deal_row, length_row):
    seq_ends = jnp.cumsum(length_row)
    starts = seq_ends - length_row
    inside = (deal_row[:, None] >= starts[None, :]) & (deal_row[:, None] < seq_ends[None, :])
    return jnp.sum(jnp.where(inside, starts[None, :], 0), axis=1)


def swiglu(gate_up):
    return gate_up[1] * jax.nn.sigmoid(gate_up[1]) * gate_up[0]


def adam_step(weight, grad_sum, first, second, clip_factor, learn_rate):
    clipped = grad_sum * clip_factor
    first_new = BETA_ONE * first + (1.0 - BETA_ONE) * clipped
    second_new = BETA_TWO * second + (1.0 - BETA_TWO) * clipped * clipped
    first_hat = first_new / (1.0 - BETA_ONE**STEP)
    second_hat = second_new / (1.0 - BETA_TWO**STEP)
    weight_new = weight - learn_rate * (
        first_hat / (jnp.sqrt(second_hat) + EPS_ADAM) + DECAY * weight
    )
    return (first_new, second_new, weight_new)


def tensor_sum(partial_sum):
    return lax.psum(partial_sum, "tp")


def gather_weights(att_proj, attn_out, ff_proj, ff_out):
    att_full, proj_full = (
        lax.all_gather(att_proj.astype(jnp.bfloat16), ("fsdp", "ctx"), axis=1, tiled=True),
        lax.all_gather(ff_proj.astype(jnp.bfloat16), ("fsdp", "ctx"), axis=1, tiled=True),
    )
    out_full, down_full = (
        lax.all_gather(attn_out.astype(jnp.bfloat16), ("fsdp", "ctx"), axis=0, tiled=True),
        lax.all_gather(ff_out.astype(jnp.bfloat16), ("fsdp", "ctx"), axis=0, tiled=True),
    )
    return (att_full, out_full, proj_full, down_full)


def reduce_grads(att_grad, out_grad, proj_grad, down_grad):
    att_part, proj_part = (
        lax.psum_scatter(
            att_grad.astype(jnp.bfloat16), ("fsdp", "ctx"), scatter_dimension=1, tiled=True
        ).astype(jnp.float32),
        lax.psum_scatter(
            proj_grad.astype(jnp.bfloat16), ("fsdp", "ctx"), scatter_dimension=1, tiled=True
        ).astype(jnp.float32),
    )
    out_part, down_part = (
        lax.psum_scatter(
            out_grad.astype(jnp.bfloat16), ("fsdp", "ctx"), scatter_dimension=0, tiled=True
        ).astype(jnp.float32),
        lax.psum_scatter(
            down_grad.astype(jnp.bfloat16), ("fsdp", "ctx"), scatter_dimension=0, tiled=True
        ).astype(jnp.float32),
    )
    return (att_part, out_part, proj_part, down_part)


def micro_step(resid_in, grad_out, deal_row, length_row, weights, ctx_index):
    att_full, out_full, proj_full, down_full = weights
    row_count = resid_in.shape[0]
    head_width = att_full.shape[2]
    local_heads = head_width // HEAD_DIM
    score_scale = HEAD_DIM ** (-0.5)
    key_first = first_positions(deal_row, length_row)
    query_place = lax.dynamic_slice_in_dim(deal_row, ctx_index * row_count, row_count)
    query_first = lax.dynamic_slice_in_dim(key_first, ctx_index * row_count, row_count)
    allowed = (deal_row[None, :] <= query_place[:, None]) & (
        deal_row[None, :] >= query_first[:, None]
    )
    cos_table, sine_table = rope_tables(query_place - query_first)
    normed_one, norm_one_pull = jax.vjp(layer_norm, resid_in)
    act_one = normed_one.astype(jnp.bfloat16)
    joint_qkv = jnp.einsum("td,cdf->ctf", act_one, att_full, preferred_element_type=jnp.float32)

    def turn_pair(query_raw, key_raw):
        return (rotary(query_raw, cos_table, sine_table), rotary(key_raw, cos_table, sine_table))

    (query_rot, key_rot), turn_pull = jax.vjp(
        turn_pair,
        joint_qkv[0].reshape(row_count, local_heads, HEAD_DIM),
        joint_qkv[1].reshape(row_count, local_heads, HEAD_DIM),
    )
    query_low = query_rot.astype(jnp.bfloat16)
    key_low = key_rot.reshape(row_count, head_width).astype(jnp.bfloat16)
    value_low = joint_qkv[2].astype(jnp.bfloat16)
    keys_flat, values_flat = (
        lax.all_gather(key_low, "ctx", axis=0, tiled=True),
        lax.all_gather(value_low, "ctx", axis=0, tiled=True),
    )
    pack_len = keys_flat.shape[0]
    keys_all = keys_flat.reshape(pack_len, local_heads, HEAD_DIM)
    values_all = values_flat.reshape(pack_len, local_heads, HEAD_DIM)

    def scores_of():
        raw_scores = (
            jnp.einsum("thd,khd->htk", query_low, keys_all, preferred_element_type=jnp.float32)
            * score_scale
        )
        return jnp.where(allowed[None], raw_scores, NEG_FILL)

    scores = scores_of()
    row_peak = jnp.max(scores, axis=2, keepdims=True)
    exp_scores = jnp.exp(scores - row_peak)
    row_mass = jnp.sum(exp_scores, axis=2, keepdims=True)
    log_mass = row_peak + jnp.log(row_mass)
    attended = jnp.einsum(
        "htk,khd->thd",
        (exp_scores / row_mass).astype(jnp.bfloat16),
        values_all,
        preferred_element_type=jnp.float32,
    )
    attended_low = attended.reshape(row_count, head_width).astype(jnp.bfloat16)
    attn_branch = tensor_sum(
        jnp.einsum("tf,df->td", attended_low, out_full, preferred_element_type=jnp.float32)
    )
    resid_mid = resid_in + attn_branch
    normed_two, norm_two_pull = jax.vjp(layer_norm, resid_mid)
    act_two = normed_two.astype(jnp.bfloat16)
    gate_up = jnp.einsum("td,cdf->ctf", act_two, proj_full, preferred_element_type=jnp.float32)
    hidden, glu_pull = jax.vjp(swiglu, gate_up)
    hidden_low = hidden.astype(jnp.bfloat16)
    ff_branch = tensor_sum(
        jnp.einsum("tf,df->td", hidden_low, down_full, preferred_element_type=jnp.float32)
    )
    block_rows = (resid_mid + ff_branch).astype(jnp.bfloat16)
    down_grad = jnp.einsum("td,tf->df", grad_out, hidden_low, preferred_element_type=jnp.float32)
    hidden_grad = jnp.einsum("td,df->tf", grad_out, down_full, preferred_element_type=jnp.float32)
    (gate_up_grad,) = glu_pull(hidden_grad)
    gate_up_low = gate_up_grad.astype(jnp.bfloat16)
    proj_grad = jnp.einsum("td,ctf->cdf", act_two, gate_up_low, preferred_element_type=jnp.float32)
    act_two_grad = tensor_sum(
        jnp.einsum("ctf,cdf->td", gate_up_low, proj_full, preferred_element_type=jnp.float32)
    )
    (mid_back,) = norm_two_pull(act_two_grad)
    mid_grad = mid_back + grad_out.astype(jnp.float32)
    mid_low = mid_grad.astype(jnp.bfloat16)
    out_grad = jnp.einsum("td,tf->df", mid_low, attended_low, preferred_element_type=jnp.float32)
    attended_grad = jnp.einsum("td,df->tf", mid_low, out_full, preferred_element_type=jnp.float32)
    attended_grad = attended_grad.astype(jnp.bfloat16).reshape(row_count, local_heads, HEAD_DIM)
    scores = scores_of()
    probs = jnp.exp(scores - log_mass)
    value_grad = jnp.einsum(
        "htk,thd->khd",
        probs.astype(jnp.bfloat16),
        attended_grad,
        preferred_element_type=jnp.float32,
    )
    prob_grad = jnp.einsum(
        "thd,khd->htk", attended_grad, values_all, preferred_element_type=jnp.float32
    )
    delta_rows = jnp.sum(probs * prob_grad, axis=2, keepdims=True)
    score_grad = (probs * (prob_grad - delta_rows)).astype(jnp.bfloat16)
    query_grad = (
        jnp.einsum("htk,khd->thd", score_grad, keys_all, preferred_element_type=jnp.float32)
        * score_scale
    )
    key_grad = (
        jnp.einsum("htk,thd->khd", score_grad, query_low, preferred_element_type=jnp.float32)
        * score_scale
    )
    key_mine, value_mine = (
        lax.psum_scatter(
            key_grad.reshape(pack_len, head_width), "ctx", scatter_dimension=0, tiled=True
        ),
        lax.psum_scatter(
            value_grad.reshape(pack_len, head_width), "ctx", scatter_dimension=0, tiled=True
        ),
    )
    query_raw_grad, key_raw_grad = turn_pull(
        (query_grad, key_mine.reshape(row_count, local_heads, HEAD_DIM))
    )
    joint_grad = jnp.stack(
        [
            query_raw_grad.reshape(row_count, head_width),
            key_raw_grad.reshape(row_count, head_width),
            value_mine,
        ]
    ).astype(jnp.bfloat16)
    att_grad = jnp.einsum("td,ctf->cdf", act_one, joint_grad, preferred_element_type=jnp.float32)
    act_one_grad = tensor_sum(
        jnp.einsum("ctf,cdf->td", joint_grad, att_full, preferred_element_type=jnp.float32)
    )
    (in_back,) = norm_one_pull(act_one_grad)
    input_grad = in_back + mid_grad
    return (block_rows, input_grad, (att_grad, out_grad, proj_grad, down_grad))


def shards(
    tokens,
    cotangent,
    lengths,
    deal,
    att_proj,
    attn_out,
    ff_proj,
    ff_out,
    att_proj_first,
    attn_out_first,
    ff_proj_first,
    ff_out_first,
    att_proj_second,
    attn_out_second,
    ff_proj_second,
    ff_out_second,
):
    ctx_index = lax.axis_index("ctx")
    micro_count = tokens.shape[0]
    block_list = []
    input_list = []
    totals = None
    for batch_slot in range(micro_count):
        weights = gather_weights(att_proj, attn_out, ff_proj, ff_out)
        block_rows, input_grad, local_grads = micro_step(
            tokens[batch_slot].astype(jnp.float32),
            cotangent[batch_slot],
            deal[batch_slot],
            lengths[batch_slot],
            weights,
            ctx_index,
        )
        block_list.append(block_rows)
        input_list.append(input_grad)
        step_grads = reduce_grads(local_grads[0], local_grads[1], local_grads[2], local_grads[3])
        if batch_slot == 0:
            totals = step_grads
        else:
            totals = jax.tree.map(jnp.add, totals, step_grads)
    att_total, out_total, proj_total, down_total = totals
    square_sums = lax.psum(
        (
            jnp.sum(att_total * att_total),
            jnp.sum(out_total * out_total),
            jnp.sum(proj_total * proj_total),
            jnp.sum(down_total * down_total),
        ),
        ("fsdp", "ctx", "tp"),
    )
    norm_value = jnp.sqrt(square_sums[0] + square_sums[1] + square_sums[2] + square_sums[3])
    clip_factor = jnp.minimum(1.0, MAX_NORM / (norm_value + 1e-06))
    base_rate = D ** (-0.5)
    out_rate = (D // 32) ** (-0.5)
    att_first_new, att_second_new, att_new = adam_step(
        att_proj, att_total, att_proj_first, att_proj_second, clip_factor, base_rate
    )
    out_first_new, out_second_new, out_new = adam_step(
        attn_out, out_total, attn_out_first, attn_out_second, clip_factor, out_rate
    )
    proj_first_new, proj_second_new, proj_new = adam_step(
        ff_proj, proj_total, ff_proj_first, ff_proj_second, clip_factor, base_rate
    )
    down_first_new, down_second_new, down_new = adam_step(
        ff_out, down_total, ff_out_first, ff_out_second, clip_factor, base_rate
    )
    return (
        jnp.stack(block_list),
        jnp.stack(input_list),
        norm_value.reshape(1),
        att_total,
        out_total,
        proj_total,
        down_total,
        att_first_new,
        out_first_new,
        proj_first_new,
        down_first_new,
        att_second_new,
        out_second_new,
        proj_second_new,
        down_second_new,
        att_new,
        out_new,
        proj_new,
        down_new,
        att_new.astype(jnp.bfloat16),
        out_new.astype(jnp.bfloat16),
        proj_new.astype(jnp.bfloat16),
        down_new.astype(jnp.bfloat16),
    )


def solution(mesh):
    in_specs = (
        P("fsdp", "ctx", None),
        P("fsdp", "ctx", None),
        P("fsdp", None),
        P("fsdp", None),
        P(None, ("fsdp", "ctx"), "tp"),
        P(("fsdp", "ctx"), "tp"),
        P(None, ("fsdp", "ctx"), "tp"),
        P(("fsdp", "ctx"), "tp"),
        P(None, ("fsdp", "ctx"), "tp"),
        P(("fsdp", "ctx"), "tp"),
        P(None, ("fsdp", "ctx"), "tp"),
        P(("fsdp", "ctx"), "tp"),
        P(None, ("fsdp", "ctx"), "tp"),
        P(("fsdp", "ctx"), "tp"),
        P(None, ("fsdp", "ctx"), "tp"),
        P(("fsdp", "ctx"), "tp"),
    )
    out_specs = (
        P("fsdp", "ctx", None),
        P("fsdp", "ctx", None),
        P(),
        P(None, ("fsdp", "ctx"), "tp"),
        P(("fsdp", "ctx"), "tp"),
        P(None, ("fsdp", "ctx"), "tp"),
        P(("fsdp", "ctx"), "tp"),
        P(None, ("fsdp", "ctx"), "tp"),
        P(("fsdp", "ctx"), "tp"),
        P(None, ("fsdp", "ctx"), "tp"),
        P(("fsdp", "ctx"), "tp"),
        P(None, ("fsdp", "ctx"), "tp"),
        P(("fsdp", "ctx"), "tp"),
        P(None, ("fsdp", "ctx"), "tp"),
        P(("fsdp", "ctx"), "tp"),
        P(None, ("fsdp", "ctx"), "tp"),
        P(("fsdp", "ctx"), "tp"),
        P(None, ("fsdp", "ctx"), "tp"),
        P(("fsdp", "ctx"), "tp"),
        P(None, ("fsdp", "ctx"), "tp"),
        P(("fsdp", "ctx"), "tp"),
        P(None, ("fsdp", "ctx"), "tp"),
        P(("fsdp", "ctx"), "tp"),
    )
    return jax.shard_map(shards, mesh=mesh, in_specs=in_specs, out_specs=out_specs, check_vma=False)
```

profile of v0, /device:TPU:0, one launch (start us, length us, event | category | flops | bytes accessed | tf_op | source)
XLA Modules:
  0.0 2616.3 jit_solution(11051854917980619340)
XLA Ops:
  14.9 97.6 %all-gather.11.cloned.1.call-done = bf16[3,2048,512]{2,1,0:T(8,128)(2,1)} async-done(((bf16[3,256,512]{2,1,0:T(8,128)(2,1)}), bf16[3,2048,512]{2,1,0:T(8,128)(2,1)}) %all-gather.11.cloned.1.call-update) | async-done | bytes 6291472 | tf_op jit(solution)/shard_map/all_gather | solution.py:69
  155.6 28.1 %all-gather.25.cloned.1.call-done = bf16[1,1024,512]{2,1,0:T(8,128)(2,1)} async-done(((bf16[1,256,512]{2,1,0:T(8,128)(2,1)}), bf16[1,1024,512]{2,1,0:T(8,128)(2,1)}) %all-gather.25.cloned.1.call-update) | async-done | bytes 1048592 | tf_op jit(solution)/shard_map/all_gather | solution.py:129
  185.1 28.1 %all-gather.13.cloned.1.call-done = bf16[1024,512]{1,0:T(8,128)(2,1)} async-done(((bf16[256,512]{1,0:T(8,128)(2,1)}), bf16[1024,512]{1,0:T(8,128)(2,1)}) %all-gather.13.cloned.1.call-update) | async-done | bytes 1048592 | tf_op jit(solution)/shard_map/all_gather | solution.py:128
  214.7 27.9 %all-gather.23.cloned.1.call-done = bf16[1,1024,512]{2,1,0:T(8,128)(2,1)} async-done(((bf16[1,256,512]{2,1,0:T(8,128)(2,1)}), bf16[1,1024,512]{2,1,0:T(8,128)(2,1)}) %all-gather.23.cloned.1.call-update) | async-done | bytes 1048592 | tf_op jit(solution)/shard_map/all_gather | solution.py:129
  253.3 40.7 %all-gather.15.cloned.1.call-done = bf16[2048,512]{1,0:T(8,128)(2,1)} async-done(((bf16[256,512]{1,0:T(8,128)(2,1)}), bf16[2048,512]{1,0:T(8,128)(2,1)}) %all-gather.15.cloned.1.call-update) | async-done | bytes 2097168 | tf_op jit(solution)/shard_map/all_gather | solution.py:73
  307.1 77.2 %all-reduce.25.cloned.1.call-done = (f32[256,2048]{1,0:T(8,128)}, f32[256,2048]{1,0:T(8,128)}) async-done(((f32[256,2048]{1,0:T(8,128)}, f32[256,2048]{1,0:T(8,128)}), (f32[256,2048]{1,0:T(8,128)}, f32[256,2048]{1,0:T(8,128)})) %all-reduce.25.cloned.1.call-update) | async-done | bytes 4194320 | tf_op jit(solution)/shard_map/psum | solution.py:64
  389.5 225.4 %all-gather.17.cloned.1.call-done = bf16[2,2048,2048]{2,1,0:T(8,128)(2,1)} async-done(((bf16[2,256,2048]{2,1,0:T(8,128)(2,1)}), bf16[2,2048,2048]{2,1,0:T(8,128)(2,1)}) %all-gather.17.cloned.1.call-update) | async-done | bytes 16777232 | tf_op jit(solution)/shard_map/all_gather | solution.py:70
  634.6 106.4 %all-gather.19.cloned.1.call-done = bf16[2048,2048]{1,0:T(8,128)(2,1)} async-done(((bf16[256,2048]{1,0:T(8,128)(2,1)}), bf16[2048,2048]{1,0:T(8,128)(2,1)}) %all-gather.19.cloned.1.call-update) | async-done | bytes 8388624 | tf_op jit(solution)/shard_map/all_gather | solution.py:74
  757.5 13.5 convolution_bitcast_fusion.4
  771.0 13.7 convolution_bitcast_fusion.5
  785.5 83.3 %all-reduce.23.cloned.1.call-done = (f32[256,2048]{1,0:T(8,128)}, f32[256,2048]{1,0:T(8,128)}) async-done(((f32[256,2048]{1,0:T(8,128)}, f32[256,2048]{1,0:T(8,128)}), (f32[256,2048]{1,0:T(8,128)}, f32[256,2048]{1,0:T(8,128)})) %all-reduce.23.cloned.1.call-update) | async-done | bytes 4194320 | tf_op jit(solution)/shard_map/psum | solution.py:64
  953.2 25.2 reduce-scatter.17.cloned.1.call-done
  979.8 44.6 %reduce-scatter.15.cloned.1.call-done = f32[256,512]{1,0:T(8,128)} async-done(((f32[1024,512]{1,0:T(8,128)}), f32[256,512]{1,0:T(8,128)}) %reduce-scatter.15.cloned.1.call-update) | async-done | bytes 524304 | tf_op jit(solution)/shard_map/reduce_scatter | solution.py:206
  1025.5 45.0 %reduce-scatter.19.cloned.1.call-done = f32[256,512]{1,0:T(8,128)} async-done(((f32[1024,512]{1,0:T(8,128)}), f32[256,512]{1,0:T(8,128)}) %reduce-scatter.19.cloned.1.call-update) | async-done | bytes 524304 | tf_op jit(solution)/shard_map/reduce_scatter | solution.py:206
  1114.7 14.1 convert_bitcast_fusion
  1174.6 36.5 %reduce-scatter.25.cloned.1.call-done = bf16[256,512]{1,0:T(8,128)(2,1)} async-done(((bf16[2048,512]{1,0:T(8,128)(2,1)}), bf16[256,512]{1,0:T(8,128)(2,1)}) %reduce-scatter.25.cloned.1.call-update) | async-done | bytes 262160 | tf_op jit(solution)/shard_map/reduce_scatter | solution.py:89
  1213.6 154.7 %all-reduce.21.cloned.1.call-done = (f32[256,2048]{1,0:T(8,128)}, f32[256,2048]{1,0:T(8,128)}, f32[256,2048]{1,0:T(8,128)}, f32[256,2048]{1,0:T(8,128)}) async-done(((f32[256,2048]{1,0:T(8,128)}, f32[256,2048]{1,0:T(8,128)}, f32[256,2048]{1,0:T(8,128)}, f32[256,2048]{1,0:T(8,128)}), (f32[256,2048]{1,0:T(8,128)}, f32[256,2048]{1,0:T(8,128)}, f32[256,2048]{1,0:T(8,128)}, ...) | async-done | bytes 8388624 | tf_op jit(solution)/shard_map/psum | solution.py:64
  1384.8 136.6 %reduce-scatter.35.cloned.1.call-done = bf16[256,2048]{0,1:T(8,128)(2,1)} async-done(((bf16[2048,2048]{0,1:T(8,128)(2,1)}), bf16[256,2048]{0,1:T(8,128)(2,1)}) %reduce-scatter.35.cloned.1.call-update) | async-done | bytes 1048592 | tf_op jit(solution)/shard_map/reduce_scatter | solution.py:92
  1521.4 152.5 %reduce-scatter.33.cloned.1.call-done = bf16[256,2048]{0,1:T(8,128)(2,1)} async-done(((bf16[2048,2048]{0,1:T(8,128)(2,1)}), bf16[256,2048]{0,1:T(8,128)(2,1)}) %reduce-scatter.33.cloned.1.call-update) | async-done | bytes 1048592 | tf_op jit(solution)/shard_map/reduce_scatter | solution.py:92
  1676.6 118.2 %reduce-scatter.23.cloned.1.call-done = bf16[3,256,512]{1,2,0:T(8,128)(2,1)} async-done(((bf16[3,2048,512]{1,2,0:T(8,128)(2,1)}), bf16[3,256,512]{1,2,0:T(8,128)(2,1)}) %reduce-scatter.23.cloned.1.call-update) | async-done | bytes 786448 | tf_op jit(solution)/shard_map/reduce_scatter | solution.py:81
  1794.7 121.2 %reduce-scatter.21.cloned.1.call-done = bf16[3,256,512]{1,2,0:T(8,128)(2,1)} async-done(((bf16[3,2048,512]{1,2,0:T(8,128)(2,1)}), bf16[3,256,512]{1,2,0:T(8,128)(2,1)}) %reduce-scatter.21.cloned.1.call-update) | async-done | bytes 786448 | tf_op jit(solution)/shard_map/reduce_scatter | solution.py:81
  1919.6 281.3 %reduce-scatter.31.cloned.1.call-done = bf16[2,256,2048]{1,2,0:T(8,128)(2,1)} async-done(((bf16[2,2048,2048]{1,2,0:T(8,128)(2,1)}), bf16[2,256,2048]{1,2,0:T(8,128)(2,1)}) %reduce-scatter.31.cloned.1.call-update) | async-done | bytes 2097168 | tf_op jit(solution)/shard_map/reduce_scatter | solution.py:84
  2200.9 285.2 %reduce-scatter.29.cloned.1.call-done = bf16[2,256,2048]{1,2,0:T(8,128)(2,1)} async-done(((bf16[2,2048,2048]{1,2,0:T(8,128)(2,1)}), bf16[2,256,2048]{1,2,0:T(8,128)(2,1)}) %reduce-scatter.29.cloned.1.call-update) | async-done | bytes 2097168 | tf_op jit(solution)/shard_map/reduce_scatter | solution.py:84
  2494.5 39.0 %psum.98 = f32[]{:T(128)} all-reduce(f32[]{:T(128)S(6)} %add.301), channel_id=1, replica_groups=mesh['fsdp'=2,'ctx'=4,'tp'=4] {'fsdp','ctx','tp'}, use_global_device_ids=true, to_apply=%region_41.42 | all-reduce | flops 1 | bytes 8 | tf_op jit(solution)/shard_map/psum | solution.py:270
  (437 shorter events, 400.5 us)
Async XLA Ops:
  7.2 105.3 %all-gather.11.cloned.1.call-start = ((), (), s32[]{:S(2)}) async-start(), calls=%async_computation.12 | async-start | bytes 7077888 | tf_op jit(solution)/shard_map/all_gather | solution.py:69
  9.7 144.5 %all-gather.21.cloned.1.call-start = ((), (), s32[]{:S(2)}) async-start(), calls=%async_computation.17 | async-start | bytes 1310720 | tf_op jit(solution)/shard_map/all_gather | solution.py:128
  127.9 55.9 %all-gather.25.cloned.1.call-start = ((), (), s32[]{:S(2)}) async-start(), calls=%async_computation.31 | async-start | bytes 1310720 | tf_op jit(solution)/shard_map/all_gather | solution.py:129
  132.7 80.5 %all-gather.13.cloned.1.call-start = ((), (), s32[]{:S(2)}) async-start(), calls=%async_computation.13 | async-start | bytes 1310720 | tf_op jit(solution)/shard_map/all_gather | solution.py:128
  144.2 98.5 %all-gather.23.cloned.1.call-start = ((), (), s32[]{:S(2)}) async-start(), calls=%async_computation.30 | async-start | bytes 1310720 | tf_op jit(solution)/shard_map/all_gather | solution.py:129
  145.0 149.0 %all-gather.15.cloned.1.call-start = ((), (), s32[]{:S(2)}) async-start(), calls=%async_computation.14 | async-start | bytes 2359296 | tf_op jit(solution)/shard_map/all_gather | solution.py:73
  145.8 238.4 %all-reduce.25.cloned.1.call-start = ((), (), s32[]{:S(2)}) async-start(), calls=%async_computation.34 | async-start | bytes 8388608 | tf_op jit(solution)/shard_map/psum | solution.py:64
  299.9 315.0 %all-gather.17.cloned.1.call-start = ((), (), s32[]{:S(2)}) async-start(), calls=%async_computation.15 | async-start | bytes 18874368 | tf_op jit(solution)/shard_map/all_gather | solution.py:70
  303.9 437.2 %all-gather.19.cloned.1.call-start = ((), (), s32[]{:S(2)}) async-start(), calls=%async_computation.16 | async-start | bytes 9437184 | tf_op jit(solution)/shard_map/all_gather | solution.py:74
  306.8 561.9 %all-reduce.23.cloned.1.call-start = ((), (), s32[]{:S(2)}) async-start(), calls=%async_computation.33 | async-start | bytes 8388608 | tf_op jit(solution)/shard_map/psum | solution.py:64
  389.5 238.6 %copy-start.77 = (f32[256]{0:T(256)}, f32[256]{0:T(256)S(1)}, u32[]{:S(2)}) copy-start(f32[256]{0:T(256)S(1)} %fusion.97) | copy-start | bytes 3076
  784.7 165.8 %reduce-scatter.13.cloned.1.call-start = ((), (), s32[]{:S(2)}) async-start(), calls=%async_computation.18 | async-start | bytes 2621440 | tf_op jit(solution)/shard_map/reduce_scatter | solution.py:203
  888.8 89.6 %reduce-scatter.17.cloned.1.call-start = ((), (), s32[]{:S(2)}) async-start(), calls=%async_computation.20 | async-start | bytes 2621440 | tf_op jit(solution)/shard_map/reduce_scatter | solution.py:203
  901.9 122.5 %reduce-scatter.15.cloned.1.call-start = ((), (), s32[]{:S(2)}) async-start(), calls=%async_computation.19 | async-start | bytes 2621440 | tf_op jit(solution)/shard_map/reduce_scatter | solution.py:206
  910.2 160.3 %reduce-scatter.19.cloned.1.call-start = ((), (), s32[]{:S(2)}) async-start(), calls=%async_computation.21 | async-start | bytes 2621440 | tf_op jit(solution)/shard_map/reduce_scatter | solution.py:206
  918.5 256.1 %reduce-scatter.27.cloned.1.call-start = ((), (), s32[]{:S(2)}) async-start(), calls=%async_computation.25 | async-start | bytes 2359296 | tf_op jit(solution)/shard_map/reduce_scatter | solution.py:89
  922.7 288.3 %reduce-scatter.25.cloned.1.call-start = ((), (), s32[]{:S(2)}) async-start(), calls=%async_computation.24 | async-start | bytes 2359296 | tf_op jit(solution)/shard_map/reduce_scatter | solution.py:89
  944.5 423.8 %all-reduce.21.cloned.1.call-start = ((), (), s32[]{:S(2)}) async-start(), calls=%async_computation.32 | async-start | bytes 16777216 | tf_op jit(solution)/shard_map/psum | solution.py:64
  1083.6 437.7 %reduce-scatter.35.cloned.1.call-start = ((), (), s32[]{:S(2)}) async-start(), calls=%async_computation.29 | async-start | bytes 9437184 | tf_op jit(solution)/shard_map/reduce_scatter | solution.py:92
  1092.2 581.7 %reduce-scatter.33.cloned.1.call-start = ((), (), s32[]{:S(2)}) async-start(), calls=%async_computation.28 | async-start | bytes 9437184 | tf_op jit(solution)/shard_map/reduce_scatter | solution.py:92
  1100.7 694.0 %reduce-scatter.23.cloned.1.call-start = ((), (), s32[]{:S(2)}) async-start(), calls=%async_computation.23 | async-start | bytes 7077888 | tf_op jit(solution)/shard_map/reduce_scatter | solution.py:81
  1107.2 808.8 %reduce-scatter.21.cloned.1.call-start = ((), (), s32[]{:S(2)}) async-start(), calls=%async_computation.22 | async-start | bytes 7077888 | tf_op jit(solution)/shard_map/reduce_scatter | solution.py:81
  1114.0 1086.9 %reduce-scatter.31.cloned.1.call-start = ((), (), s32[]{:S(2)}) async-start(), calls=%async_computation.27 | async-start | bytes 18874368 | tf_op jit(solution)/shard_map/reduce_scatter | solution.py:84
  1128.8 1357.3 %reduce-scatter.29.cloned.1.call-start = ((), (), s32[]{:S(2)}) async-start(), calls=%async_computation.26 | async-start | bytes 18874368 | tf_op jit(solution)/shard_map/reduce_scatter | solution.py:84
  (108 other events, 1219.8 us)
Sparse Core Ops, SparseCore 0:
  10.8 101.7 all-gather.10
  128.0 26.1 all-gather.20
  156.3 27.4 all-gather.24
  185.7 27.4 all-gather.12
  215.2 27.4 all-gather.22
  245.2 48.7 all-gather.14
  300.1 84.1 all-reduce.24
  387.2 227.7 all-gather.16
  617.9 123.0 all-gather.18
  784.8 83.8 all-reduce.22
  888.9 43.9 reduce-scatter.12
  935.2 43.1 reduce-scatter.16
  981.2 43.1 reduce-scatter.14
  1027.3 43.1 reduce-scatter.18
  1073.9 67.1 reduce-scatter.26
  1144.4 66.5 reduce-scatter.24
  1215.3 152.9 all-reduce.20
  1371.8 149.5 reduce-scatter.34
  1525.4 148.4 reduce-scatter.32
  1677.3 117.3 reduce-scatter.22
  1798.3 117.5 reduce-scatter.20
  1919.7 281.1 reduce-scatter.30
  2205.2 280.8 reduce-scatter.28
where the time goes:
time: 2630 us; the launch traced here: 2620 us
  waiting for transfers between devices  2120 us (81%)
  matrix products  203 us (8%)
  local copies, waits for them, and re-layouts  129 us (5%)
  other arithmetic  101 us (4%)
  blocking collectives  39 us (1%)
    reduce_scatter x2, waiting for transfers between devices, reduce_grads(): lax.psum_scatter(proj_grad.astype(jnp.bfloat16), ('fsdp', 'ctx'), scatter...  566 us
    psum x3, waiting for transfers between devices, tensor_sum(): return lax.psum(partial_sum, 'tp')  315 us
    reduce_scatter x2, waiting for transfers between devices, reduce_grads(): lax.psum_scatter(down_grad.astype(jnp.bfloat16), ('fsdp', 'ctx'), scatter...  289 us
    reduce_scatter x2, waiting for transfers between devices, reduce_grads(): lax.psum_scatter(att_grad.astype(jnp.bfloat16), ('fsdp', 'ctx'), scatter_...  239 us
    all_gather x1, waiting for transfers between devices, gather_weights(): lax.all_gather(ff_proj.astype(jnp.bfloat16), ('fsdp', 'ctx'), axis=1, til...  225 us
    all_gather x1, waiting for transfers between devices, gather_weights(): lax.all_gather(ff_out.astype(jnp.bfloat16), ('fsdp', 'ctx'), axis=0, tile...  106 us
    unnamed x242, local copies, waits for them, and re-layouts  102 us
    all_gather x1, waiting for transfers between devices, gather_weights(): lax.all_gather(att_proj.astype(jnp.bfloat16), ('fsdp', 'ctx'), axis=1, ti...  97.6 us
  transfers between devices with their start and end apart: 23, of which 21 were waited for; matrix products, arithmetic and copies ran while one was open for 10% of the time, Pallas kernels for 0%

commit v1 on v0

v1 whole, which is shorter than its diff:
```python
import jax
import jax.numpy as jnp
from jax import lax
from jax.sharding import PartitionSpec as P

HEAD_DIM = 128
STEP = 10
EPS_NORM = 1e-05
BETA_ONE = 0.9
BETA_TWO = 0.95
EPS_ADAM = 1e-08
DECAY = 0.1
MAX_NORM = 1.0
NEG_FILL = -1e30
BF = jnp.bfloat16
F32 = jnp.float32


def mean_spread(values):
    centre = values - jnp.mean(values, axis=-1, keepdims=True)
    spread = jnp.mean(centre * centre, axis=-1, keepdims=True)
    scale = lax.rsqrt(spread + EPS_NORM)
    return centre * scale, scale


def norm_back(grad, normed, scale):
    return scale * (
        grad
        - jnp.mean(grad, axis=-1, keepdims=True)
        - normed * jnp.mean(grad * normed, axis=-1, keepdims=True)
    )


def dot(left, right, dims):
    return lax.dot_general(left, right, (dims, ((), ())), preferred_element_type=F32)


def adam_step(weight, grad_sum, first, second, clip_factor, learn_rate):
    clipped = grad_sum * clip_factor
    first_new = BETA_ONE * first + (1.0 - BETA_ONE) * clipped
    second_new = BETA_TWO * second + (1.0 - BETA_TWO) * clipped * clipped
    first_hat = first_new / (1.0 - BETA_ONE**STEP)
    second_hat = second_new / (1.0 - BETA_TWO**STEP)
    weight_new = weight - learn_rate * (
        first_hat / (jnp.sqrt(second_hat) + EPS_ADAM) + DECAY * weight
    )
    return (first_new, second_new, weight_new)


def make_shards(mesh):
    n_f, n_c, n_t = (mesh.shape[a] for a in ("fsdp", "ctx", "tp"))

    def by_ctx(block, shift):
        return lax.ppermute(block, "ctx", [(i, (i + shift) % n_c) for i in range(n_c)])

    def by_core(block):
        return lax.ppermute(block, "tp", [(i, i ^ 1) for i in range(n_t)])

    def by_pack(block, shift, other):
        pairs = [
            (f * n_t + t, ((f + shift) % n_f) * n_t + (t ^ (2 * other)))
            for f in range(n_f)
            for t in range(n_t)
        ]
        return lax.ppermute(block, ("fsdp", "tp"), pairs)

    def gather_rows(half):
        mine = jnp.stack([half] + [by_ctx(half, s) for s in range(1, n_c)])
        both = jnp.stack([mine, by_core(mine)], axis=1)
        return both.reshape(-1, half.shape[1])

    def scatter_rows(partial):
        width = partial.shape[1]
        split = partial.astype(BF).reshape(n_c, 2, -1, width)
        summed = split[:, 0].astype(F32) + by_core(split[:, 1]).astype(F32)
        sent = summed.astype(BF)
        total = summed[0]
        for j in range(1, n_c):
            total = total + by_ctx(sent[j], -j).astype(F32)
        return total

    def gather_weight(shard):
        swapped = lax.all_to_all(shard.astype(BF), "ctx", 2, 1, tiled=True)
        columns = []
        for other in range(2):
            parts = [
                swapped if (s == 0 and other == 0) else by_pack(swapped, s, other)
                for s in range(n_f)
            ]
            columns.append(jnp.concatenate(parts, axis=1))
        return jnp.concatenate(columns, axis=2)

    def scatter_grad(grad):
        count, height, width = grad.shape
        low = grad.astype(BF).reshape(count, n_f, height // n_f, 2, width // 2)
        total = grad.reshape(low.shape)[:, 0, :, 0]
        for other in range(2):
            for i in range(n_f):
                if i or other:
                    total = total + by_pack(low[:, i, :, other], -i, other).astype(F32)
        return lax.all_to_all(total.astype(BF), "ctx", 1, 2, tiled=True).astype(F32)

    def shards(
        tokens,
        cotangent,
        lengths,
        deal,
        att_proj,
        attn_out,
        ff_proj,
        ff_out,
        att_proj_first,
        attn_out_first,
        ff_proj_first,
        ff_out_first,
        att_proj_second,
        attn_out_second,
        ff_proj_second,
        ff_out_second,
    ):
        f_at, c_at, t_at = (lax.axis_index(a) for a in ("fsdp", "ctx", "tp"))
        pack_at, core_at = t_at // 2, t_at % 2
        packs, row_count, width = tokens.shape
        half = row_count // 2
        pack_len = deal.shape[1]
        score_scale = HEAD_DIM ** (-0.5)
        f_width = width // n_f

        def turned(rows):
            return jnp.concatenate(
                [
                    lax.dynamic_slice_in_dim(rows, ((f_at - i) % n_f) * f_width, f_width, 1)
                    for i in range(n_f)
                ],
                axis=1,
            )

        def own_rows(array):
            rows = array.reshape(packs * 2, half, width)
            return turned(lax.dynamic_index_in_dim(rows, t_at, 0, keepdims=False))

        own_tokens = own_rows(tokens)
        own_cot = own_rows(cotangent)
        att_w = gather_weight(jnp.concatenate([att_proj, attn_out[None]]))
        own_input = own_tokens.astype(F32)
        normed_one, scale_one = mean_spread(own_input)
        act_one = gather_rows(normed_one.astype(BF))

        deal_pack = lax.dynamic_index_in_dim(deal, pack_at, 0, keepdims=False)
        length_row = lax.dynamic_index_in_dim(lengths, pack_at, 0, keepdims=False)
        places = jnp.concatenate(
            [
                lax.dynamic_slice_in_dim(
                    deal_pack, ((c_at - j) % n_c) * row_count + ((core_at + h) % 2) * half, half
                )
                for j in range(n_c)
                for h in range(2)
            ]
        )
        seqs = lengths.shape[1]
        before = jnp.arange(seqs)[:, None] > jnp.arange(seqs)[None, :]
        starts = jnp.sum(jnp.where(before, length_row[None, :], 0), axis=1)
        inside = (places[:, None] >= starts[None, :]) & (
            places[:, None] < (starts + length_row)[None, :]
        )
        firsts = jnp.sum(jnp.where(inside, starts[None, :], 0), axis=1)
        allowed = (places[None, :] <= places[:, None]) & (places[None, :] >= firsts[:, None])
        freq_steps = jnp.arange(HEAD_DIM // 2, dtype=F32)
        inverse = jnp.power(10000.0, -2.0 * freq_steps / HEAD_DIM)
        angles = (places - firsts).astype(F32)[:, None] * inverse[None, :]
        cos_table, sine_table = jnp.cos(angles), jnp.sin(angles)

        def turn(values, sign):
            low, high = values[..., : HEAD_DIM // 2], values[..., HEAD_DIM // 2 :]
            sine = sign * sine_table[:, None, :]
            cos = cos_table[:, None, :]
            return jnp.concatenate([low * cos - high * sine, high * cos + low * sine], axis=-1)

        rank_width = att_w.shape[2]
        heads = rank_width // HEAD_DIM
        raw = [
            dot(act_one, att_w[i], ((1,), (0,))).reshape(pack_len, heads, HEAD_DIM)
            for i in range(3)
        ]
        query = turn(raw[0], 1.0).astype(BF)
        key = turn(raw[1], 1.0).astype(BF)
        value = raw[2].astype(BF)
        scores = (
            jnp.einsum("thd,khd->htk", query, key, preferred_element_type=F32) * score_scale
        )
        scores = jnp.where(allowed[None], scores, NEG_FILL)
        exp_scores = jnp.exp(scores - jnp.max(scores, axis=2, keepdims=True))
        probs = exp_scores / jnp.sum(exp_scores, axis=2, keepdims=True)
        probs_low = probs.astype(BF)
        attended = jnp.einsum("htk,khd->thd", probs_low, value, preferred_element_type=F32)
        attended_low = attended.reshape(pack_len, rank_width).astype(BF)
        out_part = dot(attended_low, att_w[3], ((1,), (1,)))
        resid_mid = own_input + scatter_rows(out_part)
        normed_two, scale_two = mean_spread(resid_mid)
        act_two = gather_rows(normed_two.astype(BF))

        ff_w = gather_weight(jnp.concatenate([ff_proj, ff_out[None]]))
        cot_rows = gather_rows(own_cot)
        up = dot(act_two, ff_w[0], ((1,), (0,)))
        gate = dot(act_two, ff_w[1], ((1,), (0,)))
        sigma = jax.nn.sigmoid(gate)
        hidden_low = (gate * sigma * up).astype(BF)
        hidden_grad = dot(cot_rows, ff_w[2], ((1,), (0,)))
        up_grad = (hidden_grad * gate * sigma).astype(BF)
        gate_grad = (hidden_grad * up * sigma * (1.0 + gate * (1.0 - sigma))).astype(BF)
        act_two_part = dot(up_grad, ff_w[0], ((1,), (1,))) + dot(gate_grad, ff_w[1], ((1,), (1,)))
        act_two_grad = scatter_rows(act_two_part)
        mid_grad = own_cot.astype(F32) + norm_back(act_two_grad, normed_two, scale_two)
        mid_rows = gather_rows(mid_grad.astype(BF))

        ff_branch = scatter_rows(dot(hidden_low, ff_w[2], ((1,), (1,))))
        block_rows = turned((resid_mid + ff_branch).astype(BF))
        block_out = lax.all_gather(block_rows, "tp", axis=0, tiled=True)
        ff_grad = jnp.stack(
            [
                dot(act_two, up_grad, ((0,), (0,))),
                dot(act_two, gate_grad, ((0,), (0,))),
                dot(cot_rows, hidden_low, ((0,), (0,))),
            ]
        )
        ff_total = scatter_grad(ff_grad)

        attended_grad = dot(mid_rows, att_w[3], ((1,), (0,))).astype(BF)
        attended_grad = attended_grad.reshape(pack_len, heads, HEAD_DIM)
        value_grad = jnp.einsum(
            "htk,thd->khd", probs_low, attended_grad, preferred_element_type=F32
        )
        prob_grad = jnp.einsum("thd,khd->htk", attended_grad, value, preferred_element_type=F32)
        delta_rows = jnp.sum(probs * prob_grad, axis=2, keepdims=True)
        score_grad = (probs * (prob_grad - delta_rows)).astype(BF)
        query_grad = (
            jnp.einsum("htk,khd->thd", score_grad, key, preferred_element_type=F32) * score_scale
        )
        key_grad = (
            jnp.einsum("htk,thd->khd", score_grad, query, preferred_element_type=F32)
            * score_scale
        )
        joint_grad = [
            part.reshape(pack_len, rank_width).astype(BF)
            for part in (turn(query_grad, -1.0), turn(key_grad, -1.0), value_grad)
        ]
        act_one_part = sum(dot(joint_grad[i], att_w[i], ((1,), (1,))) for i in range(3))
        act_one_grad = scatter_rows(act_one_part)
        input_rows = turned(norm_back(act_one_grad, normed_one, scale_one) + mid_grad)
        input_grad = lax.all_gather(input_rows, "tp", axis=0, tiled=True)
        att_grad = jnp.stack(
            [dot(act_one, part, ((0,), (0,))) for part in joint_grad]
            + [dot(mid_rows, attended_low, ((0,), (0,)))]
        )
        att_total = scatter_grad(att_grad)

        square_sum = lax.psum(
            jnp.sum(att_total * att_total) + jnp.sum(ff_total * ff_total), ("fsdp", "ctx", "tp")
        )
        norm_value = jnp.sqrt(square_sum)
        clip_factor = jnp.minimum(1.0, MAX_NORM / (norm_value + 1e-06))
        base_rate = width ** (-0.5)
        out_rate = (width // 32) ** (-0.5)
        grads = (att_total[:3], att_total[3], ff_total[:2], ff_total[2])
        weights = (att_proj, attn_out, ff_proj, ff_out)
        firsts_old = (att_proj_first, attn_out_first, ff_proj_first, ff_out_first)
        seconds_old = (att_proj_second, attn_out_second, ff_proj_second, ff_out_second)
        rates = (base_rate, out_rate, base_rate, base_rate)
        news = [
            adam_step(w, g, m, v, clip_factor, r)
            for w, g, m, v, r in zip(weights, grads, firsts_old, seconds_old, rates)
        ]
        return (
            block_out.reshape(tokens.shape),
            input_grad.reshape(tokens.shape),
            norm_value.reshape(1),
            *grads,
            *(n[0] for n in news),
            *(n[1] for n in news),
            *(n[2] for n in news),
            *(n[2].astype(BF) for n in news),
        )

    return shards


def solution(mesh):
    act = P("fsdp", "ctx", None)
    table = P("fsdp", None)
    cube = P(None, ("fsdp", "ctx"), "tp")
    flat = P(("fsdp", "ctx"), "tp")
    group = (cube, flat, cube, flat)
    in_specs = (act, act, table, table) + group * 3
    out_specs = (act, act, P()) + group * 5
    return jax.shard_map(
        make_shards(mesh), mesh=mesh, in_specs=in_specs, out_specs=out_specs, check_vma=False
    )
```

time: 2630 us -> 1250 us (0.48)
  waiting for transfers between devices: 2120 us -> 598 us
  starting transfers between devices: 2.33 us -> 175 us
  matrix products: 203 us -> 114 us
  other arithmetic: 101 us -> 139 us
    reduce_scatter x12 -> x0, waiting for transfers between devices: 1250 us -> none  [the longest x2 566 us: reduce_grads(): lax.psum_scatter(proj_grad.astype(jnp.bfloat16), ('fsdp', 'ctx'), scatter...]
    ppermute x0 -> x44, waiting for transfers between devices: none -> 592 us  [the longest x24 370 us: by_ctx(): lax.ppermute(block, 'ctx', [(i, (i + shift) % n_c) for i in range(n_c)])]
    all_gather x8 -> x2, waiting for transfers between devices: 560 us -> 0.02 us  [the longest x1 0.02 us: shards(): block_out = lax.all_gather(block_rows, 'tp', axis=0, tiled=True)]
    psum x3 -> x0, waiting for transfers between devices: 315 us -> none  [tensor_sum(): return lax.psum(partial_sum, 'tp')]
    ppermute x0 -> x44, starting transfers between devices: none -> 141 us  [the longest x24 125 us: by_ctx(): lax.ppermute(block, 'ctx', [(i, (i + shift) % n_c) for i in range(n_c)])]
    dot_general x36 -> x26, matrix products: 203 us -> 108 us  [the longest x21 95.9 us: dot(): lax.dot_general(left, right, (dims, ((), ())), preferred_element_type=F32)]
    unnamed x242 -> x169, local copies, waits for them, and re-layouts: 102 us -> 31.6 us
    dot_general x0 -> x6, local copies, waits for them, and re-layouts: none -> 35.6 us  [dot(): lax.dot_general(left, right, (dims, ((), ())), preferred_element_type=F32)]
  transfers between devices with their start and end apart: 23 -> 50, of which waited for: 21 -> 22; matrix products, arithmetic and copies ran while one was open for 10% -> 22% of each run, Pallas kernels for 0% -> 0%
where the time goes in v1:
time: 1250 us; the launch traced here: 1240 us
  waiting for transfers between devices  598 us (48%)
  starting transfers between devices  175 us (14%)
  local copies, waits for them, and re-layouts  154 us (12%)
  other arithmetic  139 us (11%)
  matrix products  114 us (9%)
  blocking collectives  40.1 us (3%)
  between operations  19.1 us (2%)
    ppermute x24, waiting for transfers between devices, by_ctx(): lax.ppermute(block, 'ctx', [(i, (i + shift) % n_c) for i in range(n_c)])  370 us
    ppermute x12, waiting for transfers between devices, by_pack(): return lax.ppermute(block, ('fsdp', 'tp'), pairs)  222 us
    ppermute x24, starting transfers between devices, by_ctx(): lax.ppermute(block, 'ctx', [(i, (i + shift) % n_c) for i in range(n_c)])  125 us
    dot_general x21, matrix products, dot(): lax.dot_general(left, right, (dims, ((), ())), preferred_element_type=F32)  95.9 us
    psum x1, blocking collectives, shards(): lax.psum(jnp.sum(att_total * att_total) + jnp.sum(ff_total * ff_total), (...  40.1 us
    dot_general x6, local copies, waits for them, and re-layouts, dot(): lax.dot_general(left, right, (dims, ((), ())), preferred_element_type=F32)  35.6 us
    unnamed x169, local copies, waits for them, and re-layouts  31.6 us
    all_to_all x2, starting transfers between devices, scatter_grad(): return lax.all_to_all(total.astype(BF), 'ctx', 1, 2, tiled=True).astype(F32)  25.3 us
  transfers between devices with their start and end apart: 50, of which 22 were waited for; matrix products, arithmetic and copies ran while one was open for 22% of the time, Pallas kernels for 0%

profile of v1, /device:TPU:0, one launch (start us, length us, event | category | flops | bytes accessed | tf_op | source)
XLA Modules:
  0.0 1239.6 jit_solution(7783477940593059198)
XLA Ops:
  28.0 44.8 %collective-permute-done.1 = bf16[128,2048]{1,0:T(8,128)(2,1)} collective-permute-done((bf16[128,2048]{1,0:T(8,128)(2,1)}, bf16[128,2048]{1,0:T(8,128)(2,1)}, u32[]{:S(2)}, u32[]{:S(2)}) %collective-permute-start.1) | collective-permute-done | bytes 524320 | tf_op jit(solution)/shard_map/ppermute | solution.py:54
  93.8 17.7 %collective-permute-done.6 = bf16[4,1024,128]{1,2,0:T(8,128)(2,1)S(1)} collective-permute-done((bf16[4,1024,128]{1,2,0:T(8,128)(2,1)S(1)}, bf16[4,1024,128]{1,2,0:T(8,128)(2,1)S(1)}, u32[]{:S(2)}, u32[]{:S(2)}) %collective-permute-start.6) | collective-permute-done | bytes 1048608 | tf_op jit(solution)/shard_map/ppermute | solution.py:65
  111.4 20.4 %collective-permute-done.5 = bf16[4,1024,128]{1,2,0:T(8,128)(2,1)S(1)} collective-permute-done((bf16[4,1024,128]{1,2,0:T(8,128)(2,1)S(1)}, bf16[4,1024,128]{1,2,0:T(8,128)(2,1)S(1)}, u32[]{:S(2)}, u32[]{:S(2)}) %collective-permute-start.5) | collective-permute-done | bytes 1048608 | tf_op jit(solution)/shard_map/ppermute | solution.py:65
  189.7 71.6 %collective-permute-done.10 = bf16[128,2048]{1,0:T(8,128)(2,1)S(1)} collective-permute-done((bf16[128,2048]{1,0:T(8,128)(2,1)S(1)}, bf16[128,2048]{1,0:T(8,128)(2,1)S(1)}, u32[]{:S(2)}, u32[]{:S(2)}) %collective-permute-start.10) | collective-permute-done | bytes 524320 | tf_op jit(solution)/shard_map/ppermute | solution.py:54
  261.3 65.1 %collective-permute-start.22 = (bf16[128,2048]{1,0:T(8,128)(2,1)S(1)}, bf16[128,2048]{1,0:T(8,128)(2,1)S(1)}, u32[]{:S(2)}, u32[]{:S(2)}) collective-permute-start(bf16[128,2048]{1,0:T(8,128)(2,1)S(1)} %get-tuple-element.108), channel_id=1, source_target_pairs={{0,4},{4,8},{8,12},{12,0},{1,5},{5,9},{9,13},{13,1},{2,6},{6,10},{... | collective-permute-start | bytes 1572872 | tf_op jit(solution)/shard_map/ppermute | solution.py:54
  329.5 12.8 %collective-permute-start.13 = (bf16[128,2048]{1,0:T(8,128)(2,1)}, bf16[128,2048]{1,0:T(8,128)(2,1)}, u32[]{:S(2)}, u32[]{:S(2)}) collective-permute-start(bf16[128,2048]{1,0:T(8,128)(2,1)} %fusion.76), channel_id=1, source_target_pairs={{0,12},{4,0},{8,4},{12,8},{1,13},{5,1},{9,5},{13,9},{2,14},{6,2},{... | collective-permute-start | bytes 1572872 | tf_op jit(solution)/shard_map/ppermute | solution.py:54
  350.8 33.1 %collective-permute-done.23 = bf16[128,2048]{1,0:T(8,128)(2,1)S(1)} collective-permute-done((bf16[128,2048]{1,0:T(8,128)(2,1)S(1)}, bf16[128,2048]{1,0:T(8,128)(2,1)S(1)}, u32[]{:S(2)}, u32[]{:S(2)}) %collective-permute-start.23) | collective-permute-done | bytes 524320 | tf_op jit(solution)/shard_map/ppermute | solution.py:54
  423.3 11.2 copy.390
  451.4 15.5 %collective-permute-done.17 = bf16[3,1024,512]{2,1,0:T(8,128)(2,1)} collective-permute-done((bf16[3,1024,512]{2,1,0:T(8,128)(2,1)}, bf16[3,1024,512]{2,1,0:T(8,128)(2,1)}, u32[]{:S(2)}, u32[]{:S(2)}) %collective-permute-start.17) | collective-permute-done | bytes 3145760 | tf_op jit(solution)/shard_map/ppermute | solution.py:65
  466.9 67.0 %collective-permute-done.16 = bf16[3,1024,512]{2,1,0:T(8,128)(2,1)} collective-permute-done((bf16[3,1024,512]{2,1,0:T(8,128)(2,1)}, bf16[3,1024,512]{2,1,0:T(8,128)(2,1)}, u32[]{:S(2)}, u32[]{:S(2)}) %collective-permute-start.16) | collective-permute-done | bytes 3145760 | tf_op jit(solution)/shard_map/ppermute | solution.py:65
  533.8 14.6 %maximum_maximum_fusion = bf16[3,2048,1024]{2,1,0:T(8,128)(2,1)S(1)} fusion(bf16[3,1024,512]{2,1,0:T(8,128)(2,1)} %collective-permute-done.17, bf16[3,1024,512]{2,1,0:T(8,128)(2,1)} %collective-permute-done.16, bf16[3,1024,512]{2,1,0:T(8,128)(2,1)} %collective-permute-done.15, bf16[3,1024,512]{2,1,0:T(8,128)(2,1)} %bitcast.502), kind=kLoop, calls=%fused_computation.2 | loop fusion | flops 50331648 | bytes 25165824 | tf_op jit(solution)/shard_map/concatenate | solution.py:91
  566.9 14.0 %fusion.12 = (bf16[1024,1024]{1,0:T(8,128)(2,1)}, bf16[1024,1024]{1,0:T(8,128)(2,1)}, bf16[1024,1024]{1,0:T(8,128)(2,1)}, f32[1024,1024]{0,1:T(8,128)}) fusion(f32[1024,1024]{0,1:T(8,128)} %fusion.23, f32[1024,1024]{0,1:T(8,128)} %fusion.22, bf16[1024,2048]{1,0:T(8,128)(2,1)} %bitcast.482, bf16[3,2048,1024]{2,1,0:T(8,128)(2,1)} %copy-done.14), kind=kOutput, calls=%fused_computation.43 | convolution fusion | flops 4311744512 | bytes 27262976 | tf_op jit(solution)/shard_map/dot_general | solution.py:35
  611.3 11.6 add_convert_fusion.1
  659.7 22.3 %collective-permute-done.28 = bf16[128,2048]{1,0:T(8,128)(2,1)} collective-permute-done((bf16[128,2048]{1,0:T(8,128)(2,1)}, bf16[128,2048]{1,0:T(8,128)(2,1)}, u32[]{:S(2)}, u32[]{:S(2)}) %collective-permute-start.28) | collective-permute-done | bytes 524320 | tf_op jit(solution)/shard_map/ppermute | solution.py:54
  693.4 32.7 %collective-permute-done.20 = bf16[128,2048]{1,0:T(8,128)(2,1)S(1)} collective-permute-done((bf16[128,2048]{1,0:T(8,128)(2,1)S(1)}, bf16[128,2048]{1,0:T(8,128)(2,1)S(1)}, u32[]{:S(2)}, u32[]{:S(2)}) %collective-permute-start.20) | collective-permute-done | bytes 524320 | tf_op jit(solution)/shard_map/ppermute | solution.py:54
  726.9 11.0 collective-permute-start.32
  750.4 33.8 %collective-permute-done.31 = bf16[128,2048]{1,0:T(8,128)(2,1)S(1)} collective-permute-done((bf16[128,2048]{1,0:T(8,128)(2,1)S(1)}, bf16[128,2048]{1,0:T(8,128)(2,1)S(1)}, u32[]{:S(2)}, u32[]{:S(2)}) %collective-permute-start.31) | collective-permute-done | bytes 524320 | tf_op jit(solution)/shard_map/ppermute | solution.py:54
  799.4 12.5 %pad_maximum_fusion = f32[3,2,1024,2,512]{4,2,3,1,0:T(8,128)} fusion(f32[1,2,1024,2,512]{4,2,3,1,0:T(8,128)} %convolution_bitcast_fusion, f32[1,2,1024,2,512]{4,2,3,1,0:T(8,128)S(1)} %convolution_bitcast_fusion.1, f32[1,2,1024,2,512]{4,2,3,1,0:T(8,128)S(1)} %convolution_bitcast_fusion.2), kind=kLoop, calls=%fused_computation.1 | loop fusion | flops 12582912 | bytes 50331648 | tf_op jit(solution)/shard_map/stack | solution.py:219
  845.0 23.0 %collective-permute-done.43 = bf16[3,1024,512]{2,1,0:T(8,128)(2,1)} collective-permute-done((bf16[3,1024,512]{2,1,0:T(8,128)(2,1)}, bf16[3,1024,512]{2,1,0:T(8,128)(2,1)}, u32[]{:S(2)}, u32[]{:S(2)}) %collective-permute-start.43) | collective-permute-done | bytes 3145760 | tf_op jit(solution)/shard_map/ppermute | solution.py:65
  868.1 78.2 %collective-permute-done.42 = bf16[3,1024,512]{2,1,0:T(8,128)(2,1)} collective-permute-done((bf16[3,1024,512]{2,1,0:T(8,128)(2,1)}, bf16[3,1024,512]{2,1,0:T(8,128)(2,1)}, u32[]{:S(2)}, u32[]{:S(2)}) %collective-permute-start.42) | collective-permute-done | bytes 3145760 | tf_op jit(solution)/shard_map/ppermute | solution.py:65
  994.9 52.5 %collective-permute-done.37 = bf16[128,2048]{1,0:T(8,128)(2,1)S(1)} collective-permute-done((bf16[128,2048]{1,0:T(8,128)(2,1)S(1)}, bf16[128,2048]{1,0:T(8,128)(2,1)S(1)}, u32[]{:S(2)}, u32[]{:S(2)}) %collective-permute-start.37) | collective-permute-done | bytes 524320 | tf_op jit(solution)/shard_map/ppermute | solution.py:54
  1048.9 42.4 %collective-permute-done.36 = bf16[128,2048]{1,0:T(8,128)(2,1)S(1)} collective-permute-done((bf16[128,2048]{1,0:T(8,128)(2,1)S(1)}, bf16[128,2048]{1,0:T(8,128)(2,1)S(1)}, u32[]{:S(2)}, u32[]{:S(2)}) %collective-permute-start.36) | collective-permute-done | bytes 524320 | tf_op jit(solution)/shard_map/ppermute | solution.py:54
  1100.9 20.4 %all-to-all-start.2 = ((bf16[4,1024,128]{2,0,1:T(4,128)(2,1)}), bf16[4,1024,128]{2,0,1:T(4,128)(2,1)S(1)}, u32[]{:S(2)}, u32[]{:S(2)}) async-start(bf16[4,1024,128]{2,0,1:T(4,128)(2,1)} %copy.371), calls=%async_computation.2 | async-start | bytes 2097152 | tf_op jit(solution)/shard_map/all_to_all | solution.py:101
  1158.8 40.1 %psum.7 = f32[]{:T(128)} all-reduce(f32[]{:T(128)S(6)} %add.425), channel_id=1, replica_groups=mesh['fsdp'=2,'ctx'=4,'tp'=4] {'fsdp','ctx','tp'}, use_global_device_ids=true, to_apply=%region_15.16 | all-reduce | flops 1 | bytes 8 | tf_op jit(solution)/shard_map/psum | solution.py:257
  (390 shorter events, 452.2 us)
Async XLA Ops:
  171.8 213.8 %all-to-all-start.1 = ((bf16[3,256,2048]{1,0,2:T(4,128)(2,1)}), bf16[3,256,2048]{1,0,2:T(4,128)(2,1)}, u32[]{:S(2)}, u32[]{:S(2)}) async-start(bf16[3,256,2048]{1,0,2:T(4,128)(2,1)} %pad_maximum_fusion.4), calls=%async_computation.1 | async-start | bytes 8388608 | tf_op jit(solution)/shard_map/all_to_all | solution.py:83
  177.0 944.3 %all-gather.3.cloned.1.call-start = ((), (), s32[]{:S(2)}) async-start(), calls=%async_computation.4 | async-start | bytes 2621440 | tf_op jit(solution)/shard_map/all_gather | solution.py:218
  180.3 81.0 %collective-permute-start.10 = (bf16[128,2048]{1,0:T(8,128)(2,1)S(1)}, bf16[128,2048]{1,0:T(8,128)(2,1)S(1)}, u32[]{:S(2)}, u32[]{:S(2)}) collective-permute-start(bf16[128,2048]{1,0:T(8,128)(2,1)S(1)} %get-tuple-element.88), channel_id=1, source_target_pairs={{0,4},{4,8},{8,12},{12,0},{1,5},{5,9},{9,13},{13,1},{2,6},{6,10},{... | collective-permute-start | bytes 1572872 | tf_op jit(solution)/shard_map/ppermute | solution.py:54
  182.4 145.3 %collective-permute-start.9 = (bf16[128,2048]{1,0:T(8,128)(2,1)S(1)}, bf16[128,2048]{1,0:T(8,128)(2,1)S(1)}, u32[]{:S(2)}, u32[]{:S(2)}) collective-permute-start(bf16[128,2048]{1,0:T(8,128)(2,1)S(1)} %get-tuple-element.89), channel_id=1, source_target_pairs={{0,8},{4,12},{8,0},{12,4},{1,9},{5,13},{9,1},{13,5},{2,10},{6,14},... | collective-permute-start | bytes 1572872 | tf_op jit(solution)/shard_map/ppermute | solution.py:54
  184.8 143.0 %collective-permute-start.8 = (bf16[128,2048]{1,0:T(8,128)(2,1)S(1)}, bf16[128,2048]{1,0:T(8,128)(2,1)S(1)}, u32[]{:S(2)}, u32[]{:S(2)}) collective-permute-start(bf16[128,2048]{1,0:T(8,128)(2,1)S(1)} %get-tuple-element.87), channel_id=1, source_target_pairs={{0,12},{4,0},{8,4},{12,8},{1,13},{5,1},{9,5},{13,9},{2,14},{6,2},{... | collective-permute-start | bytes 1572872 | tf_op jit(solution)/shard_map/ppermute | solution.py:54
  187.6 155.2 %collective-permute-start.24 = (bf16[128,2048]{1,0:T(8,128)(2,1)S(1)}, bf16[128,2048]{1,0:T(8,128)(2,1)S(1)}, u32[]{:S(2)}, u32[]{:S(2)}) collective-permute-start(bf16[128,2048]{1,0:T(8,128)(2,1)S(1)} %get-tuple-element.108), channel_id=1, source_target_pairs={{0,12},{4,0},{8,4},{12,8},{1,13},{5,1},{9,5},{13,9},{2,14},{6,2},{... | collective-permute-start | bytes 1572872 | tf_op jit(solution)/shard_map/ppermute | solution.py:54
  188.2 195.7 %collective-permute-start.23 = (bf16[128,2048]{1,0:T(8,128)(2,1)S(1)}, bf16[128,2048]{1,0:T(8,128)(2,1)S(1)}, u32[]{:S(2)}, u32[]{:S(2)}) collective-permute-start(bf16[128,2048]{1,0:T(8,128)(2,1)S(1)} %get-tuple-element.108), channel_id=1, source_target_pairs={{0,8},{4,12},{8,0},{12,4},{1,9},{5,13},{9,1},{13,5},{2,10},{6,14},... | collective-permute-start | bytes 1572872 | tf_op jit(solution)/shard_map/ppermute | solution.py:54
  261.3 122.6 %collective-permute-start.22 = (bf16[128,2048]{1,0:T(8,128)(2,1)S(1)}, bf16[128,2048]{1,0:T(8,128)(2,1)S(1)}, u32[]{:S(2)}, u32[]{:S(2)}) collective-permute-start(bf16[128,2048]{1,0:T(8,128)(2,1)S(1)} %get-tuple-element.108), channel_id=1, source_target_pairs={{0,4},{4,8},{8,12},{12,0},{1,5},{5,9},{9,13},{13,1},{2,6},{6,10},{... | collective-permute-start | bytes 1572872 | tf_op jit(solution)/shard_map/ppermute | solution.py:54
  329.5 66.8 %collective-permute-start.13 = (bf16[128,2048]{1,0:T(8,128)(2,1)}, bf16[128,2048]{1,0:T(8,128)(2,1)}, u32[]{:S(2)}, u32[]{:S(2)}) collective-permute-start(bf16[128,2048]{1,0:T(8,128)(2,1)} %fusion.76), channel_id=1, source_target_pairs={{0,12},{4,0},{8,4},{12,8},{1,13},{5,1},{9,5},{13,9},{2,14},{6,2},{... | collective-permute-start | bytes 1572872 | tf_op jit(solution)/shard_map/ppermute | solution.py:54
  394.7 72.2 %collective-permute-start.17 = (bf16[3,1024,512]{2,1,0:T(8,128)(2,1)}, bf16[3,1024,512]{2,1,0:T(8,128)(2,1)}, u32[]{:S(2)}, u32[]{:S(2)}) collective-permute-start(bf16[3,1024,512]{2,1,0:T(8,128)(2,1)} %bitcast.499), channel_id=1, source_target_pairs={{0,18},{1,19},{2,16},{3,17},{16,2},{17,3},{18,0},{19,1},{4,22},{5,... | collective-permute-start | bytes 9437192 | tf_op jit(solution)/shard_map/ppermute | solution.py:65
  396.3 137.5 %collective-permute-start.16 = (bf16[3,1024,512]{2,1,0:T(8,128)(2,1)}, bf16[3,1024,512]{2,1,0:T(8,128)(2,1)}, u32[]{:S(2)}, u32[]{:S(2)}) collective-permute-start(bf16[3,1024,512]{2,1,0:T(8,128)(2,1)} %bitcast.500), channel_id=1, source_target_pairs={{0,2},{1,3},{2,0},{3,1},{16,18},{17,19},{18,16},{19,17},{4,6},{5,7... | collective-permute-start | bytes 9437192 | tf_op jit(solution)/shard_map/ppermute | solution.py:65
  405.8 128.1 %collective-permute-start.15 = (bf16[3,1024,512]{2,1,0:T(8,128)(2,1)}, bf16[3,1024,512]{2,1,0:T(8,128)(2,1)}, u32[]{:S(2)}, u32[]{:S(2)}) collective-permute-start(bf16[3,1024,512]{2,1,0:T(8,128)(2,1)} %bitcast.501), channel_id=1, source_target_pairs={{0,16},{1,17},{2,18},{3,19},{16,0},{17,1},{18,2},{19,3},{4,20},{5,... | collective-permute-start | bytes 9437192 | tf_op jit(solution)/shard_map/ppermute | solution.py:65
  648.2 77.9 %collective-permute-start.20 = (bf16[128,2048]{1,0:T(8,128)(2,1)S(1)}, bf16[128,2048]{1,0:T(8,128)(2,1)S(1)}, u32[]{:S(2)}, u32[]{:S(2)}) collective-permute-start(bf16[128,2048]{1,0:T(8,128)(2,1)S(1)} %get-tuple-element.84), channel_id=1, source_target_pairs={{0,8},{4,12},{8,0},{12,4},{1,9},{5,13},{9,1},{13,5},{2,10},{6,14},... | collective-permute-start | bytes 1572872 | tf_op jit(solution)/shard_map/ppermute | solution.py:54
  659.7 66.4 %collective-permute-start.19 = (bf16[128,2048]{1,0:T(8,128)(2,1)S(1)}, bf16[128,2048]{1,0:T(8,128)(2,1)S(1)}, u32[]{:S(2)}, u32[]{:S(2)}) collective-permute-start(bf16[128,2048]{1,0:T(8,128)(2,1)S(1)} %get-tuple-element.82), channel_id=1, source_target_pairs={{0,12},{4,0},{8,4},{12,8},{1,13},{5,1},{9,5},{13,9},{2,14},{6,2},{... | collective-permute-start | bytes 1572872 | tf_op jit(solution)/shard_map/ppermute | solution.py:54
  795.9 72.2 %collective-permute-start.43 = (bf16[3,1024,512]{2,1,0:T(8,128)(2,1)}, bf16[3,1024,512]{2,1,0:T(8,128)(2,1)}, u32[]{:S(2)}, u32[]{:S(2)}) collective-permute-start(bf16[3,1024,512]{2,1,0:T(8,128)(2,1)} %get-tuple-element.51), channel_id=1, source_target_pairs={{0,18},{1,19},{2,16},{3,17},{16,2},{17,3},{18,0},{19,1},{4,22},{5,... | collective-permute-start | bytes 9437192 | tf_op jit(solution)/shard_map/ppermute | solution.py:65
  797.6 148.7 %collective-permute-start.42 = (bf16[3,1024,512]{2,1,0:T(8,128)(2,1)}, bf16[3,1024,512]{2,1,0:T(8,128)(2,1)}, u32[]{:S(2)}, u32[]{:S(2)}) collective-permute-start(bf16[3,1024,512]{2,1,0:T(8,128)(2,1)} %get-tuple-element.52), channel_id=1, source_target_pairs={{0,2},{1,3},{2,0},{3,1},{16,18},{17,19},{18,16},{19,17},{4,6},{5,7... | collective-permute-start | bytes 9437192 | tf_op jit(solution)/shard_map/ppermute | solution.py:65
  798.9 147.4 %collective-permute-start.41 = (bf16[3,1024,512]{2,1,0:T(8,128)(2,1)}, bf16[3,1024,512]{2,1,0:T(8,128)(2,1)}, u32[]{:S(2)}, u32[]{:S(2)}) collective-permute-start(bf16[3,1024,512]{2,1,0:T(8,128)(2,1)} %get-tuple-element.50), channel_id=1, source_target_pairs={{0,16},{1,17},{2,18},{3,19},{16,0},{17,1},{18,2},{19,3},{4,20},{5,... | collective-permute-start | bytes 9437192 | tf_op jit(solution)/shard_map/ppermute | solution.py:65
  845.0 135.0 %collective-permute-start.34 = (bf16[4,128,2048]{2,1,0:T(8,128)(2,1)}, bf16[4,128,2048]{2,1,0:T(8,128)(2,1)}, u32[]{:S(2)}, u32[]{:S(2)}) collective-permute-start(bf16[4,128,2048]{2,1,0:T(8,128)(2,1)} %slice_bitcast_fusion.14), channel_id=1, source_target_pairs={{0,1},{1,0},{2,3},{3,2},{4,5},{5,4},{6,7},{7,6},{8,9},{9,8},{10,11... | collective-permute-start | bytes 6291464 | tf_op jit(solution)/shard_map/ppermute | solution.py:57
  958.2 142.7 %all-to-all-start.3 = ((bf16[3,1024,512]{2,0,1:T(4,128)(2,1)}), bf16[3,1024,512]{2,0,1:T(4,128)(2,1)}, u32[]{:S(2)}, u32[]{:S(2)}) async-start(bf16[3,1024,512]{2,0,1:T(4,128)(2,1)} %copy.377), calls=%async_computation.3 | async-start | bytes 8388608 | tf_op jit(solution)/shard_map/all_to_all | solution.py:101
  963.1 263.3 %all-gather.5.cloned.1.call-start = ((), (), s32[]{:S(2)}) async-start(), calls=%async_computation.5 | async-start | bytes 5242880 | tf_op jit(solution)/shard_map/all_gather | solution.py:250
  985.3 105.9 %collective-permute-start.36 = (bf16[128,2048]{1,0:T(8,128)(2,1)S(1)}, bf16[128,2048]{1,0:T(8,128)(2,1)S(1)}, u32[]{:S(2)}, u32[]{:S(2)}) collective-permute-start(bf16[128,2048]{1,0:T(8,128)(2,1)S(1)} %get-tuple-element.72), channel_id=1, source_target_pairs={{0,8},{4,12},{8,0},{12,4},{1,9},{5,13},{9,1},{13,5},{2,10},{6,14},... | collective-permute-start | bytes 1572872 | tf_op jit(solution)/shard_map/ppermute | solution.py:54
  987.7 103.6 %collective-permute-start.35 = (bf16[128,2048]{1,0:T(8,128)(2,1)S(1)}, bf16[128,2048]{1,0:T(8,128)(2,1)S(1)}, u32[]{:S(2)}, u32[]{:S(2)}) collective-permute-start(bf16[128,2048]{1,0:T(8,128)(2,1)S(1)} %get-tuple-element.70), channel_id=1, source_target_pairs={{0,12},{4,0},{8,4},{12,8},{1,13},{5,1},{9,5},{13,9},{2,14},{6,2},{... | collective-permute-start | bytes 1572872 | tf_op jit(solution)/shard_map/ppermute | solution.py:54
  991.9 104.8 %collective-permute-start.40 = (bf16[4,1024,128]{2,1,0:T(8,128)(2,1)}, bf16[4,1024,128]{2,1,0:T(8,128)(2,1)}, u32[]{:S(2)}, u32[]{:S(2)}) collective-permute-start(bf16[4,1024,128]{2,1,0:T(8,128)(2,1)} %get-tuple-element.65), channel_id=1, source_target_pairs={{0,18},{1,19},{2,16},{3,17},{16,2},{17,3},{18,0},{19,1},{4,22},{5,... | collective-permute-start | bytes 3145736 | tf_op jit(solution)/shard_map/ppermute | solution.py:65
  993.6 103.2 %collective-permute-start.39 = (bf16[4,1024,128]{2,1,0:T(8,128)(2,1)}, bf16[4,1024,128]{2,1,0:T(8,128)(2,1)}, u32[]{:S(2)}, u32[]{:S(2)}) collective-permute-start(bf16[4,1024,128]{2,1,0:T(8,128)(2,1)} %get-tuple-element.66), channel_id=1, source_target_pairs={{0,2},{1,3},{2,0},{3,1},{16,18},{17,19},{18,16},{19,17},{4,6},{5,7... | collective-permute-start | bytes 3145736 | tf_op jit(solution)/shard_map/ppermute | solution.py:65
  (105 other events, 2941.7 us)
Sparse Core Ops, SparseCore 0:
  812.9 78.6 all-gather.2
  1093.7 43.1 all-gather.4

commit v2 on v1

v2 whole, which is shorter than its diff:
```python
import functools

import jax
import jax.numpy as jnp
from jax import lax
from jax.experimental import pallas as pl
from jax.experimental.pallas import tpu as pltpu
from jax.sharding import PartitionSpec as P

HEAD_DIM = 128
STEP = 10
EPS_NORM = 1e-05
BETA_ONE = 0.9
BETA_TWO = 0.95
EPS_ADAM = 1e-08
DECAY = 0.1
MAX_NORM = 1.0
NEG_FILL = -1e30
BF = jnp.bfloat16
F32 = jnp.float32
MESH = pl.DeviceIdType.MESH
ANY = pl.BlockSpec(memory_space=pl.ANY)
VMEM = pl.BlockSpec(memory_space=pltpu.VMEM)
ROWS = 16


def mean_spread(values):
    centre = values - jnp.mean(values, axis=-1, keepdims=True)
    spread = jnp.mean(centre * centre, axis=-1, keepdims=True)
    scale = lax.rsqrt(spread + EPS_NORM)
    return centre * scale, scale


def norm_back(grad, normed, scale):
    return scale * (
        grad
        - jnp.mean(grad, axis=-1, keepdims=True)
        - normed * jnp.mean(grad * normed, axis=-1, keepdims=True)
    )


def dot(left, right, dims):
    return lax.dot_general(left, right, (dims, ((), ())), preferred_element_type=F32)


def adam_step(weight, grad_sum, first, second, clip_factor, learn_rate):
    clipped = grad_sum * clip_factor
    first_new = BETA_ONE * first + (1.0 - BETA_ONE) * clipped
    second_new = BETA_TWO * second + (1.0 - BETA_TWO) * clipped * clipped
    first_hat = first_new / (1.0 - BETA_ONE**STEP)
    second_hat = second_new / (1.0 - BETA_TWO**STEP)
    weight_new = weight - learn_rate * (
        first_hat / (jnp.sqrt(second_hat) + EPS_ADAM) + DECAY * weight
    )
    return (first_new, second_new, weight_new)


class Place:
    def __init__(self, sizes):
        self.n_f, self.n_c, self.n_t = sizes
        self.f, self.c, self.t = (lax.axis_index(a) for a in ("fsdp", "ctx", "tp"))
        self.hi, self.lo = self.t // 2, lax.rem(self.t, 2)
        self.core = (self.f, self.c, self.t + 1 - 2 * self.lo)
        self.block = self.c * 2 + self.lo
        self.pairs = [(s, o) for o in range(2) for s in range(self.n_f) if s or o]

    def ctx(self, shift):
        return lax.rem(self.c + shift + self.n_c, self.n_c)

    def fsdp(self, shift):
        return lax.rem(self.f + shift + self.n_f, self.n_f)

    def other(self, o):
        return self.hi + o * (1 - 2 * self.hi)

    def z(self, shift):
        return (self.f, self.ctx(shift), self.t)

    def xy(self, shift, o):
        return (self.fsdp(shift), self.c, self.t + o * (2 - 4 * self.hi))

    def greet(self, peers):
        barrier = pltpu.get_barrier_semaphore()
        for peer in peers:
            pl.semaphore_signal(barrier, inc=1, device_id=peer, device_id_type=MESH)
        pl.semaphore_wait(barrier, len(peers))

    def all_z(self):
        return [self.z(s) for s in range(1, self.n_c)]

    def all_xy(self):
        return [self.xy(s, o) for s, o in self.pairs]


def remote(src, dst, send, recv, peer):
    return pltpu.make_async_remote_copy(
        src_ref=src, dst_ref=dst, send_sem=send, recv_sem=recv, device_id=peer, device_id_type=MESH
    )


def by_rows(count, step):
    @pl.loop(0, count // ROWS)
    def _(i):
        step(pl.ds(pl.multiple_of(i * ROWS, ROWS), ROWS))


class Gather:
    def __init__(self, at, src, out, send, recv, local):
        self.at, self.src, self.out, self.send, self.recv = at, src, out, send, recv
        self.local = pltpu.make_async_copy(src, out.at[at.block], local)
        self.far, self.near = [], []

    def start(self):
        at = self.at
        for s in range(1, at.n_c):
            copy = remote(
                self.src, self.out.at[at.block], self.send.at[s], self.recv.at[s], at.z(s)
            )
            copy.start()
            self.far.append(copy)
        copy = remote(
            self.src, self.out.at[at.block], self.send.at[0], self.recv.at[0], at.core
        )
        copy.start()
        self.near.append(copy)
        self.local.start()

    def forward(self):
        at = self.at
        for s in range(1, at.n_c):
            self.far[s - 1].wait_recv()
            block = self.out.at[at.ctx(-s) * 2 + at.lo]
            copy = remote(
                block, block, self.send.at[at.n_c + s], self.recv.at[at.n_c + s], at.core
            )
            copy.start()
            self.near.append(copy)

    def finish(self):
        for copy in self.far:
            copy.wait_send()
        for copy in self.near:
            copy.wait()
        self.local.wait()


def gather_sems(n_c):
    return [
        pltpu.SemaphoreType.DMA((2 * n_c,)),
        pltpu.SemaphoreType.DMA((2 * n_c,)),
        pltpu.SemaphoreType.DMA,
    ]


class Scatter:
    def __init__(self, at, partial, own, near, sent, got, send, recv, local):
        self.at, self.own, self.near, self.sent, self.got = at, own, near, sent, got
        self.send, self.recv = send, recv
        self.locals, self.cores, self.far = [], [], []
        for s in range(at.n_c):
            c = at.ctx(s)
            self.locals.append(
                pltpu.make_async_copy(partial.at[c * 2 + at.lo], own.at[s], local.at[s])
            )
            self.cores.append(
                remote(
                    partial.at[c * 2 + 1 - at.lo], near.at[s], send.at[s], recv.at[s], at.core
                )
            )

    def start(self):
        order = [*range(1, self.at.n_c), 0]
        for s in order:
            self.cores[s].start()
            self.locals[s].start()

    def pass_on(self):
        at = self.at
        for s in range(1, at.n_c):
            self.cores[s].wait_recv()
            self.locals[s].wait()

            def add(rows, s=s):
                self.sent[s - 1, rows] = (
                    self.own[s, rows].astype(F32) + self.near[s, rows].astype(F32)
                ).astype(BF)

            by_rows(self.own.shape[1], add)
            copy = remote(
                self.sent.at[s - 1],
                self.got.at[s - 1],
                self.send.at[at.n_c + s],
                self.recv.at[at.n_c + s],
                at.z(s),
            )
            copy.start()
            self.far.append(copy)
        self.cores[0].wait_recv()
        self.locals[0].wait()

    def arrive(self):
        for copy in self.far:
            copy.wait_recv()

    def total(self, rows):
        value = self.own[0, rows].astype(F32) + self.near[0, rows].astype(F32)
        for s in range(1, self.at.n_c):
            value = value + self.got[s - 1, rows].astype(F32)
        return value

    def finish(self):
        for copy in (*self.cores, *self.far):
            copy.wait_send()


def scatter_scratch(n_c, half, width):
    return [
        pltpu.VMEM((n_c, half, width), BF),
        pltpu.VMEM((n_c, half, width), BF),
        pltpu.VMEM((n_c - 1, half, width), BF),
        pltpu.VMEM((n_c - 1, half, width), BF),
        pltpu.SemaphoreType.DMA((2 * n_c,)),
        pltpu.SemaphoreType.DMA((2 * n_c,)),
        pltpu.SemaphoreType.DMA((n_c,)),
    ]


class Swap:
    def __init__(self, at, shard, full, send, recv, local):
        self.at = at
        rows, width = shard.shape[1], full.shape[3]
        here = pl.ds((at.f * at.n_c + at.c) * rows, rows)
        target = full.at[at.hi, :, here, :]

        def columns(c):
            return shard.at[:, :, pl.ds(pl.multiple_of(c * width, 128), width)]

        self.local = pltpu.make_async_copy(columns(at.c), target, local)
        self.far = [
            remote(columns(at.ctx(s)), target, send.at[s], recv.at[s], at.z(s))
            for s in range(1, at.n_c)
        ]

    def start(self):
        self.local.start()
        for copy in self.far:
            copy.start()

    def wait(self):
        self.local.wait()
        for copy in self.far:
            copy.wait()


class Spread:
    def __init__(self, at, full, send, recv):
        height = full.shape[2] // at.n_f
        part = full.at[at.hi, :, pl.ds(at.f * height, height), :]
        self.copies = [
            remote(part, part, send.at[i], recv.at[i], at.xy(s, o))
            for i, (s, o) in enumerate(at.pairs)
        ]

    def start(self):
        for copy in self.copies:
            copy.start()

    def wait(self):
        for copy in self.copies:
            copy.wait()


class Collect:
    def __init__(self, at, partial, got, send, recv):
        height = partial.shape[2] // at.n_f
        self.copies = []
        for i, (s, o) in enumerate(at.pairs):
            part = partial.at[at.other(o), :, pl.ds(at.fsdp(s) * height, height), :]
            self.copies.append(remote(part, got.at[i], send.at[i], recv.at[i], at.xy(s, o)))

    def start(self):
        for copy in self.copies:
            copy.start()

    def wait(self):
        for copy in self.copies:
            copy.wait()


class Return:
    def __init__(self, at, summed, shard, send, recv, local):
        rows, width = shard.shape[1], summed.shape[2]
        target = shard.at[:, :, pl.ds(pl.multiple_of(at.c * width, 128), width)]

        def part(c):
            return summed.at[:, pl.ds(pl.multiple_of(c * rows, rows), rows), :]

        self.local = pltpu.make_async_copy(part(at.c), target, local)
        self.far = [
            remote(part(at.ctx(s)), target, send.at[s], recv.at[s], at.z(s))
            for s in range(1, at.n_c)
        ]

    start = Swap.start
    wait = Swap.wait


def dma(count):
    return pltpu.SemaphoreType.DMA((count,))


def make_shards(mesh):
    sizes = tuple(mesh.shape[a] for a in ("fsdp", "ctx", "tp"))
    n_f, n_c, n_t = sizes
    pairs = 2 * n_f - 1

    def call(kernel, name, collective, outs, ins, out_specs, scratch, aliases=None, vmem=40):
        return pl.pallas_call(
            kernel,
            out_shape=outs,
            in_specs=ins,
            out_specs=out_specs,
            scratch_shapes=scratch,
            input_output_aliases=aliases or {},
            compiler_params=pltpu.CompilerParams(
                collective_id=collective, has_side_effects=True, vmem_limit_bytes=vmem << 20
            ),
            name=name,
        )

    def first_kernel(
        a1_ref, att_ref, ff_ref, rows_ref, attw_ref, ffw_ref, gs, gr, gl, s1, r1, l1, s2, r2, l2, s3, r3
    ):
        at = Place(sizes)
        at.greet([at.core, *at.all_z(), *at.all_xy()])
        gather = Gather(at, a1_ref, rows_ref, gs, gr, gl)
        swap_att = Swap(at, att_ref, attw_ref, s1, r1, l1)
        swap_ff = Swap(at, ff_ref, ffw_ref, s2, r2, l2)
        swap_att.start()
        gather.start()
        swap_ff.start()
        swap_att.wait()
        spread = Spread(at, attw_ref, s3, r3)
        spread.start()
        gather.forward()
        gather.finish()
        spread.wait()
        swap_ff.wait()

    def second_kernel(
        part_ref, x_ref, cot_ref, ffw_in, a2_ref, cots_ref, mid_ref, ffw_ref,
        own, near, sent, got, ss, sr, sl, low, s1, r1, l1, s2, r2, l2, s3, r3,
    ):
        at = Place(sizes)
        at.greet([at.core, *at.all_z(), *at.all_xy()])
        scatter = Scatter(at, part_ref, own, near, sent, got, ss, sr, sl)
        spread = Spread(at, ffw_ref, s3, r3)
        cots = Gather(at, cot_ref, cots_ref, s1, r1, l1)
        scatter.start()
        spread.start()
        scatter.pass_on()
        cots.start()
        scatter.arrive()

        def norm(rows):
            mid = x_ref[rows].astype(F32) + scatter.total(rows)
            mid_ref[rows] = mid
            low[rows] = mean_spread(mid)[0].astype(BF)

        by_rows(x_ref.shape[0], norm)
        a2 = Gather(at, low, a2_ref, s2, r2, l2)
        a2.start()
        cots.forward()
        a2.forward()
        cots.finish()
        a2.finish()
        scatter.finish()
        spread.wait()

    def third_kernel(
        part_ref, branch_ref, mid_ref, cot_ref, grad_ref, rows_ref, block_ref, own_ref, got_ref,
        own, near, sent, got, ss, sr, sl, own2, near2, sent2, got2, ss2, sr2, sl2, low, s1, r1, l1, s3, r3,
    ):
        at = Place(sizes)
        at.greet([at.core, *at.all_z(), *at.all_xy()])
        scatter = Scatter(at, part_ref, own, near, sent, got, ss, sr, sl)
        branch = Scatter(at, branch_ref, own2, near2, sent2, got2, ss2, sr2, sl2)
        collect = Collect(at, grad_ref, got_ref, s3, r3)
        scatter.start()
        collect.start()
        scatter.pass_on()
        branch.start()
        branch.pass_on()
        scatter.arrive()

        def norm(rows):
            normed, scale = mean_spread(mid_ref[rows])
            grad = cot_ref[rows].astype(F32) + norm_back(scatter.total(rows), normed, scale)
            own_ref[rows] = grad
            low[rows] = grad.astype(BF)

        by_rows(mid_ref.shape[0], norm)
        gather = Gather(at, low, rows_ref, s1, r1, l1)
        gather.start()
        branch.arrive()

        def add(rows):
            block_ref[rows] = (mid_ref[rows] + branch.total(rows)).astype(BF)

        by_rows(mid_ref.shape[0], add)
        gather.forward()
        gather.finish()
        scatter.finish()
        branch.finish()
        collect.wait()

    def fourth_kernel(
        part_ref, x_ref, mid_ref, block_ref, att_ref, ff_ref, input_ref, out_ref, attg_ref, ffg_ref,
        own, near, sent, got, ss, sr, sl, mine, theirs, total, low, s1, r1, l1, s2, r2, l2, s3, r3, s4, r4, l4,
    ):
        at = Place(sizes)
        tps = [(at.f, at.c, lax.rem(at.t + s, n_t)) for s in range(1, n_t)]
        at.greet([*tps, *at.all_z(), *[at.xy(s, o) for s, o in at.pairs if s]])
        scatter = Scatter(at, part_ref, own, near, sent, got, ss, sr, sl)
        collect = Collect(at, att_ref, theirs, s3, r3)
        height = att_ref.shape[2] // n_f
        kept = pltpu.make_async_copy(
            att_ref.at[at.hi, :, pl.ds(at.f * height, height), :], mine, l4.at[0]
        )
        give_ff = Return(at, ff_ref, ffg_ref, s2, r2, l2)
        scatter.start()
        collect.start()
        kept.start()

        def tp_gather(src, dst, k):
            copies = [
                remote(src, dst.at[at.t], s4.at[k, i], r4.at[k, i], peer) for i, peer in enumerate(tps)
            ]
            keep = pltpu.make_async_copy(src, dst.at[at.t], l4.at[1 + k])
            for copy in (*copies, keep):
                copy.start()
            return [*copies, keep]

        waits = tp_gather(block_ref, out_ref, 0)
        scatter.pass_on()
        kept.wait()
        collect.wait()
        for m in range(mine.shape[0]):

            def add(rows, m=m):
                value = mine[m, rows].astype(F32)
                for i in range(pairs):
                    value = value + theirs[i, m, rows].astype(F32)
                total[m, rows] = value.astype(BF)

            by_rows(height, add)
        give_att = Return(at, total, attg_ref, s1, r1, l1)
        give_att.start()
        give_ff.start()
        scatter.arrive()

        def norm(rows):
            normed, scale = mean_spread(x_ref[rows].astype(F32))
            low[rows] = mid_ref[rows] + norm_back(scatter.total(rows), normed, scale)

        by_rows(mid_ref.shape[0], norm)
        waits += tp_gather(low, input_ref, 1)
        for copy in waits:
            copy.wait()
        scatter.finish()
        give_att.wait()
        give_ff.wait()

    def norm_kernel(value_ref, out_ref, everyone, send, recv):
        f, c, t = (lax.axis_index(a) for a in ("fsdp", "ctx", "tp"))
        me = (f * n_c + c) * n_t + t
        count = n_f * n_c * n_t

        def device(i):
            i = lax.rem(me + i, count)
            return (i // (n_c * n_t), lax.rem(i // n_t, n_c), lax.rem(i, n_t))

        barrier = pltpu.get_barrier_semaphore()
        for i in range(1, count):
            pl.semaphore_signal(barrier, inc=1, device_id=device(i), device_id_type=MESH)
        pl.semaphore_wait(barrier, count - 1)
        copies = [
            remote(value_ref, everyone.at[i], send.at[i], recv.at[i], device(i))
            for i in range(1, count)
        ]
        for copy in copies:
            copy.start()
        everyone[0] = value_ref[...]
        for copy in copies:
            copy.wait()
        out_ref[...] = jnp.sum(everyone[...], axis=0)

    def shards(
        tokens,
        cotangent,
        lengths,
        deal,
        att_proj,
        attn_out,
        ff_proj,
        ff_out,
        att_proj_first,
        attn_out_first,
        ff_proj_first,
        ff_out_first,
        att_proj_second,
        attn_out_second,
        ff_proj_second,
        ff_out_second,
    ):
        t_at = lax.axis_index("tp")
        f_at = lax.axis_index("fsdp")
        pack_at = t_at // 2
        packs, row_count, width = tokens.shape
        half = row_count // 2
        pack_len = deal.shape[1]
        blocks = n_c * 2
        score_scale = HEAD_DIM ** (-0.5)
        rows_bf = jax.ShapeDtypeStruct((blocks, half, width), BF)
        own_f32 = jax.ShapeDtypeStruct((half, width), F32)
        own_bf = jax.ShapeDtypeStruct((half, width), BF)

        def own_rows(array):
            rows = array.reshape(packs * 2, half, width)
            return lax.dynamic_index_in_dim(rows, t_at, 0, keepdims=False)

        own_tokens = own_rows(tokens)
        own_cot = own_rows(cotangent)
        att_low = jnp.concatenate([att_proj, attn_out[None]]).astype(BF)
        ff_low = jnp.concatenate([ff_proj, ff_out[None]]).astype(BF)
        normed_one, _ = mean_spread(own_tokens.astype(F32))
        att_cols, ff_cols = att_low.shape[2] // n_c, ff_low.shape[2] // n_c
        act_one, att_w, ff_w = call(
            first_kernel,
            "first",
            0,
            (
                rows_bf,
                jax.ShapeDtypeStruct((2, 4, width, att_cols), BF),
                jax.ShapeDtypeStruct((2, 3, width, ff_cols), BF),
            ),
            [ANY] * 3,
            (ANY,) * 3,
            gather_sems(n_c)
            + [dma(n_c), dma(n_c), pltpu.SemaphoreType.DMA] * 2
            + [dma(pairs), dma(pairs)],
        )(normed_one.astype(BF), att_low, ff_low)
        act_one = act_one.reshape(pack_len, width)

        places = lax.dynamic_index_in_dim(deal, pack_at, 0, keepdims=False)
        length_row = lax.dynamic_index_in_dim(lengths, pack_at, 0, keepdims=False)
        seqs = lengths.shape[1]
        before = jnp.arange(seqs)[:, None] > jnp.arange(seqs)[None, :]
        starts = jnp.sum(jnp.where(before, length_row[None, :], 0), axis=1)
        inside = (places[:, None] >= starts[None, :]) & (
            places[:, None] < (starts + length_row)[None, :]
        )
        firsts = jnp.sum(jnp.where(inside, starts[None, :], 0), axis=1)
        allowed = (places[None, :] <= places[:, None]) & (places[None, :] >= firsts[:, None])
        freq_steps = jnp.arange(HEAD_DIM // 2, dtype=F32)
        inverse = jnp.power(10000.0, -2.0 * freq_steps / HEAD_DIM)
        angles = (places - firsts).astype(F32)[:, None] * inverse[None, :]
        cos_table, sine_table = jnp.cos(angles), jnp.sin(angles)

        def turn(values, sign):
            low, high = values[..., : HEAD_DIM // 2], values[..., HEAD_DIM // 2 :]
            sine = sign * sine_table
            return jnp.concatenate(
                [low * cos_table - high * sine, high * cos_table + low * sine], axis=-1
            )

        def heads_of(rows, matrix):
            return jnp.stack([dot(rows, att_w[y, matrix], ((1,), (0,))) for y in range(2)])

        query = turn(heads_of(act_one, 0), 1.0).astype(BF)
        key = turn(heads_of(act_one, 1), 1.0).astype(BF)
        value = heads_of(act_one, 2).astype(BF)
        scores = (
            jnp.einsum("htd,hkd->htk", query, key, preferred_element_type=F32) * score_scale
        )
        scores = jnp.where(allowed[None], scores, NEG_FILL)
        exp_scores = jnp.exp(scores - jnp.max(scores, axis=2, keepdims=True))
        probs = exp_scores / jnp.sum(exp_scores, axis=2, keepdims=True)
        probs_low = probs.astype(BF)
        attended = jnp.einsum(
            "htk,hkd->htd", probs_low, value, preferred_element_type=F32
        ).astype(BF)
        out_part = sum(dot(attended[y], att_w[y, 3], ((1,), (1,))) for y in range(2))
        act_two, cot_rows, resid_mid, ff_w = call(
            second_kernel,
            "second",
            1,
            (rows_bf, rows_bf, own_f32, jax.ShapeDtypeStruct(ff_w.shape, BF)),
            [ANY, VMEM, VMEM, ANY],
            (ANY, ANY, VMEM, ANY),
            scatter_scratch(n_c, half, width)
            + [pltpu.VMEM((half, width), BF)]
            + gather_sems(n_c) * 2
            + [dma(pairs), dma(pairs)],
            {3: 3},
        )(out_part.astype(BF).reshape(rows_bf.shape), own_tokens, own_cot, ff_w)
        act_two = act_two.reshape(pack_len, width)
        cot_rows = cot_rows.reshape(pack_len, width)

        act_two_part, branch_part, ff_grads = 0.0, 0.0, []
        for y in range(2):
            up = dot(act_two, ff_w[y, 0], ((1,), (0,)))
            gate = dot(act_two, ff_w[y, 1], ((1,), (0,)))
            sigma = jax.nn.sigmoid(gate)
            hidden_low = (gate * sigma * up).astype(BF)
            hidden_grad = dot(cot_rows, ff_w[y, 2], ((1,), (0,)))
            up_grad = (hidden_grad * gate * sigma).astype(BF)
            gate_grad = (hidden_grad * up * sigma * (1.0 + gate * (1.0 - sigma))).astype(BF)
            act_two_part += dot(up_grad, ff_w[y, 0], ((1,), (1,)))
            act_two_part += dot(gate_grad, ff_w[y, 1], ((1,), (1,)))
            branch_part += dot(hidden_low, ff_w[y, 2], ((1,), (1,)))
            ff_grads.append(
                jnp.stack(
                    [
                        dot(act_two, up_grad, ((0,), (0,))).astype(BF),
                        dot(act_two, gate_grad, ((0,), (0,))).astype(BF),
                        dot(cot_rows, hidden_low, ((0,), (0,))).astype(BF),
                    ]
                )
            )
        ff_grad = jnp.stack(ff_grads)
        height = width // n_f
        mid_rows, block_own, mid_grad, ff_got = call(
            third_kernel,
            "third",
            2,
            (rows_bf, own_bf, own_f32, jax.ShapeDtypeStruct((pairs, 3, height, ff_cols), BF)),
            [ANY, ANY, VMEM, VMEM, ANY],
            (ANY, VMEM, VMEM, ANY),
            scatter_scratch(n_c, half, width) * 2
            + [pltpu.VMEM((half, width), BF)]
            + gather_sems(n_c)
            + [dma(pairs), dma(pairs)],
        )(
            act_two_part.astype(BF).reshape(rows_bf.shape),
            branch_part.astype(BF).reshape(rows_bf.shape),
            resid_mid,
            own_cot,
            ff_grad,
        )
        mid_rows = mid_rows.reshape(pack_len, width)
        ff_mine = lax.dynamic_slice(
            ff_grad, (pack_at, 0, f_at * height, 0), (1, 3, height, ff_cols)
        )[0]
        ff_sum = ff_mine.astype(F32) + sum(ff_got[i].astype(F32) for i in range(pairs))

        attended_grad = heads_of(mid_rows, 3).astype(BF)
        value_grad = jnp.einsum(
            "htk,htd->hkd", probs_low, attended_grad, preferred_element_type=F32
        )
        prob_grad = jnp.einsum("htd,hkd->htk", attended_grad, value, preferred_element_type=F32)
        delta_rows = jnp.sum(probs * prob_grad, axis=2, keepdims=True)
        score_grad = (probs * (prob_grad - delta_rows)).astype(BF)
        query_grad = (
            jnp.einsum("htk,hkd->htd", score_grad, key, preferred_element_type=F32) * score_scale
        )
        key_grad = (
            jnp.einsum("htk,htd->hkd", score_grad, query, preferred_element_type=F32)
            * score_scale
        )
        joint_grad = [
            part.astype(BF) for part in (turn(query_grad, -1.0), turn(key_grad, -1.0), value_grad)
        ]
        act_one_part = sum(
            dot(joint_grad[i][y], att_w[y, i], ((1,), (1,))) for i in range(3) for y in range(2)
        )
        att_grad = jnp.stack(
            [
                jnp.stack(
                    [dot(act_one, part[y], ((0,), (0,))).astype(BF) for part in joint_grad]
                    + [dot(mid_rows, attended[y], ((0,), (0,))).astype(BF)]
                )
                for y in range(2)
            ]
        )
        input_grad, block_out, att_total, ff_total = call(
            fourth_kernel,
            "fourth",
            3,
            (
                jax.ShapeDtypeStruct((n_t, half, width), F32),
                jax.ShapeDtypeStruct((n_t, half, width), BF),
                jax.ShapeDtypeStruct(att_low.shape, BF),
                jax.ShapeDtypeStruct(ff_low.shape, BF),
            ),
            [ANY, VMEM, VMEM, ANY, ANY, ANY],
            (ANY,) * 4,
            scatter_scratch(n_c, half, width)
            + [
                pltpu.VMEM((4, height, att_cols), BF),
                pltpu.VMEM((pairs, 4, height, att_cols), BF),
                pltpu.VMEM((4, height, att_cols), BF),
                pltpu.VMEM((half, width), F32),
            ]
            + [dma(n_c), dma(n_c), pltpu.SemaphoreType.DMA] * 2
            + [dma(pairs), dma(pairs)]
            + [
                pltpu.SemaphoreType.DMA((2, n_t - 1)),
                pltpu.SemaphoreType.DMA((2, n_t - 1)),
                dma(3),
            ],
        )(
            act_one_part.astype(BF).reshape(rows_bf.shape),
            own_tokens,
            mid_grad,
            block_own,
            att_grad,
            ff_sum.astype(BF),
        )
        att_total, ff_total = att_total.astype(F32), ff_total.astype(F32)

        square = jnp.sum(att_total * att_total) + jnp.sum(ff_total * ff_total)
        count = n_f * n_c * n_t
        square_sum = call(
            norm_kernel,
            "norm",
            4,
            jax.ShapeDtypeStruct((8, 128), F32),
            [VMEM],
            VMEM,
            [pltpu.VMEM((count, 8, 128), F32), dma(count), dma(count)],
            vmem=8,
        )(jnp.broadcast_to(square, (8, 128)))[0, 0]
        norm_value = jnp.sqrt(square_sum)
        clip_factor = jnp.minimum(1.0, MAX_NORM / (norm_value + 1e-06))
        base_rate = width ** (-0.5)
        out_rate = (width // 32) ** (-0.5)
        grads = (att_total[:3], att_total[3], ff_total[:2], ff_total[2])
        weights = (att_proj, attn_out, ff_proj, ff_out)
        firsts_old = (att_proj_first, attn_out_first, ff_proj_first, ff_out_first)
        seconds_old = (att_proj_second, attn_out_second, ff_proj_second, ff_out_second)
        rates = (base_rate, out_rate, base_rate, base_rate)
        news = [
            adam_step(w, g, m, v, clip_factor, r)
            for w, g, m, v, r in zip(weights, grads, firsts_old, seconds_old, rates)
        ]
        return (
            block_out.reshape(tokens.shape),
            input_grad.reshape(tokens.shape),
            norm_value.reshape(1),
            *grads,
            *(n[0] for n in news),
            *(n[1] for n in news),
            *(n[2] for n in news),
            *(n[2].astype(BF) for n in news),
        )

    return shards


def solution(mesh):
    act = P("fsdp", "ctx", None)
    table = P("fsdp", None)
    cube = P(None, ("fsdp", "ctx"), "tp")
    flat = P(("fsdp", "ctx"), "tp")
    group = (cube, flat, cube, flat)
    in_specs = (act, act, table, table) + group * 3
    out_specs = (act, act, P()) + group * 5
    return jax.shard_map(
        make_shards(mesh), mesh=mesh, in_specs=in_specs, out_specs=out_specs, check_vma=False
    )
```

time: 1250 us -> 854 us (0.68)
  waiting for transfers between devices: 598 us -> 0 us
  Pallas kernels: 0 us -> 581 us
  starting transfers between devices: 175 us -> 0 us
  local copies, waits for them, and re-layouts: 154 us -> 18.8 us
  other arithmetic: 139 us -> 70.4 us
  matrix products: 114 us -> 169 us
  blocking collectives: 40.1 us -> 0 us
  between operations: 19.1 us -> 5.23 us
    ppermute x44 -> x0, waiting for transfers between devices: 592 us -> none  [the longest x24 370 us: by_ctx(): lax.ppermute(block, 'ctx', [(i, (i + shift) % n_c) for i in range(n_c)])]
    pallas_call x0 -> x5, Pallas kernels: none -> 581 us  [the longest x1 155 us: shards(): call(second_kernel, 'second', 1, (rows_bf, rows_bf, own_f32, jax.ShapeDty...]
    ppermute x44 -> x0, starting transfers between devices: 141 us -> none  [the longest x24 125 us: by_ctx(): lax.ppermute(block, 'ctx', [(i, (i + shift) % n_c) for i in range(n_c)])]
    dot_general x21 -> x42, matrix products: 95.9 us -> 149 us  [dot(): lax.dot_general(left, right, (dims, ((), ())), preferred_element_type=F32)]
    psum x1 -> x0, blocking collectives: 40.1 us -> none  [shards(): lax.psum(jnp.sum(att_total * att_total) + jnp.sum(ff_total * ff_total), (...]
    dot_general x6 -> x0, local copies, waits for them, and re-layouts: 35.6 us -> none  [dot(): lax.dot_general(left, right, (dims, ((), ())), preferred_element_type=F32)]
    all_to_all x4 -> x0, starting transfers between devices: 34.7 us -> none  [the longest x2 25.3 us: scatter_grad(): return lax.all_to_all(total.astype(BF), 'ctx', 1, 2, tiled=True).astype(F32)]
    concatenate x6 -> x2, other arithmetic: 23.9 us -> 0.37 us  [the longest x1 0.27 us: shards(): ff_low = jnp.concatenate([ff_proj, ff_out[None]]).astype(BF)]
  transfers between devices with their start and end apart: 50 -> 0, of which waited for: 22 -> 0; matrix products, arithmetic and copies ran while one was open for 22% -> 0% of each run, Pallas kernels for 0% -> 0%
where the time goes in v2:
time: 854 us; the launch traced here: 845 us
  Pallas kernels  581 us (68%)
  matrix products  169 us (20%)
  other arithmetic  70.4 us (8%)
  local copies, waits for them, and re-layouts  18.8 us (2%)
    pallas_call x1, Pallas kernels, shards(): call(second_kernel, 'second', 1, (rows_bf, rows_bf, own_f32, jax.ShapeDty...  155 us
    dot_general x42, matrix products, dot(): lax.dot_general(left, right, (dims, ((), ())), preferred_element_type=F32)  149 us
    pallas_call x1, Pallas kernels, shards(): call(third_kernel, 'third', 2, (rows_bf, own_bf, own_f32, jax.ShapeDtypeS...  145 us
    pallas_call x1, Pallas kernels, shards(): call(fourth_kernel, 'fourth', 3, (jax.ShapeDtypeStruct((n_t, half, width)...  130 us
    pallas_call x1, Pallas kernels, shards(): call(first_kernel, 'first', 0, (rows_bf, jax.ShapeDtypeStruct((2, 4, widt...  127 us
    pallas_call x1, Pallas kernels, shards(): call(norm_kernel, 'norm', 4, jax.ShapeDtypeStruct((8, 128), F32), [VMEM],...  25 us
    convert_element_type x4, other arithmetic, shards(): n[2].astype(BF)  24.8 us

profile of v2, /device:TPU:0, one launch (start us, length us, event | category | flops | bytes accessed | tf_op | source)
XLA Modules:
  0.0 845.0 jit_solution(10714271654973774270)
XLA Ops:
  12.7 126.7 %first.1 = (bf16[8,128,2048]{2,1,0:T(8,128)(2,1)S(1)}, bf16[2,4,2048,128]{3,2,1,0:T(8,128)(2,1)S(1)}, bf16[2,3,2048,512]{3,2,1,0:T(8,128)(2,1)}) custom-call(bf16[128,2048]{1,0:T(8,128)(2,1)S(1)} %fusion.75.a1_ref, bf16[4,256,512]{2,1,0:T(8,128)(2,1)S(1)} %pad_maximum_fusion.3.att_ref, bf16[3,256,2048]{2,1,0:T(8,128)(2,1)S(1)} %pad_maximum_fusion.2.ff_ref), custom_call_target="tpu_custom_call" | custom-call | tf_op jit(solution)/shard_map/first/pallas_call | solution.py:538
  150.4 7.5 fusion.162
  158.0 5.1 fusion.62
  169.7 154.8 %second.1 = (bf16[8,128,2048]{2,1,0:T(8,128)(2,1)S(1)}, bf16[8,128,2048]{2,1,0:T(8,128)(2,1)S(1)}, f32[128,2048]{1,0:T(8,128)S(1)}, bf16[2,3,2048,512]{3,2,1,0:T(8,128)(2,1)}) custom-call(bf16[8,128,2048]{2,1,0:T(8,128)(2,1)} %bitcast.271, bf16[128,2048]{1,0:T(8,128)(2,1)S(1)} %get-tuple-element.74.x_ref, ...), custom_call_target="tpu_custom_call", output_to_operand_aliasing={{3}: (3, {})} | custom-call | tf_op jit(solution)/shard_map/second/pallas_call | solution.py:594
  342.4 11.2 %fusion.11 = bf16[1,2048,512]{2,1,0:T(8,128)(2,1)S(1)} fusion(bf16[1024,2048]{1,0:T(8,128)(2,1)S(1)} %bitcast.258, bf16[1024,512]{1,0:T(8,128)(2,1)S(1)} %get-tuple-element.77), kind=kOutput, calls=%fused_computation.40 | convolution fusion | flops 2148532224 | bytes 7340032 | tf_op jit(solution)/shard_map/dot_general | solution.py:43
  357.2 4.8 multiply_convert_fusion.2
  369.5 5.0 maximum_bitcast_fusion
  374.5 5.7 fusion.35
  380.1 5.6 fusion.37
  392.6 5.6 fusion.25
  398.2 11.2 %add_convert_fusion.2 = bf16[1024,2048]{1,0:T(8,128)(2,1)S(1)} fusion(f32[1024,2048]{1,0:T(8,128)} %fusion.25, f32[1024,2048]{1,0:T(8,128)} %fusion.35, f32[1024,2048]{1,0:T(8,128)} %fusion.37, bf16[1024,512]{1,0:T(8,128)(2,1)S(1)} %get-tuple-element.76, bf16[2,3,2048,512]{3,2,1,0:T(8,128)(2,1)} %get-tuple-element.42), kind=kOutput, calls=%fused_computation.8 | convolution fusion | flops 2155872256 | bytes 32505856 | tf_op jit(solution)/shard_map/dot_general | solution.py:43
  409.4 10.5 %pad_maximum_fusion.grad_ref = bf16[2,3,2048,512]{3,2,1,0:T(8,128)(2,1)} fusion(bf16[1,3,2048,512]{3,2,1,0:T(8,128)(2,1)} %get-tuple-element.101, bf16[1,3,2048,512]{3,2,1,0:T(8,128)(2,1)} %get-tuple-element.100), kind=kLoop, calls=%fused_computation.2 | loop fusion | flops 6291456 | bytes 25165824 | tf_op jit(solution)/shard_map/stack | solution.py:631
  419.9 144.7 %third.1 = (bf16[8,128,2048]{2,1,0:T(8,128)(2,1)S(1)}, bf16[128,2048]{1,0:T(8,128)(2,1)S(1)}, f32[128,2048]{1,0:T(8,128)S(1)}, bf16[3,3,1024,512]{3,2,1,0:T(8,128)(2,1)}) custom-call(bf16[8,128,2048]{2,1,0:T(8,128)(2,1)S(1)} %bitcast.253, bf16[8,128,2048]{2,1,0:T(8,128)(2,1)} %bitcast.278, f32[128,2048]{1,0:T(8,128)S(1)} %get-tuple-element.44.mid_ref, ...), custom_call_target="tpu_custom_call" | custom-call | tf_op jit(solution)/shard_map/third/pallas_call | solution.py:633
  564.6 7.6 fusion.6.ff_ref
  587.2 4.8 multiply_convert_fusion
  607.9 4.5 fusion.100
  612.5 4.6 fusion.91
  617.0 4.8 fusion.94
  621.9 4.5 fusion.88
  626.4 16.5 %add_convert_fusion = bf16[1024,2048]{1,0:T(8,128)(2,1)} fusion(f32[1024,2048]{1,0:T(8,128)} %fusion.88, f32[1024,2048]{1,0:T(8,128)} %fusion.91, f32[1024,2048]{1,0:T(8,128)} %fusion.94, f32[1024,2048]{1,0:T(8,128)} %fusion.100, f32[1024,2048]{1,0:T(8,128)} %fusion.97, bf16[2,4,2048,128]{3,2,1,0:T(8,128)(2,1)} %copy-done.9, ...), kind=kOutput, calls=%fused_computation.4 | convolution fusion | flops 549453824 | bytes 46923776 | tf_op jit(solution)/shard_map/dot_general | solution.py:43
  648.1 130.1 %fourth.1 = (f32[4,128,2048]{2,1,0:T(8,128)}, bf16[4,128,2048]{2,1,0:T(8,128)(2,1)S(1)}, bf16[4,256,512]{2,1,0:T(8,128)(2,1)S(1)}, bf16[3,256,2048]{2,1,0:T(8,128)(2,1)S(1)}) custom-call(bf16[8,128,2048]{2,1,0:T(8,128)(2,1)} %bitcast.272, bf16[128,2048]{1,0:T(8,128)(2,1)S(1)} %copy-done.5, f32[128,2048]{1,0:T(8,128)S(1)} %copy-done.14, ...), custom_call_target="tpu_custom_call" | custom-call | tf_op jit(solution)/shard_map/fourth/pallas_call | solution.py:686
  784.2 25.0 %norm.1 = f32[8,128]{1,0:T(8,128)S(1)} custom-call(f32[8,128]{1,0:T(8,128)S(1)} %broadcast_in_dim.52.value_ref), custom_call_target="tpu_custom_call" | custom-call | tf_op jit(solution)/shard_map/norm/pallas_call | solution.py:724
  820.2 7.1 fusion.154
  827.4 11.2 %fusion.156 = (bf16[2,256,2048]{2,1,0:T(8,128)(2,1)}, f32[2,256,2048]{2,1,0:T(8,128)}, f32[2,256,2048]{2,1,0:T(8,128)}, f32[2,256,2048]{2,1,0:T(8,128)}, f32[2,256,2048]{2,1,0:T(8,128)}) fusion(f32[2,256,2048]{2,1,0:T(8,128)S(1)} %copy-done.19, f32[]{:T(128)} %bitcast.72, f32[2,256,2048]{2,1,0:T(8,128)S(1)} %copy-done.24, f32[2,256,2048]{2,1,0:T(8,128)} %param.26, ...), kind=kLoop, calls=%fused_computation.255 | loop fusion | flops 17825792 | bytes 35651588 | tf_op jit(solution)/shard_map/convert_element_type | solution.py:755
  (189 shorter events, 120.8 us)
Async XLA Ops:
  2.3 7.2 copy-start.22
  7.0 162.7 %copy-start.4 = (bf16[128,2048]{1,0:T(8,128)(2,1)}, bf16[128,2048]{1,0:T(8,128)(2,1)S(1)}, u32[]{:S(2)}) copy-start(bf16[128,2048]{1,0:T(8,128)(2,1)S(1)} %get-tuple-element.74.x_ref) | copy-start | bytes 1572868
  9.5 140.5 %copy-start.26 = (f32[1024,64]{0,1:T(8,128)}, f32[1024,64]{0,1:T(8,128)S(1)}, u32[]{:S(2)}) copy-start(f32[1024,64]{0,1:T(8,128)S(1)} %get-tuple-element.95) | copy-start | bytes 786436
  139.4 9.0 %copy-start.2 = (bf16[8,128,2048]{2,1,0:T(8,128)(2,1)}, bf16[8,128,2048]{2,1,0:T(8,128)(2,1)S(1)}, u32[]{:S(2)}) copy-start(bf16[8,128,2048]{2,1,0:T(8,128)(2,1)S(1)} %get-tuple-element.38) | copy-start | bytes 12582916
  139.4 9.0 %copy-start.9 = (bf16[2,4,2048,128]{3,2,1,0:T(8,128)(2,1)}, bf16[2,4,2048,128]{3,2,1,0:T(8,128)(2,1)S(1)}, u32[]{:S(2)}) copy-start(bf16[2,4,2048,128]{3,2,1,0:T(8,128)(2,1)S(1)} %get-tuple-element.39) | copy-start | bytes 12582916
  150.3 7.6 copy-start.30
  150.4 7.5 copy-start.32
  150.4 7.5 copy-start.36
  150.4 7.5 copy-start.38
  150.4 7.5 copy-start.50
  150.4 7.5 copy-start.52
  374.5 5.7 copy-start.47
  419.9 154.8 %slice-start = ((s8[8388608]{0:T(1024)(128)(4,1)}), s8[4194304]{0:T(1024)(128)(4,1)S(1)}, s32[]{:S(2)}) async-start(s8[8388608]{0:T(1024)(128)(4,1)} %bitcast.273), calls=%async_computation | async-start | bytes 8388608
  564.6 7.6 copy-start.13
  564.6 7.6 copy-start.15
  564.6 7.6 copy-start.10
  564.6 10.1 %slice-start.1 = ((s8[8388608]{0:T(1024)(128)(4,1)}), s8[4194304]{0:T(1024)(128)(4,1)S(1)}, s32[]{:S(2)}) async-start(s8[8388608]{0:T(1024)(128)(4,1)} %bitcast.273), calls=%async_computation.1 | async-start | bytes 8388608
  784.2 30.8 %copy-start.7 = (bf16[4,256,512]{2,1,0:T(8,128)(2,1)S(1)}, bf16[4,256,512]{2,1,0:T(8,128)(2,1)}, u32[]{:S(2)}) copy-start(bf16[4,256,512]{2,1,0:T(8,128)(2,1)} %copy-done.6) | copy-start | bytes 3145732
  784.2 30.8 %copy-start.23 = (f32[3,256,512]{2,1,0:T(8,128)S(1)}, f32[3,256,512]{2,1,0:T(8,128)}, u32[]{:S(2)}) copy-start(f32[3,256,512]{2,1,0:T(8,128)} %param.20) | copy-start | bytes 4718596
  784.2 30.8 %copy-start.28 = (f32[3,256,512]{2,1,0:T(8,128)S(1)}, f32[3,256,512]{2,1,0:T(8,128)}, u32[]{:S(2)}) copy-start(f32[3,256,512]{2,1,0:T(8,128)} %param.28) | copy-start | bytes 4718596
  784.2 30.8 %copy-start.29 = (f32[3,256,512]{2,1,0:T(8,128)S(1)}, f32[3,256,512]{2,1,0:T(8,128)}, u32[]{:S(2)}) copy-start(f32[3,256,512]{2,1,0:T(8,128)} %param.24) | copy-start | bytes 4718596
  820.2 7.1 copy-start.19
  820.2 7.1 copy-start.24
  827.3 11.2 %copy-start.12 = (bf16[4,128,2048]{2,1,0:T(8,128)(2,1)S(1)}, bf16[4,128,2048]{2,1,0:T(8,128)(2,1)}, u32[]{:S(2)}) copy-start(bf16[4,128,2048]{2,1,0:T(8,128)(2,1)} %copy-done.11) | copy-start | bytes 6291460
  (34 other events, 101.5 us)

commit v3 on v2

v3 whole, which is shorter than its diff:
```python
import functools

import jax
import jax.numpy as jnp
from jax import lax
from jax.experimental import pallas as pl
from jax.experimental.pallas import tpu as pltpu
from jax.sharding import PartitionSpec as P

HEAD_DIM = 128
STEP = 10
EPS_NORM = 1e-05
BETA_ONE = 0.9
BETA_TWO = 0.95
EPS_ADAM = 1e-08
DECAY = 0.1
MAX_NORM = 1.0
NEG_FILL = -1e30
BF = jnp.bfloat16
F32 = jnp.float32
MESH = pl.DeviceIdType.MESH
ANY = pl.BlockSpec(memory_space=pl.ANY)
VMEM = pl.BlockSpec(memory_space=pltpu.VMEM)
ROWS = 16
QUERIES = 256
SCORE_SCALE = HEAD_DIM ** (-0.5)


def mean_spread(values):
    centre = values - jnp.mean(values, axis=-1, keepdims=True)
    spread = jnp.mean(centre * centre, axis=-1, keepdims=True)
    scale = lax.rsqrt(spread + EPS_NORM)
    return centre * scale, scale


def norm_back(grad, normed, scale):
    return scale * (
        grad
        - jnp.mean(grad, axis=-1, keepdims=True)
        - normed * jnp.mean(grad * normed, axis=-1, keepdims=True)
    )


def dot(left, right, dims):
    return lax.dot_general(left, right, (dims, ((), ())), preferred_element_type=F32)


def adam_step(weight, grad_sum, first, second, clip_factor, learn_rate):
    clipped = grad_sum * clip_factor
    first_new = BETA_ONE * first + (1.0 - BETA_ONE) * clipped
    second_new = BETA_TWO * second + (1.0 - BETA_TWO) * clipped * clipped
    first_hat = first_new / (1.0 - BETA_ONE**STEP)
    second_hat = second_new / (1.0 - BETA_TWO**STEP)
    weight_new = weight - learn_rate * (
        first_hat / (jnp.sqrt(second_hat) + EPS_ADAM) + DECAY * weight
    )
    return (first_new, second_new, weight_new)


class Place:
    def __init__(self, sizes):
        self.n_f, self.n_c, self.n_t = sizes
        self.f, self.c, self.t = (lax.axis_index(a) for a in ("fsdp", "ctx", "tp"))
        self.hi, self.lo = self.t // 2, lax.rem(self.t, 2)
        self.core = (self.f, self.c, self.t + 1 - 2 * self.lo)
        self.block = self.c * 2 + self.lo
        self.pairs = [(s, o) for o in range(2) for s in range(self.n_f) if s or o]

    def ctx(self, shift):
        return lax.rem(self.c + shift + self.n_c, self.n_c)

    def fsdp(self, shift):
        return lax.rem(self.f + shift + self.n_f, self.n_f)

    def other(self, o):
        return self.hi + o * (1 - 2 * self.hi)

    def z(self, shift):
        return (self.f, self.ctx(shift), self.t)

    def xy(self, shift, o):
        return (self.fsdp(shift), self.c, self.t + o * (2 - 4 * self.hi))

    def greet(self, peers):
        barrier = pltpu.get_barrier_semaphore()
        for peer in peers:
            pl.semaphore_signal(barrier, inc=1, device_id=peer, device_id_type=MESH)
        pl.semaphore_wait(barrier, len(peers))

    def all_z(self):
        return [self.z(s) for s in range(1, self.n_c)]

    def all_xy(self):
        return [self.xy(s, o) for s, o in self.pairs]


def remote(src, dst, send, recv, peer):
    return pltpu.make_async_remote_copy(
        src_ref=src, dst_ref=dst, send_sem=send, recv_sem=recv, device_id=peer, device_id_type=MESH
    )


def by_rows(count, step):
    @pl.loop(0, count // ROWS)
    def _(i):
        step(pl.ds(pl.multiple_of(i * ROWS, ROWS), ROWS))


class Gather:
    def __init__(self, at, src, out, send, recv, local):
        self.at, self.src, self.out, self.send, self.recv = at, src, out, send, recv
        self.local = pltpu.make_async_copy(src, out.at[at.block], local)

    def far(self, way, hop, src=None):
        at = self.at
        block = self.out.at[jnp.clip(at.c - way * (hop - 1), 0, at.n_c - 1) * 2 + at.lo]
        k = hop + (0 if way > 0 else at.n_c)
        return remote(
            block if src is None else src, block, self.send.at[k], self.recv.at[k], at.z(way)
        )

    def near(self, distance, src=None):
        at = self.at
        block = self.out.at[jnp.clip(at.c - distance, 0, at.n_c - 1) * 2 + at.lo]
        k = 2 * at.n_c + distance + at.n_c
        return remote(
            block if src is None else src, block, self.send.at[k], self.recv.at[k], at.core
        )

    def there(self, way, hop):
        return self.at.c + hop < self.at.n_c if way > 0 else self.at.c >= hop

    def start(self):
        for way in (1, -1):

            @pl.when(self.there(way, 1))
            def _(way=way):
                self.far(way, 1, self.src).start()

        self.near(0, self.src).start()
        self.local.start()

    def forward(self, hops=None):
        at = self.at
        for hop in hops or range(1, at.n_c):
            for way in (1, -1):

                @pl.when(self.there(-way, hop))
                def _(way=way, hop=hop):
                    self.far(way, hop).wait_recv()
                    if hop < at.n_c - 1:

                        @pl.when(self.there(way, 1))
                        def _():
                            self.far(way, hop + 1).start()

                    self.near(way * hop).start()

    def finish(self):
        at = self.at
        for hop in range(1, at.n_c):
            for way in (1, -1):

                @pl.when(self.there(way, 1) & self.there(-way, hop - 1))
                def _(way=way, hop=hop):
                    self.far(way, hop).wait_send()

                @pl.when(self.there(-way, hop))
                def _(way=way, hop=hop):
                    self.near(way * hop).wait()

        self.near(0, self.src).wait()
        self.local.wait()


def gather_sems(n_c):
    return [
        pltpu.SemaphoreType.DMA((4 * n_c,)),
        pltpu.SemaphoreType.DMA((4 * n_c,)),
        pltpu.SemaphoreType.DMA,
    ]


class Scatter:
    def __init__(self, at, partial, own, near, sent, got, send, recv, local):
        self.at, self.partial, self.own, self.near = at, partial, own, near
        self.sent, self.got, self.send, self.recv, self.local = sent, got, send, recv, local

    def keep(self, c):
        return pltpu.make_async_copy(
            self.partial.at[c * 2 + self.at.lo], self.own.at[c], self.local.at[c]
        )

    def core(self, c):
        at = self.at
        return remote(
            self.partial.at[c * 2 + 1 - at.lo], self.near.at[c], self.send.at[c], self.recv.at[c], at.core
        )

    def far(self, way, hop):
        at = self.at
        c = jnp.clip(at.c + way * hop, 0, at.n_c - 1)
        slot = c if hop > 1 else c + (0 if way > 0 else at.n_c)
        k = at.n_c + hop + (0 if way > 0 else at.n_c)
        return remote(
            self.sent.at[c], self.got.at[slot], self.send.at[k], self.recv.at[k], at.z(way)
        )

    there = Gather.there

    def start(self):
        at = self.at
        for i in range(at.n_c):
            c = jnp.where(at.c * 2 < at.n_c, at.n_c - 1 - i, i)
            self.core(c).start()
            self.keep(c).start()

    def pass_on(self):
        at = self.at
        for hop in range(at.n_c - 1, 0, -1):
            for way in (1, -1):

                @pl.when(self.there(way, hop))
                def _(way=way, hop=hop):
                    c = at.c + way * hop
                    self.core(c).wait_recv()
                    self.keep(c).wait()
                    if hop < at.n_c - 1:
                        more = self.there(-way, 1)

                        @pl.when(more)
                        def _():
                            self.far(way, hop + 1).wait_recv()

                            def add(rows):
                                self.sent[c, rows] = (
                                    self.own[c, rows].astype(F32)
                                    + self.near[c, rows].astype(F32)
                                    + self.got[c, rows].astype(F32)
                                ).astype(BF)

                            by_rows(self.own.shape[1], add)

                        @pl.when(jnp.logical_not(more))
                        def _():
                            self.both(c)

                    else:
                        self.both(c)
                    self.far(way, hop).start()

        self.core(at.c).wait_recv()
        self.keep(at.c).wait()

    def both(self, c):
        def add(rows):
            self.sent[c, rows] = (
                self.own[c, rows].astype(F32) + self.near[c, rows].astype(F32)
            ).astype(BF)

        by_rows(self.own.shape[1], add)

    def arrive(self):
        at = self.at
        for way in (1, -1):

            @pl.when(self.there(-way, 1))
            def _(way=way):
                self.far(way, 1).wait_recv()

            @pl.when(jnp.logical_not(self.there(-way, 1)))
            def _(way=way):
                slot = at.c + (0 if way > 0 else at.n_c)
                self.got[slot] = jnp.zeros(self.got.shape[1:], BF)

    def total(self, rows):
        c = self.at.c
        return (
            self.own[c, rows].astype(F32)
            + self.near[c, rows].astype(F32)
            + self.got[c, rows].astype(F32)
            + self.got[c + self.at.n_c, rows].astype(F32)
        )

    def finish(self):
        at = self.at
        for c in range(at.n_c):
            self.core(c).wait_send()
        for hop in range(1, at.n_c):
            for way in (1, -1):

                @pl.when(self.there(way, hop))
                def _(way=way, hop=hop):
                    self.far(way, hop).wait_send()


def scatter_scratch(n_c, half, width):
    return [
        pltpu.VMEM((n_c, half, width), BF),
        pltpu.VMEM((n_c, half, width), BF),
        pltpu.VMEM((n_c, half, width), BF),
        pltpu.VMEM((2 * n_c, half, width), BF),
        pltpu.SemaphoreType.DMA((3 * n_c,)),
        pltpu.SemaphoreType.DMA((3 * n_c,)),
        pltpu.SemaphoreType.DMA((n_c,)),
    ]


class Swap:
    def __init__(self, at, shard, full, send, recv, local):
        self.at = at
        rows, width = shard.shape[1], full.shape[3]
        here = pl.ds((at.f * at.n_c + at.c) * rows, rows)
        target = full.at[at.hi, :, here, :]

        def columns(c):
            return shard.at[:, :, pl.ds(pl.multiple_of(c * width, 128), width)]

        self.local = pltpu.make_async_copy(columns(at.c), target, local)
        self.far = [
            remote(columns(at.ctx(s)), target, send.at[s], recv.at[s], at.z(s))
            for s in range(1, at.n_c)
        ]

    def start(self):
        self.local.start()
        for copy in self.far:
            copy.start()

    def wait(self):
        self.local.wait()
        for copy in self.far:
            copy.wait()


class Spread:
    def __init__(self, at, full, send, recv):
        self.at, self.full, self.send, self.recv = at, full, send, recv
        self.height = full.shape[2] // at.n_f // 2

    def part(self, o, shift, half):
        at = self.at
        first = (at.fsdp(shift) * 2 + half) * self.height
        return self.full.at[at.other(o), :, pl.ds(first, self.height), :]

    def copy(self, part, k, peer):
        return remote(part, part, self.send.at[k], self.recv.at[k], peer)

    def copies(self):
        at = self.at
        n = at.n_f
        return [
            *(
                self.copy(self.part(0, 0, h), h * n + s, at.xy(s, 0))
                for h in range(2)
                for s in range(1, n)
            ),
            *(self.copy(self.part(0, 0, h), 2 * n + h, at.xy(0, 1)) for h in (1, 0)),
        ]

    def passes(self):
        at = self.at
        n = at.n_f
        return [
            *(self.copy(self.part(0, -s, 0), 3 * n + s, at.xy(0, 1)) for s in range(1, n)),
            *(self.copy(self.part(1, 0, 1), 4 * n + s, at.xy(s, 0)) for s in range(1, n)),
        ]

    def start(self):
        for copy in self.copies():
            copy.start()

    def forward(self):
        copies, n = self.copies(), self.at.n_f
        for copy in copies[: n - 1]:
            copy.wait_recv()
        copies[2 * n - 2].wait_recv()
        for copy in self.passes():
            copy.start()

    def wait(self):
        copies, n = self.copies(), self.at.n_f
        for copy in copies[n - 1 : 2 * n - 2]:
            copy.wait_recv()
        copies[2 * n - 1].wait_recv()
        for copy in copies:
            copy.wait_send()
        for copy in self.passes():
            copy.wait()


class Collect:
    def __init__(self, at, partial, mine, by_x, by_y, pass_x, pass_y, part_x, part_y, send, recv, local):
        self.at, self.partial, self.mine, self.by_x, self.by_y = at, partial, mine, by_x, by_y
        self.pass_x, self.pass_y, self.part_x, self.part_y = pass_x, pass_y, part_x, part_y
        self.send, self.recv, self.local = send, recv, local
        self.height = partial.shape[2] // at.n_f // 2

    def part(self, o, shift, half):
        at = self.at
        first = (at.fsdp(shift) * 2 + half) * self.height
        return self.partial.at[at.other(o), :, pl.ds(first, self.height), :]

    def half(self, ref, half):
        return ref.at[:, pl.ds(half * self.height, self.height), :]

    def copy(self, src, dst, k, peer):
        return remote(src, dst, self.send.at[k], self.recv.at[k], peer)

    def raw(self):
        at = self.at
        n, shifts = at.n_f, range(1, at.n_f)
        return [
            [self.copy(self.part(1, s, 0), self.pass_x.at[s - 1], s, at.xy(s, 0)) for s in shifts],
            [self.copy(self.part(1, s, 1), self.pass_y.at[s - 1], n + s, at.xy(0, 1)) for s in shifts],
            [
                *(
                    self.copy(self.part(0, s, 0), self.half(self.by_x.at[s - 1], 0), 2 * n + s, at.xy(s, 0))
                    for s in shifts
                ),
                self.copy(self.part(1, 0, 1), self.half(self.by_y, 1), 0, at.xy(0, 1)),
            ],
        ]

    def added(self):
        at = self.at
        n, shifts = at.n_f, range(1, at.n_f)
        return [
            self.copy(self.part_y, self.half(self.by_y, 0), n, at.xy(0, 1)),
            *(
                self.copy(self.part_x.at[s - 1], self.half(self.by_x.at[s - 1], 1), 3 * n + s, at.xy(s, 0))
                for s in shifts
            ),
        ]

    def keeps(self):
        first = self.at.f * 2 * self.height
        own = self.partial.at[self.at.hi, :, pl.ds(first, 2 * self.height), :]
        return [
            pltpu.make_async_copy(own, self.mine, self.local.at[0]),
            pltpu.make_async_copy(self.part(1, 0, 0), self.part_y, self.local.at[1]),
            *(
                pltpu.make_async_copy(self.part(0, s, 1), self.part_x.at[s - 1], self.local.at[1 + s])
                for s in range(1, self.at.n_f)
            ),
        ]

    def start(self):
        for copies in self.raw():
            for copy in copies:
                copy.start()
        for copy in self.keeps():
            copy.start()

    def forward(self):
        raw, added, keeps = self.raw(), self.added(), self.keeps()
        for copy in (*raw[0], keeps[1]):
            copy.wait() if copy is keeps[1] else copy.wait_recv()
        n = self.at.n_f
        for m in range(self.mine.shape[0]):

            def add_y(rows, m=m):
                value = self.part_y[m, rows].astype(F32)
                for s in range(n - 1):
                    value = value + self.pass_x[s, m, rows].astype(F32)
                self.part_y[m, rows] = value.astype(BF)

            by_rows(self.height, add_y)
        added[0].start()
        for s in range(1, n):
            raw[1][s - 1].wait_recv()
            keeps[1 + s].wait()
            for m in range(self.mine.shape[0]):

                def add_x(rows, m=m, s=s):
                    self.part_x[s - 1, m, rows] = (
                        self.part_x[s - 1, m, rows].astype(F32) + self.pass_y[s - 1, m, rows].astype(F32)
                    ).astype(BF)

                by_rows(self.height, add_x)
            added[s].start()

    def total(self, out):
        raw, added = self.raw(), self.added()
        for copy in (*raw[2], *added):
            copy.wait_recv()
        self.keeps()[0].wait()
        for m in range(self.mine.shape[0]):

            def add(rows, m=m):
                value = self.mine[m, rows].astype(F32) + self.by_y[m, rows].astype(F32)
                for s in range(self.at.n_f - 1):
                    value = value + self.by_x[s, m, rows].astype(F32)
                out[m, rows] = value.astype(BF)

            by_rows(2 * self.height, add)

    def finish(self):
        for copies in (*self.raw(), self.added()):
            for copy in copies:
                copy.wait_send()


def collect_scratch(n_f, matrices, height, columns):
    half = (matrices, height // 2, columns)
    return [
        pltpu.VMEM((matrices, height, columns), BF),
        pltpu.VMEM((n_f - 1, matrices, height, columns), BF),
        pltpu.VMEM((matrices, height, columns), BF),
        pltpu.VMEM((n_f - 1, *half), BF),
        pltpu.VMEM((n_f - 1, *half), BF),
        pltpu.VMEM((n_f - 1, *half), BF),
        pltpu.VMEM(half, BF),
        dma(4 * n_f),
        dma(4 * n_f),
        dma(n_f + 1),
    ]


class Return:
    def __init__(self, at, summed, shard, send, recv, local):
        rows, width = shard.shape[1], summed.shape[2]
        target = shard.at[:, :, pl.ds(pl.multiple_of(at.c * width, 128), width)]

        def part(c):
            return summed.at[:, pl.ds(pl.multiple_of(c * rows, rows), rows), :]

        self.local = pltpu.make_async_copy(part(at.c), target, local)
        self.far = [
            remote(part(at.ctx(s)), target, send.at[s], recv.at[s], at.z(s))
            for s in range(1, at.n_c)
        ]

    start = Swap.start
    wait = Swap.wait


def pack_weights(w, packed):
    heads = w.shape[0]
    for i in range(4):
        for y in range(heads):
            k = (i * heads + y) * HEAD_DIM
            packed[:, k : k + HEAD_DIM] = w[y, i]


def turn(values, cos, sine):
    return values * cos + pltpu.roll(values, HEAD_DIM // 2, 1) * sine


def dma(count):
    return pltpu.SemaphoreType.DMA((count,))


def make_shards(mesh):
    sizes = tuple(mesh.shape[a] for a in ("fsdp", "ctx", "tp"))
    n_f, n_c, n_t = sizes

    def call(kernel, name, collective, outs, ins, out_specs, scratch, aliases=None, vmem=40):
        return pl.pallas_call(
            kernel,
            out_shape=outs,
            in_specs=ins,
            out_specs=out_specs,
            scratch_shapes=scratch,
            input_output_aliases=aliases or {},
            compiler_params=pltpu.CompilerParams(
                collective_id=collective, has_side_effects=True, vmem_limit_bytes=vmem << 20
            ),
            name=name,
        )

    def local(kernel, name, outs, scratch):
        return pl.pallas_call(
            kernel,
            out_shape=outs,
            scratch_shapes=scratch,
            compiler_params=pltpu.CompilerParams(vmem_limit_bytes=60 << 20),
            name=name,
        )

    def first_kernel(
        a1_ref, att_ref, ff_ref, rows_ref, attw_ref, ffw_ref, gs, gr, gl, s1, r1, l1, s2, r2, l2, s3, r3
    ):
        at = Place(sizes)
        at.greet([at.core, *at.all_z(), *at.all_xy()])
        gather = Gather(at, a1_ref, rows_ref, gs, gr, gl)
        swap_att = Swap(at, att_ref, attw_ref, s1, r1, l1)
        swap_ff = Swap(at, ff_ref, ffw_ref, s2, r2, l2)
        spread = Spread(at, attw_ref, s3, r3)
        swap_att.start()
        gather.start()
        swap_ff.start()
        swap_att.wait()
        spread.start()
        gather.forward()
        spread.forward()
        gather.finish()
        spread.wait()
        swap_ff.wait()

    def second_kernel(
        part_ref, x_ref, cot_ref, ffw_in, a2_ref, cots_ref, mid_ref, ffw_ref,
        own, near, sent, got, ss, sr, sl, low, s1, r1, l1, s2, r2, l2, s3, r3,
    ):
        at = Place(sizes)
        at.greet([at.core, *at.all_z(), *at.all_xy()])
        scatter = Scatter(at, part_ref, own, near, sent, got, ss, sr, sl)
        spread = Spread(at, ffw_ref, s3, r3)
        cots = Gather(at, cot_ref, cots_ref, s1, r1, l1)
        scatter.start()
        spread.start()
        scatter.pass_on()
        cots.start()
        scatter.arrive()

        def norm(rows):
            mid = x_ref[rows].astype(F32) + scatter.total(rows)
            mid_ref[rows] = mid
            low[rows] = mean_spread(mid)[0].astype(BF)

        by_rows(x_ref.shape[0], norm)
        a2 = Gather(at, low, a2_ref, s2, r2, l2)
        a2.start()
        spread.forward()
        for hop in range(1, n_c):
            cots.forward(range(hop, hop + 1))
            a2.forward(range(hop, hop + 1))
        cots.finish()
        a2.finish()
        scatter.finish()
        spread.wait()

    def third_kernel(
        part_ref, branch_ref, mid_ref, cot_ref, grad_ref, rows_ref, block_ref, own_ref, sum_ref,
        own, near, sent, got, ss, sr, sl, own2, near2, sent2, got2, ss2, sr2, sl2, low, s1, r1, l1, *collected,
    ):
        at = Place(sizes)
        at.greet([at.core, *at.all_z(), *at.all_xy()])
        scatter = Scatter(at, part_ref, own, near, sent, got, ss, sr, sl)
        branch = Scatter(at, branch_ref, own2, near2, sent2, got2, ss2, sr2, sl2)
        collect = Collect(at, grad_ref, *collected)
        scatter.start()
        collect.start()
        scatter.pass_on()
        branch.start()
        scatter.arrive()

        def norm(rows):
            normed, scale = mean_spread(mid_ref[rows])
            grad = cot_ref[rows].astype(F32) + norm_back(scatter.total(rows), normed, scale)
            own_ref[rows] = grad
            low[rows] = grad.astype(BF)

        by_rows(mid_ref.shape[0], norm)
        gather = Gather(at, low, rows_ref, s1, r1, l1)
        gather.start()
        branch.pass_on()
        gather.forward(range(1, 2))
        collect.forward()
        gather.forward(range(2, n_c))
        branch.arrive()

        def add(rows):
            block_ref[rows] = (mid_ref[rows] + branch.total(rows)).astype(BF)

        by_rows(mid_ref.shape[0], add)
        gather.finish()
        scatter.finish()
        branch.finish()
        collect.total(sum_ref)
        collect.finish()

    def fourth_kernel(
        part_ref, x_ref, mid_ref, block_ref, att_ref, ff_ref, input_ref, out_ref, attg_ref, ffg_ref,
        own, near, sent, got, ss, sr, sl, total, low, s1, r1, l1, s2, r2, l2, s4, r4, l4, *collected,
    ):
        at = Place(sizes)
        tps = [(at.f, at.c, lax.rem(at.t + s, n_t)) for s in range(1, n_t)]
        at.greet([*tps, *at.all_z(), *[at.xy(s, o) for s, o in at.pairs if s]])
        scatter = Scatter(at, part_ref, own, near, sent, got, ss, sr, sl)
        collect = Collect(at, att_ref, *collected)
        give_ff = Return(at, ff_ref, ffg_ref, s2, r2, l2)
        scatter.start()
        collect.start()

        def tp_gather(src, dst, k):
            copies = [
                remote(src, dst.at[at.t], s4.at[k, i], r4.at[k, i], peer) for i, peer in enumerate(tps)
            ]
            keep = pltpu.make_async_copy(src, dst.at[at.t], l4.at[k])
            for copy in (*copies, keep):
                copy.start()
            return [*copies, keep]

        scatter.pass_on()
        give_ff.start()
        collect.forward()
        waits = tp_gather(block_ref, out_ref, 0)
        collect.total(total)
        give_att = Return(at, total, attg_ref, s1, r1, l1)
        give_att.start()
        scatter.arrive()

        def norm(rows):
            normed, scale = mean_spread(x_ref[rows].astype(F32))
            low[rows] = mid_ref[rows] + norm_back(scatter.total(rows), normed, scale)

        by_rows(mid_ref.shape[0], norm)
        waits += tp_gather(low, input_ref, 1)
        for copy in waits:
            copy.wait()
        scatter.finish()
        collect.finish()
        give_att.wait()
        give_ff.wait()

    def norm_kernel(value_ref, out_ref, total, got_t, got_c, got_f, send, recv):
        at = Place(sizes)
        tps = [(at.f, at.c, lax.rem(at.t + s, n_t)) for s in range(1, n_t)]
        fs = [at.xy(s, 0) for s in range(1, n_f)]
        at.greet([*tps, *at.all_z(), *fs])
        total[0] = value_ref[...]
        base = 0
        for stage, (peers, got) in enumerate(((tps, got_t), (at.all_z(), got_c), (fs, got_f))):
            copies = [
                remote(total.at[stage], got.at[i], send.at[base + i], recv.at[base + i], peer)
                for i, peer in enumerate(peers)
            ]
            base += len(peers)
            for copy in copies:
                copy.start()
            for copy in copies:
                copy.wait()
            value = total[stage]
            for i in range(len(peers)):
                value = value + got[i]
            total[stage + 1] = value
        out_ref[...] = total[3]

    def forward_kernel(
        a1, w, place, key_place, first, cos, sine, qkv, attended, mass, part, packed
    ):
        heads = w.shape[0]
        wide = heads * HEAD_DIM
        pack_weights(w, packed)
        for i in range(3):
            joint = dot(a1[...], packed[:, i * wide : (i + 1) * wide], ((1,), (0,)))
            for y in range(heads):
                cols = slice(y * HEAD_DIM, (y + 1) * HEAD_DIM)
                head = joint[:, cols]
                if i < 2:
                    head = turn(head, cos[...], sine[...])
                qkv[i, :, cols] = head.astype(BF)
        for y in range(heads):
            cols = slice(y * HEAD_DIM, (y + 1) * HEAD_DIM)

            @pl.loop(0, a1.shape[0] // QUERIES)
            def _(c, y=y, cols=cols):
                rows = pl.ds(pl.multiple_of(c * QUERIES, QUERIES), QUERIES)
                scores = dot(qkv[0, rows, cols], qkv[1, :, cols], ((1,), (1,))) * SCORE_SCALE
                allowed = (key_place[...] <= place[rows]) & (key_place[...] >= first[rows])
                scores = jnp.where(allowed, scores, NEG_FILL)
                peak = jnp.max(scores, axis=1, keepdims=True)
                exp_scores = jnp.exp(scores - peak)
                total = jnp.sum(exp_scores, axis=1, keepdims=True)
                probs = (exp_scores * (1.0 / total)).astype(BF)
                attended[rows, cols] = dot(probs, qkv[2, :, cols], ((1,), (0,))).astype(BF)
                mass[rows, y : y + 1] = peak + jnp.log(total)

        width = part.shape[1] // 4

        @pl.loop(0, 4)
        def _(c):
            cols = pl.ds(pl.multiple_of(c * width, width), width)
            part[:, cols] = dot(attended[...], packed[cols, 3 * wide :], ((1,), (1,))).astype(BF)

    def backward_kernel(
        mid, a1, w, place, key_place, first, cos, sine, qkv, attended, mass, part, grad, packed, joint, d_v, d_k
    ):
        heads = w.shape[0]
        wide = heads * HEAD_DIM
        pack_weights(w, packed)
        joint[:, :wide] = dot(mid[...], packed[:, 3 * wide :], ((1,), (0,))).astype(BF)
        for y in range(heads):
            cols = slice(y * HEAD_DIM, (y + 1) * HEAD_DIM)

            @pl.loop(0, a1.shape[0] // QUERIES)
            def _(c, y=y, cols=cols):
                rows = pl.ds(pl.multiple_of(c * QUERIES, QUERIES), QUERIES)
                query, key, value = qkv[0, rows, cols], qkv[1, :, cols], qkv[2, :, cols]
                d_att = joint[rows, cols]
                scores = dot(query, key, ((1,), (1,))) * SCORE_SCALE
                allowed = (key_place[...] <= place[rows]) & (key_place[...] >= first[rows])
                probs = jnp.exp(jnp.where(allowed, scores, NEG_FILL) - mass[rows, y : y + 1])
                d_prob = dot(d_att, value, ((1,), (1,)))
                delta = jnp.sum(probs * d_prob, axis=1, keepdims=True)
                d_score = (probs * (d_prob - delta)).astype(BF)
                v_part = dot(probs.astype(BF), d_att, ((0,), (0,)))
                k_part = dot(d_score, query, ((0,), (0,)))

                @pl.when(c == 0)
                def _():
                    d_v[...] = v_part
                    d_k[...] = k_part

                @pl.when(c > 0)
                def _():
                    d_v[...] += v_part
                    d_k[...] += k_part

                d_query = dot(d_score, key, ((1,), (0,))) * SCORE_SCALE
                joint[rows, cols] = turn(d_query, cos[rows], -sine[rows]).astype(BF)

            joint[:, wide + y * HEAD_DIM : wide + (y + 1) * HEAD_DIM] = turn(
                d_k[...] * SCORE_SCALE, cos[...], -sine[...]
            ).astype(BF)
            joint[:, 2 * wide + y * HEAD_DIM : 2 * wide + (y + 1) * HEAD_DIM] = d_v[...].astype(BF)
        width = part.shape[1] // 4

        @pl.loop(0, 4)
        def _(c):
            cols = pl.ds(pl.multiple_of(c * width, width), width)
            part[:, cols] = dot(joint[...], packed[cols, : 3 * wide], ((1,), (1,))).astype(BF)

        @pl.loop(0, 2)
        def _(c):
            cols = pl.ds(pl.multiple_of(c * 2 * width, width), 2 * width)
            for i in range(4):
                if i < 3:
                    value = dot(a1[:, cols], joint[:, i * wide : (i + 1) * wide], ((0,), (0,)))
                else:
                    value = dot(mid[:, cols], attended[...], ((0,), (0,)))
                for y in range(heads):
                    grad[y, i, cols] = value[:, y * HEAD_DIM : (y + 1) * HEAD_DIM].astype(BF)

    def hidden_kernel(a2, cot, w, d_a2, branch, grad, hidden, d_up, d_gate, kept):
        step, steps = pl.program_id(0), pl.num_programs(0)
        tile = w.shape[3]
        here = pl.ds(pl.multiple_of(step * tile, tile), tile)
        length, width = a2.shape
        chunk = length // 2

        @pl.loop(0, 2)
        def _(i):
            rows = pl.ds(pl.multiple_of(i * chunk, chunk), chunk)
            up = dot(a2[rows], w[0, 0], ((1,), (0,)))
            gate = dot(a2[rows], w[0, 1], ((1,), (0,)))
            d_hid = dot(cot[rows], w[0, 2], ((1,), (0,)))
            sigma = jax.nn.sigmoid(gate)
            act = gate * sigma
            hidden[rows, here] = (act * up).astype(BF)
            d_up[rows, here] = (d_hid * act).astype(BF)
            d_gate[rows, here] = (d_hid * up * sigma * (1.0 + gate * (1.0 - sigma))).astype(BF)

        for m in range(3):
            kept[m, :, here] = w[0, m]
        grad[0, 0] = dot(a2[...], d_up[:, here], ((0,), (0,))).astype(BF)
        grad[0, 1] = dot(a2[...], d_gate[:, here], ((0,), (0,))).astype(BF)
        grad[0, 2] = dot(cot[...], hidden[:, here], ((0,), (0,))).astype(BF)

        @pl.when(step == steps - 1)
        def _():
            @pl.loop(0, 8)
            def _(i):
                cols = pl.ds(pl.multiple_of(i * (width // 8), width // 8), width // 8)
                d_a2[:, cols] = (
                    dot(d_up[...], kept[0, cols], ((1,), (1,)))
                    + dot(d_gate[...], kept[1, cols], ((1,), (1,)))
                ).astype(BF)
                branch[:, cols] = dot(hidden[...], kept[2, cols], ((1,), (1,))).astype(BF)

    def shards(
        tokens,
        cotangent,
        lengths,
        deal,
        att_proj,
        attn_out,
        ff_proj,
        ff_out,
        att_proj_first,
        attn_out_first,
        ff_proj_first,
        ff_out_first,
        att_proj_second,
        attn_out_second,
        ff_proj_second,
        ff_out_second,
    ):
        t_at = lax.axis_index("tp")
        pack_at = t_at // 2
        packs, row_count, width = tokens.shape
        half = row_count // 2
        pack_len = deal.shape[1]
        blocks = n_c * 2
        rows_bf = jax.ShapeDtypeStruct((blocks, half, width), BF)
        own_f32 = jax.ShapeDtypeStruct((half, width), F32)
        own_bf = jax.ShapeDtypeStruct((half, width), BF)

        def own_rows(array):
            rows = array.reshape(packs * 2, half, width)
            return lax.dynamic_index_in_dim(rows, t_at, 0, keepdims=False)

        own_tokens = own_rows(tokens)
        own_cot = own_rows(cotangent)
        att_low = jnp.concatenate([att_proj, attn_out[None]]).astype(BF)
        ff_low = jnp.concatenate([ff_proj, ff_out[None]]).astype(BF)
        normed_one, _ = mean_spread(own_tokens.astype(F32))
        att_cols, ff_cols = att_low.shape[2] // n_c, ff_low.shape[2] // n_c
        act_one, att_w, ff_w = call(
            first_kernel,
            "first",
            0,
            (
                rows_bf,
                jax.ShapeDtypeStruct((2, 4, width, att_cols), BF),
                jax.ShapeDtypeStruct((2, 3, width, ff_cols), BF),
            ),
            [ANY] * 3,
            (ANY,) * 3,
            gather_sems(n_c)
            + [dma(n_c), dma(n_c), pltpu.SemaphoreType.DMA] * 2
            + [dma(5 * n_f), dma(5 * n_f)],
        )(normed_one.astype(BF), att_low, ff_low)
        act_one = act_one.reshape(pack_len, width)

        places = lax.dynamic_index_in_dim(deal, pack_at, 0, keepdims=False)
        length_row = lax.dynamic_index_in_dim(lengths, pack_at, 0, keepdims=False)
        seqs = lengths.shape[1]
        before = jnp.arange(seqs)[:, None] > jnp.arange(seqs)[None, :]
        starts = jnp.sum(jnp.where(before, length_row[None, :], 0), axis=1)
        inside = (places[:, None] >= starts[None, :]) & (
            places[:, None] < (starts + length_row)[None, :]
        )
        firsts = jnp.sum(jnp.where(inside, starts[None, :], 0), axis=1)
        freq_steps = jnp.arange(HEAD_DIM // 2, dtype=F32)
        inverse = jnp.power(10000.0, -2.0 * freq_steps / HEAD_DIM)
        angles = (places - firsts).astype(F32)[:, None] * inverse[None, :]
        cos_table, sine_table = jnp.cos(angles), jnp.sin(angles)
        tables = (
            places[:, None],
            places[None, :],
            firsts[:, None],
            jnp.concatenate([cos_table, cos_table], axis=1),
            jnp.concatenate([-sine_table, sine_table], axis=1),
        )
        rank_width = 2 * att_cols
        qkv, attended, mass, out_part = local(
            forward_kernel,
            "forward",
            (
                jax.ShapeDtypeStruct((3, pack_len, rank_width), BF),
                jax.ShapeDtypeStruct((pack_len, rank_width), BF),
                jax.ShapeDtypeStruct((pack_len, 2), F32),
                jax.ShapeDtypeStruct((pack_len, width), BF),
            ),
            [pltpu.VMEM((width, 4 * rank_width), BF)],
        )(act_one, att_w, *tables)
        act_two, cot_rows, resid_mid, ff_w = call(
            second_kernel,
            "second",
            1,
            (rows_bf, rows_bf, own_f32, jax.ShapeDtypeStruct(ff_w.shape, BF)),
            [ANY, VMEM, VMEM, ANY],
            (ANY, ANY, VMEM, ANY),
            scatter_scratch(n_c, half, width)
            + [pltpu.VMEM((half, width), BF)]
            + gather_sems(n_c) * 2
            + [dma(5 * n_f), dma(5 * n_f)],
            {3: 3},
        )(out_part.reshape(rows_bf.shape), own_tokens, own_cot, ff_w)
        act_two = act_two.reshape(pack_len, width)
        cot_rows = cot_rows.reshape(pack_len, width)

        tile = 256
        tiles = ff_cols // tile
        kept = pl.BlockSpec((pack_len, width), lambda i: (0, 0), pipeline_mode=pl.Buffered(1))
        moved = pl.BlockSpec((1, 3, width, tile), lambda i: (i // tiles, 0, 0, i % tiles))
        rows_flat = jax.ShapeDtypeStruct((pack_len, width), BF)
        act_two_part, branch_part, ff_grad = pl.pallas_call(
            hidden_kernel,
            grid=(2 * tiles,),
            out_shape=(rows_flat, rows_flat, jax.ShapeDtypeStruct(ff_w.shape, BF)),
            in_specs=[kept, kept, moved],
            out_specs=(kept, kept, moved),
            scratch_shapes=[pltpu.VMEM((pack_len, 2 * ff_cols), BF)] * 3
            + [pltpu.VMEM((3, width, 2 * ff_cols), BF)],
            compiler_params=pltpu.CompilerParams(vmem_limit_bytes=60 << 20),
            name="hidden",
        )(act_two, cot_rows, ff_w)
        height = width // n_f
        mid_rows, block_own, mid_grad, ff_sum = call(
            third_kernel,
            "third",
            2,
            (rows_bf, own_bf, own_f32, jax.ShapeDtypeStruct((3, height, ff_cols), BF)),
            [ANY, ANY, VMEM, VMEM, ANY],
            (ANY, VMEM, VMEM, VMEM),
            scatter_scratch(n_c, half, width) * 2
            + [pltpu.VMEM((half, width), BF)]
            + gather_sems(n_c)
            + collect_scratch(n_f, 3, height, ff_cols),
            vmem=56,
        )(
            act_two_part.reshape(rows_bf.shape),
            branch_part.reshape(rows_bf.shape),
            resid_mid,
            own_cot,
            ff_grad,
        )
        mid_rows = mid_rows.reshape(pack_len, width)

        act_one_part, att_grad = local(
            backward_kernel,
            "backward",
            (rows_flat, jax.ShapeDtypeStruct(att_w.shape, BF)),
            [
                pltpu.VMEM((width, 4 * rank_width), BF),
                pltpu.VMEM((pack_len, 3 * rank_width), BF),
                pltpu.VMEM((pack_len, HEAD_DIM), F32),
                pltpu.VMEM((pack_len, HEAD_DIM), F32),
            ],
        )(mid_rows, act_one, att_w, *tables, qkv, attended, mass)
        input_grad, block_out, att_total, ff_total = call(
            fourth_kernel,
            "fourth",
            3,
            (
                jax.ShapeDtypeStruct((n_t, half, width), F32),
                jax.ShapeDtypeStruct((n_t, half, width), BF),
                jax.ShapeDtypeStruct(att_low.shape, BF),
                jax.ShapeDtypeStruct(ff_low.shape, BF),
            ),
            [ANY, VMEM, VMEM, ANY, ANY, ANY],
            (ANY,) * 4,
            scatter_scratch(n_c, half, width)
            + [pltpu.VMEM((4, height, att_cols), BF), pltpu.VMEM((half, width), F32)]
            + [dma(n_c), dma(n_c), pltpu.SemaphoreType.DMA] * 2
            + [
                pltpu.SemaphoreType.DMA((2, n_t - 1)),
                pltpu.SemaphoreType.DMA((2, n_t - 1)),
                dma(2),
            ]
            + collect_scratch(n_f, 4, height, att_cols),
        )(
            act_one_part.reshape(rows_bf.shape),
            own_tokens,
            mid_grad,
            block_own,
            att_grad,
            ff_sum,
        )
        att_total, ff_total = att_total.astype(F32), ff_total.astype(F32)

        square = jnp.sum(att_total * att_total) + jnp.sum(ff_total * ff_total)
        count = n_f + n_c + n_t
        square_sum = call(
            norm_kernel,
            "norm",
            4,
            jax.ShapeDtypeStruct((8, 128), F32),
            [VMEM],
            VMEM,
            [pltpu.VMEM((k, 8, 128), F32) for k in (4, n_t - 1, n_c - 1, n_f - 1)]
            + [dma(count), dma(count)],
            vmem=8,
        )(jnp.broadcast_to(square, (8, 128)))[0, 0]
        norm_value = jnp.sqrt(square_sum)
        clip_factor = jnp.minimum(1.0, MAX_NORM / (norm_value + 1e-06))
        base_rate = width ** (-0.5)
        out_rate = (width // 32) ** (-0.5)
        grads = (att_total[:3], att_total[3], ff_total[:2], ff_total[2])
        weights = (att_proj, attn_out, ff_proj, ff_out)
        firsts_old = (att_proj_first, attn_out_first, ff_proj_first, ff_out_first)
        seconds_old = (att_proj_second, attn_out_second, ff_proj_second, ff_out_second)
        rates = (base_rate, out_rate, base_rate, base_rate)
        news = [
            adam_step(w, g, m, v, clip_factor, r)
            for w, g, m, v, r in zip(weights, grads, firsts_old, seconds_old, rates)
        ]
        return (
            block_out.reshape(tokens.shape),
            input_grad.reshape(tokens.shape),
            norm_value.reshape(1),
            *grads,
            *(n[0] for n in news),
            *(n[1] for n in news),
            *(n[2] for n in news),
            *(n[2].astype(BF) for n in news),
        )

    return shards


def solution(mesh):
    act = P("fsdp", "ctx", None)
    table = P("fsdp", None)
    cube = P(None, ("fsdp", "ctx"), "tp")
    flat = P(("fsdp", "ctx"), "tp")
    group = (cube, flat, cube, flat)
    in_specs = (act, act, table, table) + group * 3
    out_specs = (act, act, P()) + group * 5
    return jax.shard_map(
        make_shards(mesh), mesh=mesh, in_specs=in_specs, out_specs=out_specs, check_vma=False
    )
```

time: 854 us -> 710 us (0.83)
  matrix products: 169 us -> 0 us
  Pallas kernels: 581 us -> 631 us
  other arithmetic: 70.4 us -> 37.2 us
  local copies, waits for them, and re-layouts: 18.8 us -> 29.5 us
    dot_general x47 -> x0, matrix products: 162 us -> none  [the longest x42 149 us: dot(): lax.dot_general(left, right, (dims, ((), ())), preferred_element_type=F32)]
    pallas_call x0 -> x3, Pallas kernels: none -> 106 us  [the longest x1 55.3 us: shards(): pl.pallas_call(hidden_kernel, grid=(2 * tiles,), out_shape=(rows_flat, ro...]
    pallas_call x1, Pallas kernels: 155 us -> 114 us  [shards(): call(second_kernel, 'second', 1, (rows_bf, rows_bf, own_f32, jax.ShapeDty...]
    pallas_call x1, Pallas kernels: 145 us -> 122 us  [shards(): call(third_kernel, 'third', 2, (rows_bf, own_bf, own_f32, jax.ShapeDtypeS...]
    another operation x9 -> x2, other arithmetic: 19.5 us -> 0.41 us  [the longest x2 15.4 us: shards(): ff_grad = jnp.stack(ff_grads)]
    pallas_call x1, Pallas kernels: 127 us -> 143 us  [shards(): call(first_kernel, 'first', 0, (rows_bf, jax.ShapeDtypeStruct((2, 4, widt...]
    pallas_call x1, Pallas kernels: 25 us -> 13.7 us  [shards(): call(norm_kernel, 'norm', 4, jax.ShapeDtypeStruct((8, 128), F32), [VMEM],...]
    unnamed x118 -> x60, local copies, waits for them, and re-layouts: 16.8 us -> 24.8 us
where the time goes in v3:
time: 710 us; the launch traced here: 702 us
  Pallas kernels  631 us (89%)
  other arithmetic  37.2 us (5%)
  local copies, waits for them, and re-layouts  29.5 us (4%)
    pallas_call x1, Pallas kernels, shards(): call(first_kernel, 'first', 0, (rows_bf, jax.ShapeDtypeStruct((2, 4, widt...  143 us
    pallas_call x1, Pallas kernels, shards(): call(fourth_kernel, 'fourth', 3, (jax.ShapeDtypeStruct((n_t, half, width)...  131 us
    pallas_call x1, Pallas kernels, shards(): call(third_kernel, 'third', 2, (rows_bf, own_bf, own_f32, jax.ShapeDtypeS...  122 us
    pallas_call x1, Pallas kernels, shards(): call(second_kernel, 'second', 1, (rows_bf, rows_bf, own_f32, jax.ShapeDty...  114 us
    pallas_call x1, Pallas kernels, shards(): pl.pallas_call(hidden_kernel, grid=(2 * tiles,), out_shape=(rows_flat, ro...  55.3 us
    pallas_call x1, Pallas kernels, shards(): local(backward_kernel, 'backward', (rows_flat, jax.ShapeDtypeStruct(att_w...  31.8 us
    unnamed x60, local copies, waits for them, and re-layouts  24.8 us
    convert_element_type x4, other arithmetic, shards(): n[2].astype(BF)  23.2 us

profile of v3, /device:TPU:0, one launch (start us, length us, event | category | flops | bytes accessed | tf_op | source)
XLA Modules:
  0.0 701.9 jit_solution(12338245376529093536)
XLA Ops:
  0.7 1.6 copy-done
  8.5 1.4 convert_reduce_fusion
  12.3 1.9 fusion.8
  16.1 143.0 %first.1 = (bf16[8,128,2048]{2,1,0:T(8,128)(2,1)S(1)}, bf16[2,4,2048,128]{3,2,1,0:T(8,128)(2,1)S(1)}, bf16[2,3,2048,512]{3,2,1,0:T(8,128)(2,1)}) custom-call(bf16[128,2048]{1,0:T(8,128)(2,1)S(1)} %fusion.6.a1_ref, bf16[4,256,512]{2,1,0:T(8,128)(2,1)S(1)} %pad_maximum_fusion.1.att_ref, bf16[3,256,2048]{2,1,0:T(8,128)(2,1)S(1)} %pad_maximum_fusion.ff_ref), custom_call_target="tpu_custom_call" | custom-call | tf_op jit(solution)/shard_map/first/pallas_call | solution.py:910
  159.2 2.0 copy-done.2
  161.2 2.0 copy-done.3
  163.2 19.2 %forward.1 = (bf16[3,1024,256]{2,1,0:T(8,128)(2,1)}, bf16[1024,256]{1,0:T(8,128)(2,1)}, f32[1024,2]{1,0:T(8,128)}, bf16[1024,2048]{1,0:T(8,128)(2,1)}) custom-call(bf16[1024,2048]{1,0:T(8,128)(2,1)} %bitcast.42, bf16[2,4,2048,128]{3,2,1,0:T(8,128)(2,1)} %copy-done.3, s32[1024,1]{1,0:T(8,128)} %copy.44.place, s32[1,1024]{1,0:T(1,128)} %copy-done.28, ...), custom_call_target="tpu_custom_call" | custom-call | tf_op jit(solution)/shard_map/forward/pallas_call | solution.py:948
  182.4 114.2 %second.1 = (bf16[8,128,2048]{2,1,0:T(8,128)(2,1)S(1)}, bf16[8,128,2048]{2,1,0:T(8,128)(2,1)S(1)}, f32[128,2048]{1,0:T(8,128)S(1)}, bf16[2,3,2048,512]{3,2,1,0:T(8,128)(2,1)}) custom-call(bf16[8,128,2048]{2,1,0:T(8,128)(2,1)} %bitcast.48, bf16[128,2048]{1,0:T(8,128)(2,1)S(1)} %get-tuple-element.92.x_ref, ...), custom_call_target="tpu_custom_call", output_to_operand_aliasing={{3}: (3, {})} | custom-call | tf_op jit(solution)/shard_map/second/pallas_call | solution.py:959
  296.7 2.0 copy-done.7
  298.7 2.0 copy-done.8
  300.7 55.3 %hidden.1 = (bf16[1024,2048]{1,0:T(8,128)(2,1)}, bf16[1024,2048]{1,0:T(8,128)(2,1)}, bf16[2,3,2048,512]{3,2,1,0:T(8,128)(2,1)}) custom-call(bf16[1024,2048]{1,0:T(8,128)(2,1)} %bitcast.44, bf16[1024,2048]{1,0:T(8,128)(2,1)} %bitcast.45, bf16[2,3,2048,512]{3,2,1,0:T(8,128)(2,1)} %get-tuple-element.53.w), custom_call_target="tpu_custom_call" | custom-call | tf_op jit(solution)/shard_map/hidden/pallas_call | solution.py:980
  356.0 122.0 %third.1 = (bf16[8,128,2048]{2,1,0:T(8,128)(2,1)}, bf16[128,2048]{1,0:T(8,128)(2,1)}, f32[128,2048]{1,0:T(8,128)}, bf16[3,1024,512]{2,1,0:T(8,128)(2,1)}) custom-call(bf16[8,128,2048]{2,1,0:T(8,128)(2,1)} %bitcast.51, bf16[8,128,2048]{2,1,0:T(8,128)(2,1)} %bitcast.52, f32[128,2048]{1,0:T(8,128)} %copy-done.12, bf16[128,2048]{1,0:T(8,128)(2,1)} %copy-done.6, ...), custom_call_target="tpu_custom_call" | custom-call | tf_op jit(solution)/shard_map/third/pallas_call | solution.py:992
  478.0 31.8 %backward.1 = (bf16[1024,2048]{1,0:T(8,128)(2,1)}, bf16[2,4,2048,128]{3,2,1,0:T(8,128)(2,1)}) custom-call(bf16[1024,2048]{1,0:T(8,128)(2,1)} %bitcast.47, bf16[1024,2048]{1,0:T(8,128)(2,1)} %bitcast.43, bf16[2,4,2048,128]{3,2,1,0:T(8,128)(2,1)} %copy-done.3, s32[1024,1]{1,0:T(8,128)} %copy.44.place, s32[1,1024]{1,0:T(1,128)} %copy-done.28, ...), custom_call_target="tpu_custom_call" | custom-call | tf_op jit(solution)/shard_map/backward/pallas_call | solution.py:1013
  509.9 1.9 copy-done.9
  514.0 131.3 %fourth.1 = (f32[4,128,2048]{2,1,0:T(8,128)}, bf16[4,128,2048]{2,1,0:T(8,128)(2,1)S(1)}, bf16[4,256,512]{2,1,0:T(8,128)(2,1)S(1)}, bf16[3,256,2048]{2,1,0:T(8,128)(2,1)S(1)}) custom-call(bf16[8,128,2048]{2,1,0:T(8,128)(2,1)} %bitcast.50, bf16[128,2048]{1,0:T(8,128)(2,1)S(1)} %get-tuple-element.92.x_ref, f32[128,2048]{1,0:T(8,128)S(1)} %copy-done.13, ...), custom_call_target="tpu_custom_call" | custom-call | tf_op jit(solution)/shard_map/fourth/pallas_call | solution.py:1024
  646.7 2.2 multiply_reduce_fusion
  651.4 13.7 %norm.1 = f32[8,128]{1,0:T(8,128)S(1)} custom-call(f32[8,128]{1,0:T(8,128)S(1)} %broadcast_in_dim.62.value_ref), custom_call_target="tpu_custom_call" | custom-call | tf_op jit(solution)/shard_map/norm/pallas_call | solution.py:1057
  666.3 1.6 convert_element_type.36
  668.0 1.6 fusion.17
  671.0 3.6 fusion.19
  676.3 7.1 %fusion.13 = (bf16[256,2048]{1,0:T(8,128)(2,1)}, f32[256,2048]{1,0:T(8,128)}, f32[256,2048]{1,0:T(8,128)}, f32[256,2048]{1,0:T(8,128)}, f32[256,2048]{1,0:T(8,128)}) fusion(f32[256,2048]{1,0:T(8,128)S(1)} %copy-done.18, f32[]{:T(128)} %bitcast.25, f32[256,2048]{1,0:T(8,128)} %param.31, f32[256,2048]{1,0:T(8,128)} %param.27, ...), kind=kLoop, calls=%fused_computation.50 | loop fusion | flops 8912896 | bytes 17825796 | tf_op jit(solution)/shard_map/convert_element_type | solution.py:1089
  683.4 10.9 %fusion.15 = (bf16[2,256,2048]{2,1,0:T(8,128)(2,1)}, f32[2,256,2048]{2,1,0:T(8,128)}, f32[2,256,2048]{2,1,0:T(8,128)}, f32[2,256,2048]{2,1,0:T(8,128)}, f32[2,256,2048]{2,1,0:T(8,128)}) fusion(f32[2,256,2048]{2,1,0:T(8,128)S(1)} %copy-done.16, f32[]{:T(128)} %bitcast.25, f32[2,256,2048]{2,1,0:T(8,128)S(1)} %copy-done.21, f32[2,256,2048]{2,1,0:T(8,128)} %param.26, ...), kind=kLoop, calls=%fused_computation.51 | loop fusion | flops 17825792 | bytes 35651588 | tf_op jit(solution)/shard_map/convert_element_type | solution.py:1089
  695.6 1.6 copy-done.22
  697.3 2.1 copy.52
  (78 shorter events, 21.0 us)
Async XLA Ops:
  0.7 1.6 copy-start
  4.5 5.7 copy-start.28
  8.4 2.1 copy-start.19
  8.5 174.0 %copy-start.6 = (bf16[128,2048]{1,0:T(8,128)(2,1)}, bf16[128,2048]{1,0:T(8,128)(2,1)S(1)}, u32[]{:S(2)}) copy-start(bf16[128,2048]{1,0:T(8,128)(2,1)S(1)} %dynamic-slice_bitcast_fusion.cot_ref) | copy-start | bytes 1572868
  12.3 3.2 copy-start.15
  159.1 2.0 copy-start.2
  161.2 2.0 copy-start.3
  296.7 2.0 copy-start.7
  298.7 2.0 copy-start.8
  300.7 55.4 %copy-start.12 = (f32[128,2048]{1,0:T(8,128)}, f32[128,2048]{1,0:T(8,128)S(1)}, u32[]{:S(2)}) copy-start(f32[128,2048]{1,0:T(8,128)S(1)} %get-tuple-element.56.mid_ref) | copy-start | bytes 3145732
  509.9 1.9 copy-start.9
  646.7 2.2 copy-start.4
  651.3 16.6 %copy-start.23 = (f32[256,512]{1,0:T(8,128)S(1)}, f32[256,512]{1,0:T(8,128)}, u32[]{:S(2)}) copy-start(f32[256,512]{1,0:T(8,128)} %param.21) | copy-start | bytes 1572868
  651.3 16.6 %copy-start.26 = (f32[256,512]{1,0:T(8,128)S(1)}, f32[256,512]{1,0:T(8,128)}, u32[]{:S(2)}) copy-start(f32[256,512]{1,0:T(8,128)} %param.29) | copy-start | bytes 1572868
  651.4 16.6 %copy-start.27 = (f32[256,512]{1,0:T(8,128)S(1)}, f32[256,512]{1,0:T(8,128)}, u32[]{:S(2)}) copy-start(f32[256,512]{1,0:T(8,128)} %param.25) | copy-start | bytes 1572868
  666.3 3.3 copy-start.25
  668.0 1.6 copy-start.5
  668.0 2.6 copy-start.20
  668.0 3.0 copy-start.24
  676.3 7.1 %copy-start.16 = (f32[2,256,2048]{2,1,0:T(8,128)S(1)}, f32[2,256,2048]{2,1,0:T(8,128)}, u32[]{:S(2)}) copy-start(f32[2,256,2048]{2,1,0:T(8,128)} %param.22) | copy-start | bytes 12582916
  676.3 7.1 %copy-start.21 = (f32[2,256,2048]{2,1,0:T(8,128)S(1)}, f32[2,256,2048]{2,1,0:T(8,128)}, u32[]{:S(2)}) copy-start(f32[2,256,2048]{2,1,0:T(8,128)} %param.30) | copy-start | bytes 12582916
  683.4 10.9 %copy-start.11 = (bf16[4,128,2048]{2,1,0:T(8,128)(2,1)S(1)}, bf16[4,128,2048]{2,1,0:T(8,128)(2,1)}, u32[]{:S(2)}) copy-start(bf16[4,128,2048]{2,1,0:T(8,128)(2,1)} %copy-done.10) | copy-start | bytes 6291460
  694.3 2.9 copy-start.22
  697.3 3.1 copy-start.1
  (5 other events, 6.8 us)

commit v4 on v3

--- a/solution.py
+++ b/solution.py
@@ -182,104 +182,87 @@
 
 
 class Scatter:
-    def __init__(self, at, partial, own, near, sent, got, send, recv, local):
-        self.at, self.partial, self.own, self.near = at, partial, own, near
-        self.sent, self.got, self.send, self.recv, self.local = sent, got, send, recv, local
-
-    def keep(self, c):
-        return pltpu.make_async_copy(
-            self.partial.at[c * 2 + self.at.lo], self.own.at[c], self.local.at[c]
+    def __init__(self, at, part, near, sent, got, send, recv):
+        self.at, self.part, self.near = at, part, near
+        self.sent, self.got, self.send, self.recv = sent, got, send, recv
+
+    def core(self, c):
+        at = self.at
+        return remote(
+            self.part.at[c * 2 + 1 - at.lo], self.near.at[c], self.send.at[c], self.recv.at[c], at.core
         )
 
-    def core(self, c):
-        at = self.at
-        return remote(
-            self.partial.at[c * 2 + 1 - at.lo], self.near.at[c], self.send.at[c], self.recv.at[c], at.core
-        )
-
-    def far(self, way, hop):
-        at = self.at
-        c = jnp.clip(at.c + way * hop, 0, at.n_c - 1)
-        slot = c if hop > 1 else c + (0 if way > 0 else at.n_c)
+    def far(self, way, hop, slot):
+        at = self.at
         k = at.n_c + hop + (0 if way > 0 else at.n_c)
-        return remote(
-            self.sent.at[c], self.got.at[slot], self.send.at[k], self.recv.at[k], at.z(way)
-        )
+        sent = self.sent.at[jnp.clip(at.c + way * hop, 0, at.n_c - 1)]
+        return remote(sent, self.got.at[slot], self.send.at[k], self.recv.at[k], at.z(way))
+
+    def end(self, way):
+        return self.at.n_c + (0 if way > 0 else 1)
 
     there = Gather.there
 
     def start(self):
         at = self.at
         for i in range(at.n_c):
-            c = jnp.where(at.c * 2 < at.n_c, at.n_c - 1 - i, i)
-            self.core(c).start()
-            self.keep(c).start()
-
-    def pass_on(self):
-        at = self.at
-        for hop in range(at.n_c - 1, 0, -1):
+            self.core(jnp.where(at.c * 2 < at.n_c, at.n_c - 1 - i, i)).start()
+
+    def pass_on(self, hops=None):
+        at = self.at
+        for hop in hops or range(at.n_c - 1, 0, -1):
             for way in (1, -1):
 
                 @pl.when(self.there(way, hop))
                 def _(way=way, hop=hop):
                     c = at.c + way * hop
                     self.core(c).wait_recv()
-                    self.keep(c).wait()
                     if hop < at.n_c - 1:
                         more = self.there(-way, 1)
 
                         @pl.when(more)
                         def _():
-                            self.far(way, hop + 1).wait_recv()
-
-                            def add(rows):
-                                self.sent[c, rows] = (
-                                    self.own[c, rows].astype(F32)
-                                    + self.near[c, rows].astype(F32)
-                                    + self.got[c, rows].astype(F32)
-                                ).astype(BF)
-
-                            by_rows(self.own.shape[1], add)
+                            self.far(way, hop + 1, c).wait_recv()
+                            self.add(c, True)
 
                         @pl.when(jnp.logical_not(more))
                         def _():
-                            self.both(c)
+                            self.add(c, False)
 
                     else:
-                        self.both(c)
-                    self.far(way, hop).start()
-
-        self.core(at.c).wait_recv()
-        self.keep(at.c).wait()
-
-    def both(self, c):
-        def add(rows):
-            self.sent[c, rows] = (
-                self.own[c, rows].astype(F32) + self.near[c, rows].astype(F32)
-            ).astype(BF)
-
-        by_rows(self.own.shape[1], add)
+                        self.add(c, False)
+                    self.far(way, hop, self.end(way) if hop == 1 else c).start()
+
+    def add(self, c, more):
+        at = self.at
+
+        def rows_of(rows):
+            value = self.part[c * 2 + at.lo, rows].astype(F32) + self.near[c, rows].astype(F32)
+            if more:
+                value = value + self.got[c, rows].astype(F32)
+            self.sent[c, rows] = value.astype(BF)
+
+        by_rows(self.near.shape[1], rows_of)
 
     def arrive(self):
-        at = self.at
+        self.core(self.at.c).wait_recv()
         for way in (1, -1):
 
             @pl.when(self.there(-way, 1))
             def _(way=way):
-                self.far(way, 1).wait_recv()
+                self.far(way, 1, self.end(way)).wait_recv()
 
             @pl.when(jnp.logical_not(self.there(-way, 1)))
             def _(way=way):
-                slot = at.c + (0 if way > 0 else at.n_c)
-                self.got[slot] = jnp.zeros(self.got.shape[1:], BF)
+                self.got[self.end(way)] = jnp.zeros(self.got.shape[1:], BF)
 
     def total(self, rows):
-        c = self.at.c
+        c, at = self.at.c, self.at
         return (
-            self.own[c, rows].astype(F32)
+            self.part[c * 2 + at.lo, rows].astype(F32)
             + self.near[c, rows].astype(F32)
-            + self.got[c, rows].astype(F32)
-            + self.got[c + self.at.n_c, rows].astype(F32)
+            + self.got[self.end(1), rows].astype(F32)
+            + self.got[self.end(-1), rows].astype(F32)
         )
 
     def finish(self):
@@ -291,18 +274,17 @@
 
                 @pl.when(self.there(way, hop))
                 def _(way=way, hop=hop):
-                    self.far(way, hop).wait_send()
+                    self.far(way, hop, 0).wait_send()
 
 
 def scatter_scratch(n_c, half, width):
     return [
+        pltpu.VMEM((2 * n_c, half, width), BF),
         pltpu.VMEM((n_c, half, width), BF),
         pltpu.VMEM((n_c, half, width), BF),
-        pltpu.VMEM((n_c, half, width), BF),
-        pltpu.VMEM((2 * n_c, half, width), BF),
+        pltpu.VMEM((n_c + 2, half, width), BF),
         pltpu.SemaphoreType.DMA((3 * n_c,)),
         pltpu.SemaphoreType.DMA((3 * n_c,)),
-        pltpu.SemaphoreType.DMA((n_c,)),
     ]
 
 
@@ -547,6 +529,15 @@
     return values * cos + pltpu.roll(values, HEAD_DIM // 2, 1) * sine
 
 
+def round_all(wide, low):
+    for m in range(wide.shape[0]):
+
+        def step(rows, m=m):
+            low[m, rows] = wide[m, rows].astype(BF)
+
+        by_rows(wide.shape[1], step)
+
+
 def dma(count):
     return pltpu.SemaphoreType.DMA((count,))
 
@@ -578,66 +569,117 @@
             name=name,
         )
 
-    def first_kernel(
-        a1_ref, att_ref, ff_ref, rows_ref, attw_ref, ffw_ref, gs, gr, gl, s1, r1, l1, s2, r2, l2, s3, r3
+    def front_kernel(
+        tok_ref, cot_ref, place, key_place, first, cos, sine, att_ref, out_ref, ffp_ref, ffo_ref,
+        rows_ref, attw_ref, ffw_ref, a2_ref, cots_ref, qkv, attended, mass, mid_ref,
+        x_ref, own_cot, att_wide, ff_wide, att_low, ff_low, low, a1, packed, lk, lp,
+        part, near, sent, got, ss, sr, g1, h1, l1, g2, h2, l2, g3, h3, l3, s4, r4, l4, s5, r5, l5, s6, r6, s7, r7,
     ):
         at = Place(sizes)
+        half = x_ref.shape[0]
+        mine = pl.ds(pl.multiple_of(at.lo * half, half), half)
+        loads = [
+            pltpu.make_async_copy(tok_ref.at[at.hi, mine], x_ref, lk.at[0]),
+            pltpu.make_async_copy(att_ref, att_wide.at[pl.ds(0, 3)], lk.at[1]),
+            pltpu.make_async_copy(out_ref, att_wide.at[3], lk.at[2]),
+            pltpu.make_async_copy(ffp_ref, ff_wide.at[pl.ds(0, 2)], lk.at[3]),
+            pltpu.make_async_copy(ffo_ref, ff_wide.at[2], lk.at[4]),
+            pltpu.make_async_copy(cot_ref.at[at.hi, mine], own_cot, lk.at[5]),
+        ]
+        for copy in loads:
+            copy.start()
+        scatter = Scatter(at, part, near, sent, got, ss, sr)
+        gather = Gather(at, low, rows_ref, g1, h1, l1)
+        cots = Gather(at, own_cot, cots_ref, g2, h2, l2)
+        a2 = Gather(at, low, a2_ref, g3, h3, l3)
+        swap_att = Swap(at, att_low, attw_ref, s4, r4, l4)
+        swap_ff = Swap(at, ff_low, ffw_ref, s5, r5, l5)
+        spread_att = Spread(at, attw_ref, s6, r6)
+        spread_ff = Spread(at, ffw_ref, s7, r7)
+        loads[0].wait()
+
+        def norm_one(rows):
+            low[rows] = mean_spread(x_ref[rows].astype(F32))[0].astype(BF)
+
+        by_rows(half, norm_one)
+        loads[1].wait()
+        loads[2].wait()
+        round_all(att_wide, att_low)
         at.greet([at.core, *at.all_z(), *at.all_xy()])
-        gather = Gather(at, a1_ref, rows_ref, gs, gr, gl)
-        swap_att = Swap(at, att_ref, attw_ref, s1, r1, l1)
-        swap_ff = Swap(at, ff_ref, ffw_ref, s2, r2, l2)
-        spread = Spread(at, attw_ref, s3, r3)
+        gather.start()
         swap_att.start()
-        gather.start()
+        for copy in loads[3:]:
+            copy.wait()
+        round_all(ff_wide, ff_low)
+        gather.forward(range(1, 2))
+        swap_att.wait()
+        spread_att.start()
+        gather.forward(range(2, n_c - 1))
         swap_ff.start()
-        swap_att.wait()
-        spread.start()
-        gather.forward()
-        spread.forward()
+        gather.forward(range(n_c - 1, n_c))
+        spread_att.forward()
         gather.finish()
-        spread.wait()
+        take = [pltpu.make_async_copy(rows_ref.at[b], a1.at[pl.ds(b * half, half)], lp.at[b]) for b in range(2 * n_c)]
+        for copy in take:
+            copy.start()
+        spread_att.wait()
+        heads = attw_ref.shape[0]
+        packs = [
+            pltpu.make_async_copy(
+                attw_ref.at[y, i],
+                packed.at[:, pl.ds((i * heads + y) * HEAD_DIM, HEAD_DIM)],
+                lp.at[2 * n_c + i * heads + y],
+            )
+            for i in range(4)
+            for y in range(heads)
+        ]
+        for copy in packs:
+            copy.start()
+        for copy in (*take, *packs):
+            copy.wait()
+        attend(a1, packed, place, key_place, first, cos, sine, qkv, attended, mass, part)
+        scatter.start()
+        scatter.pass_on(range(n_c - 1, 1, -1))
         swap_ff.wait()
-
-    def second_kernel(
-        part_ref, x_ref, cot_ref, ffw_in, a2_ref, cots_ref, mid_ref, ffw_ref,
-        own, near, sent, got, ss, sr, sl, low, s1, r1, l1, s2, r2, l2, s3, r3,
-    ):
-        at = Place(sizes)
-        at.greet([at.core, *at.all_z(), *at.all_xy()])
-        scatter = Scatter(at, part_ref, own, near, sent, got, ss, sr, sl)
-        spread = Spread(at, ffw_ref, s3, r3)
-        cots = Gather(at, cot_ref, cots_ref, s1, r1, l1)
-        scatter.start()
-        spread.start()
-        scatter.pass_on()
+        spread_ff.start()
+        scatter.pass_on(range(1, 2))
         cots.start()
         scatter.arrive()
 
-        def norm(rows):
+        def norm_two(rows):
             mid = x_ref[rows].astype(F32) + scatter.total(rows)
             mid_ref[rows] = mid
             low[rows] = mean_spread(mid)[0].astype(BF)
 
-        by_rows(x_ref.shape[0], norm)
-        a2 = Gather(at, low, a2_ref, s2, r2, l2)
+        by_rows(half, norm_two)
         a2.start()
-        spread.forward()
-        for hop in range(1, n_c):
+        cots.forward(range(1, 2))
+        a2.forward(range(1, 2))
+        spread_ff.forward()
+        for hop in range(2, n_c):
+            a2.forward(range(hop, hop + 1))
             cots.forward(range(hop, hop + 1))
-            a2.forward(range(hop, hop + 1))
         cots.finish()
         a2.finish()
         scatter.finish()
-        spread.wait()
+        spread_ff.wait()
 
     def third_kernel(
         part_ref, branch_ref, mid_ref, cot_ref, grad_ref, rows_ref, block_ref, own_ref, sum_ref,
-        own, near, sent, got, ss, sr, sl, own2, near2, sent2, got2, ss2, sr2, sl2, low, s1, r1, l1, *collected,
+        part, near, sent, got, ss, sr, part2, near2, sent2, got2, ss2, sr2, ls, low, s1, r1, l1, *collected,
     ):
         at = Place(sizes)
+        loads = [
+            pltpu.make_async_copy(part_ref, part, ls.at[0]),
+            pltpu.make_async_copy(branch_ref, part2, ls.at[1]),
+        ]
+        for copy in loads:
+            copy.start()
         at.greet([at.core, *at.all_z(), *at.all_xy()])
-        scatter = Scatter(at, part_ref, own, near, sent, got, ss, sr, sl)
-        branch = Scatter(at, branch_ref, own2, near2, sent2, got2, ss2, sr2, sl2)
+        scatter = Scatter(at, part, near, sent, got, ss, sr)
+        branch = Scatter(at, part2, near2, sent2, got2, ss2, sr2)
+        for copy in loads:
+            copy.wait()
         collect = Collect(at, grad_ref, *collected)
         scatter.start()
         collect.start()
@@ -672,12 +714,15 @@
 
     def fourth_kernel(
         part_ref, x_ref, mid_ref, block_ref, att_ref, ff_ref, input_ref, out_ref, attg_ref, ffg_ref,
-        own, near, sent, got, ss, sr, sl, total, low, s1, r1, l1, s2, r2, l2, s4, r4, l4, *collected,
+        part, near, sent, got, ss, sr, total, low, s1, r1, l1, s2, r2, l2, s4, r4, l4, *collected,
     ):
         at = Place(sizes)
+        load = pltpu.make_async_copy(part_ref, part, l4.at[2])
+        load.start()
         tps = [(at.f, at.c, lax.rem(at.t + s, n_t)) for s in range(1, n_t)]
         at.greet([*tps, *at.all_z(), *[at.xy(s, o) for s, o in at.pairs if s]])
-        scatter = Scatter(at, part_ref, own, near, sent, got, ss, sr, sl)
+        load.wait()
+        scatter = Scatter(at, part, near, sent, got, ss, sr)
         collect = Collect(at, att_ref, *collected)
         give_ff = Return(at, ff_ref, ffg_ref, s2, r2, l2)
         scatter.start()
@@ -714,35 +759,136 @@
         give_att.wait()
         give_ff.wait()
 
-    def norm_kernel(value_ref, out_ref, total, got_t, got_c, got_f, send, recv):
+    def norm_kernel(attg_ref, ffg_ref, norm_ref, low_att, low_ff, total, got_t, got_c, got_f, send, recv, ls):
         at = Place(sizes)
+        loads = [
+            pltpu.make_async_copy(attg_ref, low_att, ls.at[0]),
+            pltpu.make_async_copy(ffg_ref, low_ff, ls.at[1]),
+        ]
+        for copy in loads:
+            copy.start()
         tps = [(at.f, at.c, lax.rem(at.t + s, n_t)) for s in range(1, n_t)]
         fs = [at.xy(s, 0) for s in range(1, n_f)]
         at.greet([*tps, *at.all_z(), *fs])
-        total[0] = value_ref[...]
+        for copy in loads:
+            copy.wait()
+        sum_norm(at, (low_att, low_ff), norm_ref, total, got_t, got_c, got_f, send, recv)
+
+    def sum_norm(at, grads, norm_ref, total, got_t, got_c, got_f, send, recv):
+        tps = [(at.f, at.c, lax.rem(at.t + s, n_t)) for s in range(1, n_t)]
+        fs = [at.xy(s, 0) for s in range(1, n_f)]
+        total[0] = jnp.zeros(total.shape[1:], F32)
+        for low in grads:
+            for m in range(low.shape[0]):
+
+                def square(rows, low=low, m=m):
+                    value = low[m, rows].astype(F32)
+                    value = value * value
+                    value = value[: ROWS // 2] + value[ROWS // 2 :]
+                    lanes = value[:, :128]
+                    for c in range(1, value.shape[1] // 128):
+                        lanes = lanes + value[:, c * 128 : (c + 1) * 128]
+                    total[0] += lanes
+
+                by_rows(low.shape[1], square)
         base = 0
-        for stage, (peers, got) in enumerate(((tps, got_t), (at.all_z(), got_c), (fs, got_f))):
+        stages = ((tps, got_t, at.t), (at.all_z(), got_c, at.c), (fs, got_f, at.f))
+        for stage, (peers, got, place) in enumerate(stages):
             copies = [
-                remote(total.at[stage], got.at[i], send.at[base + i], recv.at[base + i], peer)
+                remote(total.at[stage], got.at[place], send.at[base + i], recv.at[base + i], peer)
                 for i, peer in enumerate(peers)
             ]
             base += len(peers)
             for copy in copies:
                 copy.start()
+            got[place] = total[stage]
             for copy in copies:
                 copy.wait()
-            value = total[stage]
-            for i in range(len(peers)):
+            value = got[0]
+            for i in range(1, got.shape[0]):
                 value = value + got[i]
             total[stage + 1] = value
-        out_ref[...] = total[3]
-
-    def forward_kernel(
-        a1, w, place, key_place, first, cos, sine, qkv, attended, mass, part, packed
-    ):
-        heads = w.shape[0]
-        wide = heads * HEAD_DIM
-        pack_weights(w, packed)
+        norm = jnp.sqrt(jnp.sum(total[3], axis=(0, 1), keepdims=True))
+        norm_ref[...] = jnp.broadcast_to(norm, norm_ref.shape)
+
+    def finish_kernel(norm_ref, block_in, input_in, attg_ref, ffg_ref, *refs):
+        olds, outs, scratch = refs[:12], refs[12:34], refs[34:]
+        low_att, low_ff, wide_att, wide_ff, old_att, old_ff, block_keep, input_keep, ls = scratch
+        groups = (
+            (attg_ref, low_att, wide_att, old_att, 0, attg_ref.shape[1]),
+            (ffg_ref, low_ff, wide_ff, old_ff, 2, attg_ref.shape[1] // 4),
+        )
+        chunks = [
+            (group, m, r)
+            for group in groups
+            for m in range(group[0].shape[0])
+            for r in range(group[0].shape[1] // group[5])
+        ]
+
+        def sheet(array, first, m, group):
+            last = group[0].shape[0] - 1
+            return array[first + 1] if m == last else array[first].at[m]
+
+        loads, stores = [], []
+        for i, (group, m, r) in enumerate(chunks):
+            here = pl.ds(r * group[5], group[5])
+            one = [pltpu.make_async_copy(group[0].at[m, here], group[1].at[m, here], ls.at[i, 0, 3])]
+            one += [
+                pltpu.make_async_copy(
+                    sheet(olds, 4 * j + group[4], m, group).at[here], group[3].at[j, m, here], ls.at[i, 0, j]
+                )
+                for j in range(3)
+            ]
+            for copy in one:
+                copy.start()
+            loads.append(one)
+        kept = ((block_in, block_keep, outs[20]), (input_in, input_keep, outs[21]))
+        through = []
+        for i, (src, keep, out) in enumerate(kept):
+            copy = pltpu.make_async_copy(src, keep, ls.at[len(chunks), 0, i])
+            copy.start()
+            through.append((copy, pltpu.make_async_copy(keep, out, ls.at[len(chunks), 1, i])))
+        norm = norm_ref[0:1, 0:1]
+        clip = jnp.minimum(1.0, MAX_NORM / (norm + 1e-06))
+        width = ffg_ref.shape[1] * n_f * n_c
+        for i, (group, m, r) in enumerate(chunks):
+            for copy in loads[i]:
+                copy.wait()
+            low, wide, old = group[1:4]
+            rate = (width // 32) ** (-0.5) if group[4] == 0 and m == 3 else width ** (-0.5)
+
+            @pl.loop(0, group[5] // ROWS)
+            def _(k, low=low, wide=wide, old=old, m=m, r=r, step=group[5], rate=rate):
+                rows = pl.ds(pl.multiple_of(r * step + k * ROWS, ROWS), ROWS)
+                grad = low[m, rows].astype(F32)
+                wide[m, rows] = grad
+                first_new, second_new, weight_new = adam_step(
+                    old[0, m, rows], grad, old[1, m, rows], old[2, m, rows], clip, rate
+                )
+                old[0, m, rows] = weight_new
+                old[1, m, rows] = first_new
+                old[2, m, rows] = second_new
+                low[m, rows] = weight_new.astype(BF)
+
+            here = pl.ds(r * group[5], group[5])
+            for k, (src, out) in enumerate(
+                ((wide, 0), (old.at[1], 4), (old.at[2], 8), (old.at[0], 12), (low, 16))
+            ):
+                store = pltpu.make_async_copy(
+                    src.at[m, here], sheet(outs, out + group[4], m, group).at[here], ls.at[i, 1, k]
+                )
+                store.start()
+                stores.append(store)
+        for load, store in through:
+            load.wait()
+            store.start()
+            stores.append(store)
+        for store in stores:
+            store.wait()
+
+    def attend(a1, packed, place, key_place, first, cos, sine, qkv, attended, mass, part):
+        wide = attended.shape[1]
+        heads = wide // HEAD_DIM
         for i in range(3):
             joint = dot(a1[...], packed[:, i * wide : (i + 1) * wide], ((1,), (0,)))
             for y in range(heads):
@@ -767,12 +913,13 @@
                 attended[rows, cols] = dot(probs, qkv[2, :, cols], ((1,), (0,))).astype(BF)
                 mass[rows, y : y + 1] = peak + jnp.log(total)
 
-        width = part.shape[1] // 4
+        width = part.shape[2] // 4
 
         @pl.loop(0, 4)
         def _(c):
             cols = pl.ds(pl.multiple_of(c * width, width), width)
-            part[:, cols] = dot(attended[...], packed[cols, 3 * wide :], ((1,), (1,))).astype(BF)
+            value = dot(attended[...], packed[cols, 3 * wide :], ((1,), (1,))).astype(BF)
+            part[:, :, cols] = value.reshape(part.shape[0], part.shape[1], width)
 
     def backward_kernel(
         mid, a1, w, place, key_place, first, cos, sine, qkv, attended, mass, part, grad, packed, joint, d_v, d_k
@@ -903,27 +1050,10 @@
 
         own_tokens = own_rows(tokens)
         own_cot = own_rows(cotangent)
-        att_low = jnp.concatenate([att_proj, attn_out[None]]).astype(BF)
-        ff_low = jnp.concatenate([ff_proj, ff_out[None]]).astype(BF)
-        normed_one, _ = mean_spread(own_tokens.astype(F32))
-        att_cols, ff_cols = att_low.shape[2] // n_c, ff_low.shape[2] // n_c
-        act_one, att_w, ff_w = call(
-            first_kernel,
-            "first",
-            0,
-            (
-                rows_bf,
-                jax.ShapeDtypeStruct((2, 4, width, att_cols), BF),
-                jax.ShapeDtypeStruct((2, 3, width, ff_cols), BF),
-            ),
-            [ANY] * 3,
-            (ANY,) * 3,
-            gather_sems(n_c)
-            + [dma(n_c), dma(n_c), pltpu.SemaphoreType.DMA] * 2
-            + [dma(5 * n_f), dma(5 * n_f)],
-        )(normed_one.astype(BF), att_low, ff_low)
-        act_one = act_one.reshape(pack_len, width)
-
+        att_cols, ff_cols = att_proj.shape[2] // n_c, ff_proj.shape[2] // n_c
+        att_shape, ff_shape = (4, *att_proj.shape[1:]), (3, *ff_proj.shape[1:])
+        att_full = jax.ShapeDtypeStruct((2, 4, width, att_cols), BF)
+        ff_full = jax.ShapeDtypeStruct((2, 3, width, ff_cols), BF)
         places = lax.dynamic_index_in_dim(deal, pack_at, 0, keepdims=False)
         length_row = lax.dynamic_index_in_dim(lengths, pack_at, 0, keepdims=False)
         seqs = lengths.shape[1]
@@ -945,30 +1075,43 @@
             jnp.concatenate([-sine_table, sine_table], axis=1),
         )
         rank_width = 2 * att_cols
-        qkv, attended, mass, out_part = local(
-            forward_kernel,
-            "forward",
+        act_one, att_w, ff_w, act_two, cot_rows, qkv, attended, mass, resid_mid = call(
+            front_kernel,
+            "front",
+            0,
             (
+                rows_bf,
+                att_full,
+                ff_full,
+                rows_bf,
+                rows_bf,
                 jax.ShapeDtypeStruct((3, pack_len, rank_width), BF),
                 jax.ShapeDtypeStruct((pack_len, rank_width), BF),
                 jax.ShapeDtypeStruct((pack_len, 2), F32),
-                jax.ShapeDtypeStruct((pack_len, width), BF),
+                own_f32,
             ),
-            [pltpu.VMEM((width, 4 * rank_width), BF)],
-        )(act_one, att_w, *tables)
-        act_two, cot_rows, resid_mid, ff_w = call(
-            second_kernel,
-            "second",
-            1,
-            (rows_bf, rows_bf, own_f32, jax.ShapeDtypeStruct(ff_w.shape, BF)),
-            [ANY, VMEM, VMEM, ANY],
-            (ANY, ANY, VMEM, ANY),
-            scatter_scratch(n_c, half, width)
-            + [pltpu.VMEM((half, width), BF)]
-            + gather_sems(n_c) * 2
-            + [dma(5 * n_f), dma(5 * n_f)],
-            {3: 3},
-        )(out_part.reshape(rows_bf.shape), own_tokens, own_cot, ff_w)
+            [ANY, ANY] + [VMEM] * 5 + [ANY] * 4,
+            (ANY,) * 5 + (VMEM,) * 4,
+            [
+                pltpu.VMEM((half, width), BF),
+                pltpu.VMEM((half, width), BF),
+                pltpu.VMEM(att_shape, F32),
+                pltpu.VMEM(ff_shape, F32),
+                pltpu.VMEM(att_shape, BF),
+                pltpu.VMEM(ff_shape, BF),
+                pltpu.VMEM((half, width), BF),
+                pltpu.VMEM((pack_len, width), BF),
+                pltpu.VMEM((width, 4 * rank_width), BF),
+                dma(6),
+                dma(2 * n_c + 8),
+            ]
+            + scatter_scratch(n_c, half, width)
+            + gather_sems(n_c) * 3
+            + [dma(n_c), dma(n_c), pltpu.SemaphoreType.DMA] * 2
+            + [dma(5 * n_f)] * 4,
+            vmem=56,
+        )(tokens, cotangent, *tables, att_proj, attn_out, ff_proj, ff_out)
+        act_one = act_one.reshape(pack_len, width)
         act_two = act_two.reshape(pack_len, width)
         cot_rows = cot_rows.reshape(pack_len, width)
 
@@ -997,7 +1140,7 @@
             [ANY, ANY, VMEM, VMEM, ANY],
             (ANY, VMEM, VMEM, VMEM),
             scatter_scratch(n_c, half, width) * 2
-            + [pltpu.VMEM((half, width), BF)]
+            + [dma(2), pltpu.VMEM((half, width), BF)]
             + gather_sems(n_c)
             + collect_scratch(n_f, 3, height, ff_cols),
             vmem=56,
@@ -1028,8 +1171,8 @@
             (
                 jax.ShapeDtypeStruct((n_t, half, width), F32),
                 jax.ShapeDtypeStruct((n_t, half, width), BF),
-                jax.ShapeDtypeStruct(att_low.shape, BF),
-                jax.ShapeDtypeStruct(ff_low.shape, BF),
+                jax.ShapeDtypeStruct(att_shape, BF),
+                jax.ShapeDtypeStruct(ff_shape, BF),
             ),
             [ANY, VMEM, VMEM, ANY, ANY, ANY],
             (ANY,) * 4,
@@ -1039,7 +1182,7 @@
             + [
                 pltpu.SemaphoreType.DMA((2, n_t - 1)),
                 pltpu.SemaphoreType.DMA((2, n_t - 1)),
-                dma(2),
+                dma(3),
             ]
             + collect_scratch(n_f, 4, height, att_cols),
         )(
@@ -1050,43 +1193,51 @@
             att_grad,
             ff_sum,
         )
-        att_total, ff_total = att_total.astype(F32), ff_total.astype(F32)
-
-        square = jnp.sum(att_total * att_total) + jnp.sum(ff_total * ff_total)
+        weights = (att_proj, attn_out, ff_proj, ff_out)
+        firsts_old = (att_proj_first, attn_out_first, ff_proj_first, ff_out_first)
+        seconds_old = (att_proj_second, attn_out_second, ff_proj_second, ff_out_second)
         count = n_f + n_c + n_t
-        square_sum = call(
+        norm_value = call(
             norm_kernel,
             "norm",
             4,
             jax.ShapeDtypeStruct((8, 128), F32),
-            [VMEM],
+            [ANY] * 2,
             VMEM,
-            [pltpu.VMEM((k, 8, 128), F32) for k in (4, n_t - 1, n_c - 1, n_f - 1)]
-            + [dma(count), dma(count)],
-            vmem=8,
-        )(jnp.broadcast_to(square, (8, 128)))[0, 0]
-        norm_value = jnp.sqrt(square_sum)
-        clip_factor = jnp.minimum(1.0, MAX_NORM / (norm_value + 1e-06))
-        base_rate = width ** (-0.5)
-        out_rate = (width // 32) ** (-0.5)
-        grads = (att_total[:3], att_total[3], ff_total[:2], ff_total[2])
-        weights = (att_proj, attn_out, ff_proj, ff_out)
-        firsts_old = (att_proj_first, attn_out_first, ff_proj_first, ff_out_first)
-        seconds_old = (att_proj_second, attn_out_second, ff_proj_second, ff_out_second)
-        rates = (base_rate, out_rate, base_rate, base_rate)
-        news = [
-            adam_step(w, g, m, v, clip_factor, r)
-            for w, g, m, v, r in zip(weights, grads, firsts_old, seconds_old, rates)
-        ]
+            [pltpu.VMEM(att_shape, BF), pltpu.VMEM(ff_shape, BF)]
+            + [pltpu.VMEM((k, 8, 128), F32) for k in (4, n_t, n_c, n_f)]
+            + [dma(count), dma(count), dma(2)],
+            vmem=16,
+        )(att_total, ff_total)
+        results = pl.pallas_call(
+            finish_kernel,
+            out_shape=(
+                *(jax.ShapeDtypeStruct(w.shape, F32) for w in weights * 4),
+                *(jax.ShapeDtypeStruct(w.shape, BF) for w in weights),
+                jax.ShapeDtypeStruct(block_out.shape, BF),
+                jax.ShapeDtypeStruct(input_grad.shape, F32),
+            ),
+            in_specs=[VMEM] + [ANY] * 16,
+            out_specs=(ANY,) * 22,
+            scratch_shapes=[
+                pltpu.VMEM(att_shape, BF),
+                pltpu.VMEM(ff_shape, BF),
+                pltpu.VMEM(att_shape, F32),
+                pltpu.VMEM(ff_shape, F32),
+                pltpu.VMEM((3, *att_shape), F32),
+                pltpu.VMEM((3, *ff_shape), F32),
+                pltpu.VMEM(block_out.shape, BF),
+                pltpu.VMEM(input_grad.shape, F32),
+                pltpu.SemaphoreType.DMA((17, 2, 5)),
+            ],
+            compiler_params=pltpu.CompilerParams(vmem_limit_bytes=56 << 20),
+            name="finish",
+        )(norm_value, block_out, input_grad, att_total, ff_total, *weights, *firsts_old, *seconds_old)
         return (
-            block_out.reshape(tokens.shape),
-            input_grad.reshape(tokens.shape),
-            norm_value.reshape(1),
-            *grads,
-            *(n[0] for n in news),
-            *(n[1] for n in news),
-            *(n[2] for n in news),
-            *(n[2].astype(BF) for n in news),
+            results[20].reshape(tokens.shape),
+            results[21].reshape(tokens.shape),
+            norm_value[0, :1],
+            *results[:20],
         )
 
     return shards

time: 710 us -> 660 us (0.930); the launches traced: 702 us -> 659 us
  other arithmetic: 37.2 us -> 4.11 us
  local copies, waits for them, and re-layouts: 29.5 us -> 10.3 us
  Pallas kernels: 631 us -> 644 us
    convert_element_type x7 -> x0, other arithmetic: 26 us -> none  [the longest x4 23.2 us: shards(): n[2].astype(BF)]
    unnamed x60 -> x20, local copies, waits for them, and re-layouts: 24.8 us -> 4.28 us
    pallas_call x4 -> x3, Pallas kernels: 290 us -> 305 us  [the longest x1 260 us: shards(): call(front_kernel, 'front', 0, (rows_bf, att_full, ff_full, rows_bf, rows...]
where the time goes in v4:
time: 660 us; the launch traced here: 659 us
  Pallas kernels  644 us (98%)
  local copies, waits for them, and re-layouts  10.3 us (2%)
    pallas_call x1, Pallas kernels, shards(): call(front_kernel, 'front', 0, (rows_bf, att_full, ff_full, rows_bf, rows...  260 us
    pallas_call x1, Pallas kernels, shards(): call(fourth_kernel, 'fourth', 3, (jax.ShapeDtypeStruct((n_t, half, width)...  130 us
    pallas_call x1, Pallas kernels, shards(): call(third_kernel, 'third', 2, (rows_bf, own_bf, own_f32, jax.ShapeDtypeS...  122 us
    pallas_call x1, Pallas kernels, shards(): pl.pallas_call(hidden_kernel, grid=(2 * tiles,), out_shape=(rows_flat, ro...  55.1 us
    pallas_call x1, Pallas kernels, shards(): local(backward_kernel, 'backward', (rows_flat, jax.ShapeDtypeStruct(att_w...  32 us
    pallas_call x1, Pallas kernels, shards(): pl.pallas_call(finish_kernel, out_shape=(*(jax.ShapeDtypeStruct(w.shape,...  29.2 us
    pallas_call x1, Pallas kernels, shards(): call(norm_kernel, 'norm', 4, jax.ShapeDtypeStruct((8, 128), F32), [ANY] *...  15.6 us

profile of v4, /device:TPU:0, one launch (start us, length us, event | category | flops | bytes accessed | tf_op | source)
XLA Modules:
  0.0 659.3 jit_solution(4227985634960508155)
XLA Ops:
  0.7 0.0 copy-start
  0.7 0.7 fusion.4
  1.4 0.1 fusion.2
  1.5 0.7 fusion.3
  2.2 0.0 copy-done
  2.2 0.0 copy-start.9
  2.2 0.1 fusion.1
  2.3 1.9 fusion
  4.2 1.3 pad_maximum_fusion
  5.5 1.0 copy.44.first
  6.6 1.0 copy.43.place
  7.6 260.3 %front.1 = (bf16[8,128,2048]{2,1,0:T(8,128)(2,1)}, bf16[2,4,2048,128]{3,2,1,0:T(8,128)(2,1)}, bf16[2,3,2048,512]{3,2,1,0:T(8,128)(2,1)}, bf16[8,128,2048]{2,1,0:...) custom-call(bf16[2,256,2048]{2,1,0:T(8,128)(2,1)} %tok_ref.1, ...), custom_call_target="tpu_custom_call" | custom-call | tf_op jit(solution)/shard_map/front/pallas_call | solution.py:1078
  268.0 55.1 %hidden.1 = (bf16[1024,2048]{1,0:T(8,128)(2,1)}, bf16[1024,2048]{1,0:T(8,128)(2,1)}, bf16[2,3,2048,512]{3,2,1,0:T(8,128)(2,1)}) custom-call(bf16[1024,2048]{1,0:T(8,128)(2,1)} %bitcast.30, bf16[1024,2048]{1,0:T(8,128)(2,1)} %bitcast.31, bf16[2,3,2048,512]{3,2,1,0:T(8,128)(2,1)} %get-tuple-element.69.w), custom_call_target="tpu_custom_call" | custom-call | tf_op jit(solution)/shard_map/hidden/pallas_call | solution.py:1123
  323.0 2.1 dynamic-slice_bitcast_fusion
  325.1 121.7 %third.1 = (bf16[8,128,2048]{2,1,0:T(8,128)(2,1)}, bf16[128,2048]{1,0:T(8,128)(2,1)}, f32[128,2048]{1,0:T(8,128)}, bf16[3,1024,512]{2,1,0:T(8,128)(2,1)}) custom-call(bf16[8,128,2048]{2,1,0:T(8,128)(2,1)} %bitcast.33, bf16[8,128,2048]{2,1,0:T(8,128)(2,1)} %bitcast.34, f32[128,2048]{1,0:T(8,128)} %get-tuple-element.72.mid_ref, ...), custom_call_target="tpu_custom_call" | custom-call | tf_op jit(solution)/shard_map/third/pallas_call | solution.py:1135
  446.8 32.0 %backward.1 = (bf16[1024,2048]{1,0:T(8,128)(2,1)}, bf16[2,4,2048,128]{3,2,1,0:T(8,128)(2,1)}) custom-call(bf16[1024,2048]{1,0:T(8,128)(2,1)} %bitcast.29, bf16[1024,2048]{1,0:T(8,128)(2,1)} %bitcast.28, bf16[2,4,2048,128]{3,2,1,0:T(8,128)(2,1)} %get-tuple-element.76.w, s32[1024,1]{1,0:T(8,128)} %copy.43.place, s32[1,1024]{1,0:T(1,128)} %copy-done.9, ...), custom_call_target="tpu_custom_call" | custom-call | tf_op jit(solution)/shard_map/backward/pallas_call | solution.py:1156
  478.8 1.2 copy-done.6
  480.0 1.0 copy-done.7
  481.1 130.2 %fourth.1 = (f32[4,128,2048]{2,1,0:T(8,128)}, bf16[4,128,2048]{2,1,0:T(8,128)(2,1)S(1)}, bf16[4,256,512]{2,1,0:T(8,128)(2,1)S(1)}, bf16[3,256,2048]{2,1,0:T(8,128)(2,1)S(1)}) custom-call(bf16[8,128,2048]{2,1,0:T(8,128)(2,1)} %bitcast.32, bf16[128,2048]{1,0:T(8,128)(2,1)S(1)} %get-tuple-element.116.x_ref, f32[128,2048]{1,0:T(8,128)S(1)} %copy-done.6, ...), custom_call_target="tpu_custom_call" | custom-call | tf_op jit(solution)/shard_map/fourth/pallas_call | solution.py:1167
  611.3 1.4 copy-done.5
  612.7 15.6 %norm.1.norm_ref = f32[8,128]{1,0:T(8,128)S(1)} custom-call(bf16[4,256,512]{2,1,0:T(8,128)(2,1)S(1)} %get-tuple-element.85.attg_ref, bf16[3,256,2048]{2,1,0:T(8,128)(2,1)S(1)} %get-tuple-element.86.ffg_ref), custom_call_target="tpu_custom_call" | custom-call | tf_op jit(solution)/shard_map/norm/pallas_call | solution.py:1200
  628.3 0.6 copy-done.8
  628.9 29.2 %finish.1 = (f32[3,256,512]{2,1,0:T(8,128)}, f32[256,512]{1,0:T(8,128)}, f32[2,256,2048]{2,1,0:T(8,128)}, f32[256,2048]{1,0:T(8,128)}, f32[3,256,512]{2,1,0:T(8,...) custom-call(f32[8,128]{1,0:T(8,128)} %copy-done.8, ...), custom_call_target="tpu_custom_call" | custom-call | tf_op jit(solution)/shard_map/finish/pallas_call | solution.py:1212
  658.1 1.2 slice.3
  (17 shorter events, 0.1 us)
Async XLA Ops:
  0.7 1.5 copy-start
  2.2 5.4 copy-start.9
  446.8 32.0 %copy-start.4 = (bf16[3,1024,512]{2,1,0:T(8,128)(2,1)S(1)}, bf16[3,1024,512]{2,1,0:T(8,128)(2,1)}, u32[]{:S(2)}) copy-start(bf16[3,1024,512]{2,1,0:T(8,128)(2,1)} %get-tuple-element.84.ff_ref) | copy-start | bytes 9437188
  478.8 1.2 copy-start.6
  480.0 1.0 copy-start.7
  611.3 1.4 copy-start.5
  612.7 16.2 %copy-start.2 = (bf16[3,256,2048]{2,1,0:T(8,128)(2,1)}, bf16[3,256,2048]{2,1,0:T(8,128)(2,1)S(1)}, u32[]{:S(2)}) copy-start(bf16[3,256,2048]{2,1,0:T(8,128)(2,1)S(1)} %get-tuple-element.86.ffg_ref) | copy-start | bytes 9437188
  612.7 16.2 %copy-start.3 = (bf16[4,256,512]{2,1,0:T(8,128)(2,1)}, bf16[4,256,512]{2,1,0:T(8,128)(2,1)S(1)}, u32[]{:S(2)}) copy-start(bf16[4,256,512]{2,1,0:T(8,128)(2,1)S(1)} %get-tuple-element.85.attg_ref) | copy-start | bytes 3145732
  628.3 0.6 copy-start.8
  628.9 30.4 %copy-start.1 = (s32[2,1024]{1,0:T(2,128)S(1)}, s32[2,1024]{1,0:T(2,128)}, u32[]{:S(2)}) copy-start(s32[2,1024]{1,0:T(2,128)} %param.19) | copy-start | bytes 24580

commit v5 on v4

--- a/solution.py
+++ b/solution.py
@@ -265,6 +265,26 @@
             + self.got[self.end(-1), rows].astype(F32)
         )
 
+    def free(self, credit):
+        at = self.at
+
+        def tell(k, peer):
+            pl.semaphore_signal(credit.at[k], inc=1, device_id=peer, device_id_type=MESH)
+
+        tell(0, at.core)
+        for k, way in ((1, 1), (2, -1)):
+
+            @pl.when(self.there(way, 1))
+            def _(k=k, way=way):
+                tell(k, at.z(way))
+
+        pl.semaphore_wait(credit.at[0], 1)
+        for k, way in ((1, 1), (2, -1)):
+
+            @pl.when(self.there(-way, 1))
+            def _(k=k):
+                pl.semaphore_wait(credit.at[k], 1)
+
     def finish(self):
         at = self.at
         for c in range(at.n_c):
@@ -372,149 +392,209 @@
 
 
 class Collect:
-    def __init__(self, at, partial, mine, by_x, by_y, pass_x, pass_y, part_x, part_y, send, recv, local):
-        self.at, self.partial, self.mine, self.by_x, self.by_y = at, partial, mine, by_x, by_y
-        self.pass_x, self.pass_y, self.part_x, self.part_y = pass_x, pass_y, part_x, part_y
-        self.send, self.recv, self.local = send, recv, local
+    def __init__(self, at, partial, stage, local, by_x, by_y, pass_x, pass_y, send, recv):
+        self.at, self.partial, self.stage, self.local = at, partial, stage, local
+        self.by_x, self.by_y, self.pass_x, self.pass_y = by_x, by_y, pass_x, pass_y
+        self.send, self.recv = send, recv
+        self.matrices = by_y.shape[0]
         self.height = partial.shape[2] // at.n_f // 2
 
-    def part(self, o, shift, half):
-        at = self.at
-        first = (at.fsdp(shift) * 2 + half) * self.height
-        return self.partial.at[at.other(o), :, pl.ds(first, self.height), :]
-
-    def half(self, ref, half):
-        return ref.at[:, pl.ds(half * self.height, self.height), :]
-
-    def copy(self, src, dst, k, peer):
+    def first(self, shift, half):
+        return (self.at.fsdp(shift) * 2 + half) * self.height
+
+    def part(self, o, shift, half, m):
+        rows = pl.ds(self.first(shift, half), self.height)
+        return self.partial.at[self.at.other(o), m, rows, :]
+
+    def half(self, ref, half, m):
+        return ref.at[m, pl.ds(half * self.height, self.height), :]
+
+    def copy(self, src, dst, k, m, peer):
+        k = k * self.matrices + m
         return remote(src, dst, self.send.at[k], self.recv.at[k], peer)
 
-    def raw(self):
+    def raw(self, group, m):
         at = self.at
         n, shifts = at.n_f, range(1, at.n_f)
+        if group == 0:
+            return [
+                self.copy(self.part(1, s, 0, m), self.pass_x.at[s - 1, m], s, m, at.xy(s, 0)) for s in shifts
+            ]
+        if group == 1:
+            return [
+                self.copy(self.part(1, s, 1, m), self.pass_y.at[s - 1, m], n + s, m, at.xy(0, 1))
+                for s in shifts
+            ]
         return [
-            [self.copy(self.part(1, s, 0), self.pass_x.at[s - 1], s, at.xy(s, 0)) for s in shifts],
-            [self.copy(self.part(1, s, 1), self.pass_y.at[s - 1], n + s, at.xy(0, 1)) for s in shifts],
-            [
-                *(
-                    self.copy(self.part(0, s, 0), self.half(self.by_x.at[s - 1], 0), 2 * n + s, at.xy(s, 0))
-                    for s in shifts
-                ),
-                self.copy(self.part(1, 0, 1), self.half(self.by_y, 1), 0, at.xy(0, 1)),
-            ],
-        ]
-
-    def added(self):
-        at = self.at
-        n, shifts = at.n_f, range(1, at.n_f)
-        return [
-            self.copy(self.part_y, self.half(self.by_y, 0), n, at.xy(0, 1)),
             *(
-                self.copy(self.part_x.at[s - 1], self.half(self.by_x.at[s - 1], 1), 3 * n + s, at.xy(s, 0))
+                self.copy(
+                    self.part(0, s, 0, m), self.half(self.by_x.at[s - 1], 0, m), 2 * n + s, m, at.xy(s, 0)
+                )
                 for s in shifts
             ),
+            self.copy(self.part(1, 0, 1, m), self.half(self.by_y, 1, m), 0, m, at.xy(0, 1)),
         ]
 
-    def keeps(self):
-        first = self.at.f * 2 * self.height
-        own = self.partial.at[self.at.hi, :, pl.ds(first, 2 * self.height), :]
-        return [
-            pltpu.make_async_copy(own, self.mine, self.local.at[0]),
-            pltpu.make_async_copy(self.part(1, 0, 0), self.part_y, self.local.at[1]),
-            *(
-                pltpu.make_async_copy(self.part(0, s, 1), self.part_x.at[s - 1], self.local.at[1 + s])
-                for s in range(1, self.at.n_f)
-            ),
+    def added(self, s, m):
+        at = self.at
+        if s == 0:
+            return self.copy(self.pass_x.at[0, m], self.half(self.by_y, 0, m), at.n_f, m, at.xy(0, 1))
+        target = self.half(self.by_x.at[s - 1], 1, m)
+        return self.copy(self.pass_y.at[s - 1, m], target, 3 * at.n_f + s, m, at.xy(s, 0))
+
+    def start(self, m):
+        for group in range(3):
+            for copy in self.raw(group, m):
+                copy.start()
+
+    def reader(self, o, shift, half):
+        at = self.at
+        if self.stage is None:
+            first = self.first(shift, half)
+            return lambda m, rows, start: self.partial[
+                at.other(o), m, pl.ds(pl.multiple_of(first + start, ROWS), ROWS)
+            ]
+        loads = [
+            pltpu.make_async_copy(
+                self.part(o, shift, half, m), self.stage(m), self.local.at[m]
+            )
+            for m in range(self.matrices)
         ]
+        for copy in loads:
+            copy.start()
+        for copy in loads:
+            copy.wait()
+        return lambda m, rows, start: self.stage(m)[rows]
+
+    def sweep(self, step, m):
+        @pl.loop(0, self.height // ROWS)
+        def _(i):
+            start = pl.multiple_of(i * ROWS, ROWS)
+            step(m, pl.ds(start, ROWS), start)
+
+    def forward(self):
+        n = self.at.n_f
+        own = self.reader(1, 0, 0)
+
+        def add_y(m, rows, start):
+            value = own(m, rows, start).astype(F32)
+            for s in range(n - 1):
+                value = value + self.pass_x[s, m, rows].astype(F32)
+            self.pass_x[0, m, rows] = value.astype(BF)
+
+        for m in range(self.matrices):
+            for copy in self.raw(0, m):
+                copy.wait_recv()
+            self.sweep(add_y, m)
+            self.added(0, m).start()
+        for s in range(1, n):
+            own_x = self.reader(0, s, 1)
+
+            def add_x(m, rows, start, s=s, own_x=own_x):
+                value = own_x(m, rows, start).astype(F32) + self.pass_y[s - 1, m, rows].astype(F32)
+                self.pass_y[s - 1, m, rows] = value.astype(BF)
+
+            for m in range(self.matrices):
+                self.raw(1, m)[s - 1].wait_recv()
+                self.sweep(add_x, m)
+                self.added(s, m).start()
+
+    def finish_sums(self, stage):
+        self.stage = stage
+        self.total()
+
+    def total(self):
+        n = self.at.n_f
+        for half in range(2):
+            own = self.reader(0, 0, half)
+
+            def add(m, rows, start, half=half, own=own):
+                here = pl.ds(pl.multiple_of(half * self.height + start, ROWS), ROWS)
+                value = own(m, rows, start).astype(F32) + self.by_y[m, here].astype(F32)
+                for s in range(n - 1):
+                    value = value + self.by_x[s, m, here].astype(F32)
+                self.by_y[m, here] = value.astype(BF)
+
+            for m in range(self.matrices):
+                if half == 0:
+                    for copy in self.raw(2, m):
+                        copy.wait_recv()
+                    for s in range(n):
+                        self.added(s, m).wait_recv()
+                self.sweep(add, m)
+
+    def finish(self):
+        for m in range(self.matrices):
+            for group in range(3):
+                for copy in self.raw(group, m):
+                    copy.wait_send()
+            for s in range(self.at.n_f):
+                self.added(s, m).wait_send()
+
+
+class Share:
+    def __init__(self, at, src, out, send, recv, local):
+        self.at, self.local = at, pltpu.make_async_copy(src, out.at[at.t], local)
+        across = at.t + 2 - 4 * at.hi
+        self.first = [
+            remote(src, out.at[at.t], send.at[0], recv.at[0], at.xy(0, 1)),
+            remote(src, out.at[at.t], send.at[1], recv.at[1], at.core),
+        ]
+        self.second = remote(out.at[across], out.at[across], send.at[2], recv.at[2], at.core)
 
     def start(self):
-        for copies in self.raw():
-            for copy in copies:
-                copy.start()
-        for copy in self.keeps():
+        for copy in (*self.first, self.local):
             copy.start()
 
     def forward(self):
-        raw, added, keeps = self.raw(), self.added(), self.keeps()
-        for copy in (*raw[0], keeps[1]):
-            copy.wait() if copy is keeps[1] else copy.wait_recv()
-        n = self.at.n_f
-        for m in range(self.mine.shape[0]):
-
-            def add_y(rows, m=m):
-                value = self.part_y[m, rows].astype(F32)
-                for s in range(n - 1):
-                    value = value + self.pass_x[s, m, rows].astype(F32)
-                self.part_y[m, rows] = value.astype(BF)
-
-            by_rows(self.height, add_y)
-        added[0].start()
-        for s in range(1, n):
-            raw[1][s - 1].wait_recv()
-            keeps[1 + s].wait()
-            for m in range(self.mine.shape[0]):
-
-                def add_x(rows, m=m, s=s):
-                    self.part_x[s - 1, m, rows] = (
-                        self.part_x[s - 1, m, rows].astype(F32) + self.pass_y[s - 1, m, rows].astype(F32)
-                    ).astype(BF)
-
-                by_rows(self.height, add_x)
-            added[s].start()
-
-    def total(self, out):
-        raw, added = self.raw(), self.added()
-        for copy in (*raw[2], *added):
-            copy.wait_recv()
-        self.keeps()[0].wait()
-        for m in range(self.mine.shape[0]):
-
-            def add(rows, m=m):
-                value = self.mine[m, rows].astype(F32) + self.by_y[m, rows].astype(F32)
-                for s in range(self.at.n_f - 1):
-                    value = value + self.by_x[s, m, rows].astype(F32)
-                out[m, rows] = value.astype(BF)
-
-            by_rows(2 * self.height, add)
+        self.first[0].wait_recv()
+        self.second.start()
 
     def finish(self):
-        for copies in (*self.raw(), self.added()):
-            for copy in copies:
-                copy.wait_send()
+        self.first[0].wait_send()
+        self.first[1].wait()
+        self.second.wait()
+        self.local.wait()
 
 
 def collect_scratch(n_f, matrices, height, columns):
     half = (matrices, height // 2, columns)
     return [
-        pltpu.VMEM((matrices, height, columns), BF),
         pltpu.VMEM((n_f - 1, matrices, height, columns), BF),
         pltpu.VMEM((matrices, height, columns), BF),
         pltpu.VMEM((n_f - 1, *half), BF),
         pltpu.VMEM((n_f - 1, *half), BF),
-        pltpu.VMEM((n_f - 1, *half), BF),
-        pltpu.VMEM(half, BF),
-        dma(4 * n_f),
-        dma(4 * n_f),
-        dma(n_f + 1),
+        dma(4 * n_f * matrices),
+        dma(4 * n_f * matrices),
     ]
 
 
 class Return:
     def __init__(self, at, summed, shard, send, recv, local):
-        rows, width = shard.shape[1], summed.shape[2]
-        target = shard.at[:, :, pl.ds(pl.multiple_of(at.c * width, 128), width)]
-
-        def part(c):
-            return summed.at[:, pl.ds(pl.multiple_of(c * rows, rows), rows), :]
-
-        self.local = pltpu.make_async_copy(part(at.c), target, local)
-        self.far = [
-            remote(part(at.ctx(s)), target, send.at[s], recv.at[s], at.z(s))
-            for s in range(1, at.n_c)
-        ]
-
-    start = Swap.start
-    wait = Swap.wait
+        rows, sheets = shard.shape[1], summed.shape[0]
+        beside = shard.shape[0] // sheets
+        width = summed.shape[2] // beside
+        self.local, self.far = [], []
+        for m in range(shard.shape[0]):
+            target = shard.at[m, :, pl.ds(pl.multiple_of(at.c * width, 128), width)]
+            first = m % beside * width
+
+            def part(c, m=m, first=first):
+                here = pl.ds(pl.multiple_of(c * rows, rows), rows)
+                return summed.at[m // beside, here, first : first + width]
+
+            self.local.append(pltpu.make_async_copy(part(at.c), target, local.at[m]))
+            for s in range(1, at.n_c):
+                k = m * at.n_c + s
+                self.far.append(remote(part(at.ctx(s)), target, send.at[k], recv.at[k], at.z(s)))
+
+    def start(self):
+        for copy in (*self.far, *self.local):
+            copy.start()
+
+    def wait(self):
+        for copy in (*self.far, *self.local):
+            copy.wait()
 
 
 def pack_weights(w, packed):
@@ -529,11 +609,11 @@
     return values * cos + pltpu.roll(values, HEAD_DIM // 2, 1) * sine
 
 
-def round_all(wide, low):
+def recast(wide, low):
     for m in range(wide.shape[0]):
 
         def step(rows, m=m):
-            low[m, rows] = wide[m, rows].astype(BF)
+            low[m, rows] = wide[m, rows].astype(low.dtype)
 
         by_rows(wide.shape[1], step)
 
@@ -604,13 +684,13 @@
         by_rows(half, norm_one)
         loads[1].wait()
         loads[2].wait()
-        round_all(att_wide, att_low)
+        recast(att_wide, att_low)
         at.greet([at.core, *at.all_z(), *at.all_xy()])
         gather.start()
         swap_att.start()
         for copy in loads[3:]:
             copy.wait()
-        round_all(ff_wide, ff_low)
+        recast(ff_wide, ff_low)
         gather.forward(range(1, 2))
         swap_att.wait()
         spread_att.start()
@@ -664,133 +744,206 @@
         scatter.finish()
         spread_ff.wait()
 
-    def third_kernel(
-        part_ref, branch_ref, mid_ref, cot_ref, grad_ref, rows_ref, block_ref, own_ref, sum_ref,
-        part, near, sent, got, ss, sr, part2, near2, sent2, got2, ss2, sr2, ls, low, s1, r1, l1, *collected,
+    def back_kernel(
+        a2_ref, cots_ref, joined_ref, d_a2_ref, branch_ref, mid_ref, tok_ref, cot_ref, a1_ref, attw_ref,
+        place, key_place, first, cos, sine, qkv, attended, mass,
+        input_ref, out_ref, attg_ref, ffg_ref, norm_ref, grad_ref, rows_ref,
+        rows_one, rows_two, wide, sheets, d_v, d_k, own, block, low, x_ref, own_cot, lk, lg, credit,
+        part, near, sent, got, ss, sr, g1, h1, l1, lf, s4, r4, l4, s5, r5, l5, s6, r6, l6,
+        total, got_t, got_c, got_f, s7, r7, *collected,
     ):
         at = Place(sizes)
-        loads = [
-            pltpu.make_async_copy(part_ref, part, ls.at[0]),
-            pltpu.make_async_copy(branch_ref, part2, ls.at[1]),
-        ]
-        for copy in loads:
-            copy.start()
-        at.greet([at.core, *at.all_z(), *at.all_xy()])
+        half = own.shape[0]
+        length, tall = rows_one.shape[0], wide.shape[1]
+        mine = pl.ds(pl.multiple_of(at.lo * half, half), half)
+
+        def load(*pairs):
+            copies = [pltpu.make_async_copy(src, dst, lk.at[i]) for i, (src, dst) in enumerate(pairs)]
+            for copy in copies:
+                copy.start()
+            for copy in copies:
+                copy.wait()
+
+        def in_blocks(src, dst):
+            return [(src.at[b], dst.at[pl.ds(b * half, half)]) for b in range(2 * n_c)]
+
         scatter = Scatter(at, part, near, sent, got, ss, sr)
-        branch = Scatter(at, part2, near2, sent2, got2, ss2, sr2)
-        for copy in loads:
-            copy.wait()
-        collect = Collect(at, grad_ref, *collected)
+        gather = Gather(at, low, rows_ref, g1, h1, l1)
+        columns = sheets.shape[3]
+        high = tall // n_f // 2
+        collect_ff = Collect(
+            at, grad_ref, lambda m: sheets.at[0, 0, pl.ds(m * high, high)], lf, *collected[:6]
+        )
+        collect_att = Collect(at, sheets, None, None, *collected[6:])
+        give_ff = Return(at, collected[1], ffg_ref, s5, r5, l5)
+        give_att = Return(at, collected[7], attg_ref, s4, r4, l4)
+        tps = [(at.f, at.c, lax.rem(at.t + s, n_t)) for s in range(1, n_t)]
+        fs = [at.xy(s, 0) for s in range(1, n_f)]
+        load((d_a2_ref, part))
+        at.greet([*tps, *at.all_z(), *fs])
         scatter.start()
-        collect.start()
-        scatter.pass_on()
-        branch.start()
+        load(
+            (a2_ref, rows_one),
+            (cots_ref, rows_two),
+            (joined_ref.at[0], wide.at[0, pl.ds(0, length)]),
+            (joined_ref.at[1], wide.at[0, pl.ds(length, length)]),
+            (joined_ref.at[2], wide.at[1, pl.ds(0, length)]),
+            (tok_ref.at[at.hi, mine], x_ref),
+            (cot_ref.at[at.hi, mine], own_cot),
+        )
+
+        def keep(k):
+            y, m = k % 2, k // 2
+            return pltpu.make_async_copy(sheets.at[y, 0], grad_ref.at[y, m], lg.at[y])
+
+        for k in range(6):
+            y, m = k % 2, k // 2
+            if k >= 2 and y == 0:
+                keep(k - 2).wait()
+                keep(k - 1).wait()
+            rows = rows_two if m == 2 else rows_one
+            slot, start = ((0, 0), (0, length), (1, 0))[m]
+
+            @pl.loop(0, 2)
+            def _(i, y=y, rows=rows, slot=slot, start=start):
+                cols = pl.ds(pl.multiple_of(i * (tall // 2), tall // 2), tall // 2)
+                side = wide[slot, start : start + length, y * columns : (y + 1) * columns]
+                sheets[y, 0, cols] = dot(rows[:, cols], side, ((0,), (0,))).astype(BF)
+
+            keep(k).start()
+            if y == 0 and m > 0:
+                collect_ff.start(m - 1)
+            if k in (0, 3, 5):
+                hop = {0: n_c - 1, 3: n_c - 2, 5: n_c - 3}[k]
+                scatter.pass_on(range(hop, hop + 1))
+        keep(4).wait()
+        keep(5).wait()
+        collect_ff.start(2)
         scatter.arrive()
 
-        def norm(rows):
+        def norm_two(rows):
             normed, scale = mean_spread(mid_ref[rows])
-            grad = cot_ref[rows].astype(F32) + norm_back(scatter.total(rows), normed, scale)
-            own_ref[rows] = grad
+            grad = own_cot[rows].astype(F32) + norm_back(scatter.total(rows), normed, scale)
+            own[rows] = grad
             low[rows] = grad.astype(BF)
 
-        by_rows(mid_ref.shape[0], norm)
-        gather = Gather(at, low, rows_ref, s1, r1, l1)
+        by_rows(half, norm_two)
         gather.start()
-        branch.pass_on()
-        gather.forward(range(1, 2))
-        collect.forward()
-        gather.forward(range(2, n_c))
-        branch.arrive()
+        scatter.finish()
+        scatter.free(credit.at[0])
+        load((branch_ref, part))
+        gather.forward(range(1, n_c - 1))
+        scatter.start()
+        collect_ff.forward()
+        gather.forward(range(n_c - 1, n_c))
+        heads = attw_ref.shape[0]
+        load(
+            *in_blocks(a1_ref, rows_two),
+            *(
+                (attw_ref.at[y, i], wide.at[0, :, pl.ds((i * heads + y) * HEAD_DIM, HEAD_DIM)])
+                for i in range(4)
+                for y in range(heads)
+            ),
+        )
+        scatter.pass_on(range(n_c - 1, n_c - 2, -1))
+        gather.finish()
+        load(*in_blocks(rows_ref, rows_one))
+        packed, joint = wide.at[0], wide.at[1, pl.ds(length, length)]
+        wide_heads = heads * HEAD_DIM
+        joint[:, :wide_heads] = dot(rows_one[...], packed[:, 3 * wide_heads :], ((1,), (0,))).astype(BF)
+        for y in range(heads):
+            attend_back(y, packed, joint, place, key_place, first, cos, sine, qkv, mass, d_v, d_k, heads)
+            if y == 0:
+                scatter.pass_on(range(n_c - 2, 1, -1))
+        scatter.pass_on(range(1, 2))
+        scatter.arrive()
 
         def add(rows):
-            block_ref[rows] = (mid_ref[rows] + branch.total(rows)).astype(BF)
-
-        by_rows(mid_ref.shape[0], add)
-        gather.finish()
+            block[rows] = (mid_ref[rows] + scatter.total(rows)).astype(BF)
+
+        by_rows(half, add)
         scatter.finish()
-        branch.finish()
-        collect.total(sum_ref)
-        collect.finish()
-
-    def fourth_kernel(
-        part_ref, x_ref, mid_ref, block_ref, att_ref, ff_ref, input_ref, out_ref, attg_ref, ffg_ref,
-        part, near, sent, got, ss, sr, total, low, s1, r1, l1, s2, r2, l2, s4, r4, l4, *collected,
-    ):
-        at = Place(sizes)
-        load = pltpu.make_async_copy(part_ref, part, l4.at[2])
-        load.start()
-        tps = [(at.f, at.c, lax.rem(at.t + s, n_t)) for s in range(1, n_t)]
-        at.greet([*tps, *at.all_z(), *[at.xy(s, o) for s, o in at.pairs if s]])
-        load.wait()
-        scatter = Scatter(at, part, near, sent, got, ss, sr)
-        collect = Collect(at, att_ref, *collected)
-        give_ff = Return(at, ff_ref, ffg_ref, s2, r2, l2)
+        scatter.free(credit.at[1])
+        width = part.shape[2] // 4
+
+        @pl.loop(0, 4)
+        def _(c):
+            cols = pl.ds(pl.multiple_of(c * width, width), width)
+            value = dot(joint[:, : 3 * wide_heads], packed[cols, : 3 * wide_heads], ((1,), (1,))).astype(BF)
+            part[:, :, cols] = value.reshape(part.shape[0], part.shape[1], width)
+
         scatter.start()
-        collect.start()
-
-        def tp_gather(src, dst, k):
-            copies = [
-                remote(src, dst.at[at.t], s4.at[k, i], r4.at[k, i], peer) for i, peer in enumerate(tps)
-            ]
-            keep = pltpu.make_async_copy(src, dst.at[at.t], l4.at[k])
-            for copy in (*copies, keep):
-                copy.start()
-            return [*copies, keep]
-
-        scatter.pass_on()
+
+        @pl.loop(0, 2)
+        def _(c):
+            cols = pl.ds(pl.multiple_of(c * 2 * width, width), 2 * width)
+            for i in range(4):
+                if i < 3:
+                    value = dot(
+                        rows_two[:, cols], joint[:, i * wide_heads : (i + 1) * wide_heads], ((0,), (0,))
+                    )
+                else:
+                    value = dot(rows_one[:, cols], attended[...], ((0,), (0,)))
+                for y in range(heads):
+                    sheets[y, 0, cols, i * HEAD_DIM : (i + 1) * HEAD_DIM] = value[
+                        :, y * HEAD_DIM : (y + 1) * HEAD_DIM
+                    ].astype(BF)
+
+        collect_att.start(0)
+        scatter.pass_on(range(n_c - 1, n_c - 2, -1))
+        share_block = Share(at, block, out_ref, s6.at[0], r6.at[0], l6.at[0])
+        share_input = Share(at, low, input_ref, s6.at[1], r6.at[1], l6.at[1])
+        share_block.start()
+        collect_ff.finish_sums(lambda m: rows_one.at[pl.ds(0, high), pl.ds(m * columns, columns)])
         give_ff.start()
-        collect.forward()
-        waits = tp_gather(block_ref, out_ref, 0)
-        collect.total(total)
-        give_att = Return(at, total, attg_ref, s1, r1, l1)
+        collect_att.forward()
+        scatter.pass_on(range(n_c - 2, 0, -1))
+        share_block.forward()
+        collect_att.total()
         give_att.start()
         scatter.arrive()
 
-        def norm(rows):
+        def norm_one(rows):
             normed, scale = mean_spread(x_ref[rows].astype(F32))
-            low[rows] = mid_ref[rows] + norm_back(scatter.total(rows), normed, scale)
-
-        by_rows(mid_ref.shape[0], norm)
-        waits += tp_gather(low, input_ref, 1)
-        for copy in waits:
-            copy.wait()
+            low[rows] = (own[rows] + norm_back(scatter.total(rows), normed, scale)).astype(BF)
+
+        by_rows(half, norm_one)
+        share_input.start()
         scatter.finish()
-        collect.finish()
+        collect_ff.finish()
+        collect_att.finish()
+        share_input.forward()
+        give_ff.wait()
         give_att.wait()
-        give_ff.wait()
-
-    def norm_kernel(attg_ref, ffg_ref, norm_ref, low_att, low_ff, total, got_t, got_c, got_f, send, recv, ls):
-        at = Place(sizes)
-        loads = [
-            pltpu.make_async_copy(attg_ref, low_att, ls.at[0]),
-            pltpu.make_async_copy(ffg_ref, low_ff, ls.at[1]),
+        own_rows, own_cols = ffg_ref.shape[1], attg_ref.shape[2]
+        ff_low = [rows_one.at[pl.ds(m * own_rows, own_rows)] for m in range(3)]
+        att_low = [
+            rows_two.at[pl.ds(0, own_rows), pl.ds(m * own_cols, own_cols)] for m in range(4)
         ]
-        for copy in loads:
-            copy.start()
-        tps = [(at.f, at.c, lax.rem(at.t + s, n_t)) for s in range(1, n_t)]
-        fs = [at.xy(s, 0) for s in range(1, n_f)]
-        at.greet([*tps, *at.all_z(), *fs])
-        for copy in loads:
-            copy.wait()
-        sum_norm(at, (low_att, low_ff), norm_ref, total, got_t, got_c, got_f, send, recv)
+        load(
+            *((ffg_ref.at[m], ff_low[m]) for m in range(3)),
+            *((attg_ref.at[m], att_low[m]) for m in range(4)),
+        )
+        sum_norm(at, (*ff_low, *att_low), norm_ref, total, got_t, got_c, got_f, s7, r7)
+        share_block.finish()
+        share_input.finish()
 
     def sum_norm(at, grads, norm_ref, total, got_t, got_c, got_f, send, recv):
         tps = [(at.f, at.c, lax.rem(at.t + s, n_t)) for s in range(1, n_t)]
         fs = [at.xy(s, 0) for s in range(1, n_f)]
         total[0] = jnp.zeros(total.shape[1:], F32)
         for low in grads:
-            for m in range(low.shape[0]):
-
-                def square(rows, low=low, m=m):
-                    value = low[m, rows].astype(F32)
-                    value = value * value
-                    value = value[: ROWS // 2] + value[ROWS // 2 :]
-                    lanes = value[:, :128]
-                    for c in range(1, value.shape[1] // 128):
-                        lanes = lanes + value[:, c * 128 : (c + 1) * 128]
-                    total[0] += lanes
-
-                by_rows(low.shape[1], square)
+
+            def square(rows, low=low):
+                value = low[rows].astype(F32)
+                value = value * value
+                value = value[: ROWS // 2] + value[ROWS // 2 :]
+                lanes = value[:, :128]
+                for c in range(1, value.shape[1] // 128):
+                    lanes = lanes + value[:, c * 128 : (c + 1) * 128]
+                total[0] += lanes
+
+            by_rows(low.shape[0], square)
         base = 0
         stages = ((tps, got_t, at.t), (at.all_z(), got_c, at.c), (fs, got_f, at.f))
         for stage, (peers, got, place) in enumerate(stages):
@@ -813,7 +966,7 @@
 
     def finish_kernel(norm_ref, block_in, input_in, attg_ref, ffg_ref, *refs):
         olds, outs, scratch = refs[:12], refs[12:34], refs[34:]
-        low_att, low_ff, wide_att, wide_ff, old_att, old_ff, block_keep, input_keep, ls = scratch
+        low_att, low_ff, wide_att, wide_ff, old_att, old_ff, block_keep, input_low, input_keep, ls = scratch
         groups = (
             (attg_ref, low_att, wide_att, old_att, 0, attg_ref.shape[1]),
             (ffg_ref, low_ff, wide_ff, old_ff, 2, attg_ref.shape[1] // 4),
@@ -842,10 +995,10 @@
             for copy in one:
                 copy.start()
             loads.append(one)
-        kept = ((block_in, block_keep, outs[20]), (input_in, input_keep, outs[21]))
+        kept = ((block_in, block_keep, block_keep, outs[20]), (input_in, input_low, input_keep, outs[21]))
         through = []
-        for i, (src, keep, out) in enumerate(kept):
-            copy = pltpu.make_async_copy(src, keep, ls.at[len(chunks), 0, i])
+        for i, (src, first, keep, out) in enumerate(kept):
+            copy = pltpu.make_async_copy(src, first, ls.at[len(chunks), 0, i])
             copy.start()
             through.append((copy, pltpu.make_async_copy(keep, out, ls.at[len(chunks), 1, i])))
         norm = norm_ref[0:1, 0:1]
@@ -881,6 +1034,8 @@
                 stores.append(store)
         for load, store in through:
             load.wait()
+            if load is through[1][0]:
+                recast(input_low, input_keep)
             store.start()
             stores.append(store)
         for store in stores:
@@ -921,66 +1076,44 @@
             value = dot(attended[...], packed[cols, 3 * wide :], ((1,), (1,))).astype(BF)
             part[:, :, cols] = value.reshape(part.shape[0], part.shape[1], width)
 
-    def backward_kernel(
-        mid, a1, w, place, key_place, first, cos, sine, qkv, attended, mass, part, grad, packed, joint, d_v, d_k
-    ):
-        heads = w.shape[0]
+    def attend_back(y, packed, joint, place, key_place, first, cos, sine, qkv, mass, d_v, d_k, heads):
         wide = heads * HEAD_DIM
-        pack_weights(w, packed)
-        joint[:, :wide] = dot(mid[...], packed[:, 3 * wide :], ((1,), (0,))).astype(BF)
-        for y in range(heads):
-            cols = slice(y * HEAD_DIM, (y + 1) * HEAD_DIM)
-
-            @pl.loop(0, a1.shape[0] // QUERIES)
-            def _(c, y=y, cols=cols):
-                rows = pl.ds(pl.multiple_of(c * QUERIES, QUERIES), QUERIES)
-                query, key, value = qkv[0, rows, cols], qkv[1, :, cols], qkv[2, :, cols]
-                d_att = joint[rows, cols]
-                scores = dot(query, key, ((1,), (1,))) * SCORE_SCALE
-                allowed = (key_place[...] <= place[rows]) & (key_place[...] >= first[rows])
-                probs = jnp.exp(jnp.where(allowed, scores, NEG_FILL) - mass[rows, y : y + 1])
-                d_prob = dot(d_att, value, ((1,), (1,)))
-                delta = jnp.sum(probs * d_prob, axis=1, keepdims=True)
-                d_score = (probs * (d_prob - delta)).astype(BF)
-                v_part = dot(probs.astype(BF), d_att, ((0,), (0,)))
-                k_part = dot(d_score, query, ((0,), (0,)))
-
-                @pl.when(c == 0)
-                def _():
-                    d_v[...] = v_part
-                    d_k[...] = k_part
-
-                @pl.when(c > 0)
-                def _():
-                    d_v[...] += v_part
-                    d_k[...] += k_part
-
-                d_query = dot(d_score, key, ((1,), (0,))) * SCORE_SCALE
-                joint[rows, cols] = turn(d_query, cos[rows], -sine[rows]).astype(BF)
-
-            joint[:, wide + y * HEAD_DIM : wide + (y + 1) * HEAD_DIM] = turn(
-                d_k[...] * SCORE_SCALE, cos[...], -sine[...]
-            ).astype(BF)
-            joint[:, 2 * wide + y * HEAD_DIM : 2 * wide + (y + 1) * HEAD_DIM] = d_v[...].astype(BF)
-        width = part.shape[1] // 4
-
-        @pl.loop(0, 4)
+        cols = slice(y * HEAD_DIM, (y + 1) * HEAD_DIM)
+
+        @pl.loop(0, qkv.shape[1] // QUERIES)
         def _(c):
-            cols = pl.ds(pl.multiple_of(c * width, width), width)
-            part[:, cols] = dot(joint[...], packed[cols, : 3 * wide], ((1,), (1,))).astype(BF)
-
-        @pl.loop(0, 2)
-        def _(c):
-            cols = pl.ds(pl.multiple_of(c * 2 * width, width), 2 * width)
-            for i in range(4):
-                if i < 3:
-                    value = dot(a1[:, cols], joint[:, i * wide : (i + 1) * wide], ((0,), (0,)))
-                else:
-                    value = dot(mid[:, cols], attended[...], ((0,), (0,)))
-                for y in range(heads):
-                    grad[y, i, cols] = value[:, y * HEAD_DIM : (y + 1) * HEAD_DIM].astype(BF)
-
-    def hidden_kernel(a2, cot, w, d_a2, branch, grad, hidden, d_up, d_gate, kept):
+            rows = pl.ds(pl.multiple_of(c * QUERIES, QUERIES), QUERIES)
+            query, key, value = qkv[0, rows, cols], qkv[1, :, cols], qkv[2, :, cols]
+            d_att = joint[rows, cols]
+            scores = dot(query, key, ((1,), (1,))) * SCORE_SCALE
+            allowed = (key_place[...] <= place[rows]) & (key_place[...] >= first[rows])
+            probs = jnp.exp(jnp.where(allowed, scores, NEG_FILL) - mass[rows, y : y + 1])
+            d_prob = dot(d_att, value, ((1,), (1,)))
+            delta = jnp.sum(probs * d_prob, axis=1, keepdims=True)
+            d_score = (probs * (d_prob - delta)).astype(BF)
+            v_part = dot(probs.astype(BF), d_att, ((0,), (0,)))
+            k_part = dot(d_score, query, ((0,), (0,)))
+
+            @pl.when(c == 0)
+            def _():
+                d_v[...] = v_part
+                d_k[...] = k_part
+
+            @pl.when(c > 0)
+            def _():
+                d_v[...] += v_part
+                d_k[...] += k_part
+
+            d_query = dot(d_score, key, ((1,), (0,))) * SCORE_SCALE
+            joint[rows, cols] = turn(d_query, cos[rows], -sine[rows]).astype(BF)
+
+        joint[:, wide + y * HEAD_DIM : wide + (y + 1) * HEAD_DIM] = turn(
+            d_k[...] * SCORE_SCALE, cos[...], -sine[...]
+        ).astype(BF)
+        joint[:, 2 * wide + y * HEAD_DIM : 2 * wide + (y + 1) * HEAD_DIM] = d_v[...].astype(BF)
+
+    def hidden_kernel(a2, cot, w, d_a2, branch, joined, kept):
+        d_up, d_gate, hidden = joined.at[0], joined.at[1], joined.at[2]
         step, steps = pl.program_id(0), pl.num_programs(0)
         tile = w.shape[3]
         here = pl.ds(pl.multiple_of(step * tile, tile), tile)
@@ -1001,9 +1134,6 @@
 
         for m in range(3):
             kept[m, :, here] = w[0, m]
-        grad[0, 0] = dot(a2[...], d_up[:, here], ((0,), (0,))).astype(BF)
-        grad[0, 1] = dot(a2[...], d_gate[:, here], ((0,), (0,))).astype(BF)
-        grad[0, 2] = dot(cot[...], hidden[:, here], ((0,), (0,))).astype(BF)
 
         @pl.when(step == steps - 1)
         def _():
@@ -1042,14 +1172,7 @@
         blocks = n_c * 2
         rows_bf = jax.ShapeDtypeStruct((blocks, half, width), BF)
         own_f32 = jax.ShapeDtypeStruct((half, width), F32)
-        own_bf = jax.ShapeDtypeStruct((half, width), BF)
-
-        def own_rows(array):
-            rows = array.reshape(packs * 2, half, width)
-            return lax.dynamic_index_in_dim(rows, t_at, 0, keepdims=False)
-
-        own_tokens = own_rows(tokens)
-        own_cot = own_rows(cotangent)
+
         att_cols, ff_cols = att_proj.shape[2] // n_c, ff_proj.shape[2] // n_c
         att_shape, ff_shape = (4, *att_proj.shape[1:]), (3, *ff_proj.shape[1:])
         att_full = jax.ShapeDtypeStruct((2, 4, width, att_cols), BF)
@@ -1111,7 +1234,6 @@
             + [dma(5 * n_f)] * 4,
             vmem=56,
         )(tokens, cotangent, *tables, att_proj, attn_out, ff_proj, ff_out)
-        act_one = act_one.reshape(pack_len, width)
         act_two = act_two.reshape(pack_len, width)
         cot_rows = cot_rows.reshape(pack_len, width)
 
@@ -1120,95 +1242,74 @@
         kept = pl.BlockSpec((pack_len, width), lambda i: (0, 0), pipeline_mode=pl.Buffered(1))
         moved = pl.BlockSpec((1, 3, width, tile), lambda i: (i // tiles, 0, 0, i % tiles))
         rows_flat = jax.ShapeDtypeStruct((pack_len, width), BF)
-        act_two_part, branch_part, ff_grad = pl.pallas_call(
+        act_two_part, branch_part, joined = pl.pallas_call(
             hidden_kernel,
             grid=(2 * tiles,),
-            out_shape=(rows_flat, rows_flat, jax.ShapeDtypeStruct(ff_w.shape, BF)),
+            out_shape=(rows_flat, rows_flat, jax.ShapeDtypeStruct((3, pack_len, 2 * ff_cols), BF)),
             in_specs=[kept, kept, moved],
-            out_specs=(kept, kept, moved),
-            scratch_shapes=[pltpu.VMEM((pack_len, 2 * ff_cols), BF)] * 3
-            + [pltpu.VMEM((3, width, 2 * ff_cols), BF)],
+            out_specs=(
+                kept,
+                kept,
+                pl.BlockSpec((3, pack_len, 2 * ff_cols), lambda i: (0, 0, 0), pipeline_mode=pl.Buffered(1)),
+            ),
+            scratch_shapes=[pltpu.VMEM((3, width, 2 * ff_cols), BF)],
             compiler_params=pltpu.CompilerParams(vmem_limit_bytes=60 << 20),
             name="hidden",
         )(act_two, cot_rows, ff_w)
         height = width // n_f
-        mid_rows, block_own, mid_grad, ff_sum = call(
-            third_kernel,
-            "third",
-            2,
-            (rows_bf, own_bf, own_f32, jax.ShapeDtypeStruct((3, height, ff_cols), BF)),
-            [ANY, ANY, VMEM, VMEM, ANY],
-            (ANY, VMEM, VMEM, VMEM),
-            scatter_scratch(n_c, half, width) * 2
-            + [dma(2), pltpu.VMEM((half, width), BF)]
-            + gather_sems(n_c)
-            + collect_scratch(n_f, 3, height, ff_cols),
-            vmem=56,
-        )(
-            act_two_part.reshape(rows_bf.shape),
-            branch_part.reshape(rows_bf.shape),
-            resid_mid,
-            own_cot,
-            ff_grad,
-        )
-        mid_rows = mid_rows.reshape(pack_len, width)
-
-        act_one_part, att_grad = local(
-            backward_kernel,
-            "backward",
-            (rows_flat, jax.ShapeDtypeStruct(att_w.shape, BF)),
-            [
-                pltpu.VMEM((width, 4 * rank_width), BF),
-                pltpu.VMEM((pack_len, 3 * rank_width), BF),
-                pltpu.VMEM((pack_len, HEAD_DIM), F32),
-                pltpu.VMEM((pack_len, HEAD_DIM), F32),
-            ],
-        )(mid_rows, act_one, att_w, *tables, qkv, attended, mass)
-        input_grad, block_out, att_total, ff_total = call(
-            fourth_kernel,
-            "fourth",
-            3,
+        count = n_f + n_c + n_t
+        input_grad, block_out, att_total, ff_total, norm_value, *_ = call(
+            back_kernel,
+            "back",
+            1,
             (
-                jax.ShapeDtypeStruct((n_t, half, width), F32),
+                jax.ShapeDtypeStruct((n_t, half, width), BF),
                 jax.ShapeDtypeStruct((n_t, half, width), BF),
                 jax.ShapeDtypeStruct(att_shape, BF),
                 jax.ShapeDtypeStruct(ff_shape, BF),
+                jax.ShapeDtypeStruct((8, 128), F32),
+                ff_full,
+                rows_bf,
             ),
-            [ANY, VMEM, VMEM, ANY, ANY, ANY],
-            (ANY,) * 4,
-            scatter_scratch(n_c, half, width)
-            + [pltpu.VMEM((4, height, att_cols), BF), pltpu.VMEM((half, width), F32)]
-            + [dma(n_c), dma(n_c), pltpu.SemaphoreType.DMA] * 2
+            [ANY] * 5 + [VMEM] + [ANY] * 4 + [VMEM] * 8,
+            (ANY,) * 4 + (VMEM,) + (ANY,) * 2,
+            [
+                pltpu.VMEM((pack_len, width), BF),
+                pltpu.VMEM((pack_len, width), BF),
+                pltpu.VMEM((2, width, 4 * rank_width), BF),
+                pltpu.VMEM((2, 1, width, 4 * att_cols), BF),
+                pltpu.VMEM((pack_len, HEAD_DIM), F32),
+                pltpu.VMEM((pack_len, HEAD_DIM), F32),
+                pltpu.VMEM((half, width), F32),
+                pltpu.VMEM((half, width), BF),
+                pltpu.VMEM((half, width), BF),
+                pltpu.VMEM((half, width), BF),
+                pltpu.VMEM((half, width), BF),
+                dma(2 * n_c + 8),
+                dma(2),
+                pltpu.SemaphoreType.REGULAR((2, 3)),
+            ]
+            + scatter_scratch(n_c, half, width)
+            + gather_sems(n_c)
+            + [dma(3)]
+            + [dma(4 * n_c), dma(4 * n_c), dma(4), dma(3 * n_c), dma(3 * n_c), dma(3)]
             + [
-                pltpu.SemaphoreType.DMA((2, n_t - 1)),
-                pltpu.SemaphoreType.DMA((2, n_t - 1)),
-                dma(3),
+                pltpu.SemaphoreType.DMA((2, 3)),
+                pltpu.SemaphoreType.DMA((2, 3)),
+                dma(2),
             ]
-            + collect_scratch(n_f, 4, height, att_cols),
+            + [pltpu.VMEM((k, 8, 128), F32) for k in (4, n_t, n_c, n_f)]
+            + [dma(count), dma(count)]
+            + collect_scratch(n_f, 3, height, ff_cols)
+            + collect_scratch(n_f, 1, height, 4 * att_cols),
+            vmem=62,
         )(
-            act_one_part.reshape(rows_bf.shape),
-            own_tokens,
-            mid_grad,
-            block_own,
-            att_grad,
-            ff_sum,
+            act_two, cot_rows, joined, act_two_part.reshape(rows_bf.shape), branch_part.reshape(rows_bf.shape),
+            resid_mid, tokens, cotangent, act_one, att_w, *tables, qkv, attended, mass,
         )
         weights = (att_proj, attn_out, ff_proj, ff_out)
         firsts_old = (att_proj_first, attn_out_first, ff_proj_first, ff_out_first)
         seconds_old = (att_proj_second, attn_out_second, ff_proj_second, ff_out_second)
-        count = n_f + n_c + n_t
-        norm_value = call(
-            norm_kernel,
-            "norm",
-            4,
-            jax.ShapeDtypeStruct((8, 128), F32),
-            [ANY] * 2,
-            VMEM,
-            [pltpu.VMEM(att_shape, BF), pltpu.VMEM(ff_shape, BF)]
-            + [pltpu.VMEM((k, 8, 128), F32) for k in (4, n_t, n_c, n_f)]
-            + [dma(count), dma(count), dma(2)],
-            vmem=16,
-        )(att_total, ff_total)
         results = pl.pallas_call(
             finish_kernel,
             out_shape=(
@@ -1227,6 +1328,7 @@
                 pltpu.VMEM((3, *att_shape), F32),
                 pltpu.VMEM((3, *ff_shape), F32),
                 pltpu.VMEM(block_out.shape, BF),
+                pltpu.VMEM(input_grad.shape, BF),
                 pltpu.VMEM(input_grad.shape, F32),
                 pltpu.SemaphoreType.DMA((17, 2, 5)),
             ],

time: 660 us -> 624 us (0.945)
  Pallas kernels: 644 us -> 614 us
    pallas_call x4 -> x1, Pallas kernels: 299 us -> 284 us  [shards(): call(back_kernel, 'back', 1, (jax.ShapeDtypeStruct((n_t, half, width), BF...]
    pallas_call x1, Pallas kernels: 55.1 us -> 41.3 us  [shards(): pl.pallas_call(hidden_kernel, grid=(2 * tiles,), out_shape=(rows_flat, ro...]
where the time goes in v5:
time: 624 us; the launch traced here: 623 us
  Pallas kernels  614 us (98%)
    pallas_call x1, Pallas kernels, shards(): call(back_kernel, 'back', 1, (jax.ShapeDtypeStruct((n_t, half, width), BF...  284 us
    pallas_call x1, Pallas kernels, shards(): call(front_kernel, 'front', 0, (rows_bf, att_full, ff_full, rows_bf, rows...  260 us
    pallas_call x1, Pallas kernels, shards(): pl.pallas_call(hidden_kernel, grid=(2 * tiles,), out_shape=(rows_flat, ro...  41.3 us
    pallas_call x1, Pallas kernels, shards(): pl.pallas_call(finish_kernel, out_shape=(*(jax.ShapeDtypeStruct(w.shape,...  28.6 us

profile of v5, /device:TPU:0, one launch (start us, length us, event | category | flops | bytes accessed | tf_op | source)
XLA Modules:
  0.0 623.5 jit_solution(11927412081608931363)
XLA Ops:
  0.7 0.0 copy-start
  0.7 0.7 fusion.4
  1.4 0.1 fusion.2
  1.5 0.7 fusion.3
  2.2 0.0 copy-done
  2.2 0.0 copy-start.2
  2.2 0.1 fusion.1
  2.4 1.0 copy.43.place
  3.4 1.0 copy.44.first
  4.4 1.9 fusion
  6.3 1.3 pad_maximum_fusion
  7.6 0.0 copy-done.2
  7.6 260.2 %front.1 = (bf16[8,128,2048]{2,1,0:T(8,128)(2,1)}, bf16[2,4,2048,128]{3,2,1,0:T(8,128)(2,1)}, bf16[2,3,2048,512]{3,2,1,0:T(8,128)(2,1)}, bf16[8,128,2048]{2,1,0:...) custom-call(bf16[2,256,2048]{2,1,0:T(8,128)(2,1)} %tok_ref.3, ...), custom_call_target="tpu_custom_call" | custom-call | tf_op jit(solution)/shard_map/front/pallas_call | solution.py:1201
  267.8 41.3 %hidden.1 = (bf16[1024,2048]{1,0:T(8,128)(2,1)}, bf16[1024,2048]{1,0:T(8,128)(2,1)}, bf16[3,1024,1024]{2,1,0:T(8,128)(2,1)}) custom-call(bf16[1024,2048]{1,0:T(8,128)(2,1)} %bitcast.19, bf16[1024,2048]{1,0:T(8,128)(2,1)} %bitcast.21, bf16[2,3,2048,512]{3,2,1,0:T(8,128)(2,1)} %get-tuple-element.64.w), custom_call_target="tpu_custom_call" | custom-call | tf_op jit(solution)/shard_map/hidden/pallas_call | solution.py:1245
  309.1 284.3 %back.1 = (bf16[4,128,2048]{2,1,0:T(8,128)(2,1)}, bf16[4,128,2048]{2,1,0:T(8,128)(2,1)}, bf16[4,256,512]{2,1,0:T(8,128)(2,1)}, bf16[3,256,2048]{2,1,0:T(8,128)(2...) custom-call(bf16[1024,2048]{1,0:T(8,128)(2,1)} %bitcast.20, ...), custom_call_target="tpu_custom_call" | custom-call | tf_op jit(solution)/shard_map/back/pallas_call | solution.py:1261
  593.5 1.2 slice.3
  594.7 0.0 copy-start.1
  594.7 28.6 %finish.1 = (f32[3,256,512]{2,1,0:T(8,128)}, f32[256,512]{1,0:T(8,128)}, f32[2,256,2048]{2,1,0:T(8,128)}, f32[256,2048]{1,0:T(8,128)}, f32[3,256,512]{2,1,0:T(8,...) custom-call(f32[8,128]{1,0:T(8,128)} %get-tuple-element.74.norm_ref,, ...), custom_call_target="tpu_custom_call" | custom-call | tf_op jit(solution)/shard_map/finish/pallas_call | solution.py:1313
  623.3 0.0 copy-done.1
  (4 shorter events, 0.0 us)
Async XLA Ops:
  0.7 1.5 copy-start
  2.2 5.4 copy-start.2
  594.7 28.6 %copy-start.1 = (s32[2,1024]{1,0:T(2,128)S(1)}, s32[2,1024]{1,0:T(2,128)}, u32[]{:S(2)}) copy-start(s32[2,1024]{1,0:T(2,128)} %param.19) | copy-start | bytes 24580

commit v6 on v5

--- a/solution.py
+++ b/solution.py
@@ -22,6 +22,7 @@
 ANY = pl.BlockSpec(memory_space=pl.ANY)
 VMEM = pl.BlockSpec(memory_space=pltpu.VMEM)
 ROWS = 16
+STEP_ROWS = 32
 QUERIES = 256
 SCORE_SCALE = HEAD_DIM ** (-0.5)
 
@@ -329,71 +330,71 @@
         for copy in self.far:
             copy.start()
 
-    def wait(self):
-        self.local.wait()
+    def arrived(self, s):
+        if s == 0:
+            self.local.wait()
+        else:
+            self.far[s - 1].wait_recv()
+        return self.at.ctx(-s)
+
+    def finish(self):
         for copy in self.far:
-            copy.wait()
+            copy.wait_send()
 
 
 class Spread:
     def __init__(self, at, full, send, recv):
         self.at, self.full, self.send, self.recv = at, full, send, recv
-        self.height = full.shape[2] // at.n_f // 2
-
-    def part(self, o, shift, half):
-        at = self.at
-        first = (at.fsdp(shift) * 2 + half) * self.height
+        self.height = full.shape[2] // at.n_f // at.n_c
+
+    def part(self, o, shift, piece):
+        at = self.at
+        first = (at.fsdp(shift) * at.n_c + piece) * self.height
         return self.full.at[at.other(o), :, pl.ds(first, self.height), :]
 
-    def copy(self, part, k, peer):
+    def copy(self, part, k, piece, peer):
+        k = k * self.at.n_c + piece
         return remote(part, part, self.send.at[k], self.recv.at[k], peer)
 
-    def copies(self):
+    def own(self, piece):
+        at = self.at
+        return [
+            *(self.copy(self.part(0, 0, piece), s, piece, at.xy(s, 0)) for s in range(1, at.n_f)),
+            self.copy(self.part(0, 0, piece), 0, piece, at.xy(0, 1)),
+        ]
+
+    def passes(self, piece):
         at = self.at
         n = at.n_f
-        return [
-            *(
-                self.copy(self.part(0, 0, h), h * n + s, at.xy(s, 0))
-                for h in range(2)
-                for s in range(1, n)
-            ),
-            *(self.copy(self.part(0, 0, h), 2 * n + h, at.xy(0, 1)) for h in (1, 0)),
-        ]
-
-    def passes(self):
-        at = self.at
-        n = at.n_f
-        return [
-            *(self.copy(self.part(0, -s, 0), 3 * n + s, at.xy(0, 1)) for s in range(1, n)),
-            *(self.copy(self.part(1, 0, 1), 4 * n + s, at.xy(s, 0)) for s in range(1, n)),
-        ]
-
-    def start(self):
-        for copy in self.copies():
+        if piece < at.n_c // 2:
+            return [self.copy(self.part(0, -s, piece), n + s, piece, at.xy(0, 1)) for s in range(1, n)]
+        return [self.copy(self.part(1, 0, piece), n + s, piece, at.xy(s, 0)) for s in range(1, n)]
+
+    def start(self, piece):
+        for copy in self.own(piece):
             copy.start()
 
-    def forward(self):
-        copies, n = self.copies(), self.at.n_f
-        for copy in copies[: n - 1]:
+    def forward(self, piece):
+        own = self.own(piece)
+        for copy in own[:-1] if piece < self.at.n_c // 2 else own[-1:]:
             copy.wait_recv()
-        copies[2 * n - 2].wait_recv()
-        for copy in self.passes():
+        for copy in self.passes(piece):
             copy.start()
 
     def wait(self):
-        copies, n = self.copies(), self.at.n_f
-        for copy in copies[n - 1 : 2 * n - 2]:
-            copy.wait_recv()
-        copies[2 * n - 1].wait_recv()
-        for copy in copies:
-            copy.wait_send()
-        for copy in self.passes():
-            copy.wait()
+        for piece in range(self.at.n_c):
+            own = self.own(piece)
+            for copy in own[-1:] if piece < self.at.n_c // 2 else own[:-1]:
+                copy.wait_recv()
+            for copy in own:
+                copy.wait_send()
+            for copy in self.passes(piece):
+                copy.wait()
 
 
 class Collect:
-    def __init__(self, at, partial, stage, local, by_x, by_y, pass_x, pass_y, send, recv):
-        self.at, self.partial, self.stage, self.local = at, partial, stage, local
+    def __init__(self, at, partial, local, by_x, by_y, pass_x, pass_y, send, recv):
+        self.at, self.partial, self.local = at, partial, local
         self.by_x, self.by_y, self.pass_x, self.pass_y = by_x, by_y, pass_x, pass_y
         self.send, self.recv = send, recv
         self.matrices = by_y.shape[0]
@@ -447,81 +448,82 @@
             for copy in self.raw(group, m):
                 copy.start()
 
-    def reader(self, o, shift, half):
-        at = self.at
-        if self.stage is None:
+    def load(self, o, shift, half, m, stage, k):
+        return pltpu.make_async_copy(self.part(o, shift, half, m), stage, self.local.at[k])
+
+    def fetch(self, m, stages):
+        self.load(1, 0, 0, m, stages[0], 0).start()
+        self.load(0, 1, 1, m, stages[1], 1).start()
+
+    def fetch_own(self, m, stages):
+        for half in range(2):
+            self.load(0, 0, half, m, stages[half], 2 + 2 * m + half).start()
+
+    def reader(self, o, shift, half, m, stage):
+        if stage is None:
             first = self.first(shift, half)
-            return lambda m, rows, start: self.partial[
-                at.other(o), m, pl.ds(pl.multiple_of(first + start, ROWS), ROWS)
+            return lambda rows, start: self.partial[
+                self.at.other(o), m, pl.ds(pl.multiple_of(first + start, STEP_ROWS), STEP_ROWS)
             ]
-        loads = [
-            pltpu.make_async_copy(
-                self.part(o, shift, half, m), self.stage(m), self.local.at[m]
-            )
-            for m in range(self.matrices)
-        ]
-        for copy in loads:
-            copy.start()
-        for copy in loads:
-            copy.wait()
-        return lambda m, rows, start: self.stage(m)[rows]
-
-    def sweep(self, step, m):
-        @pl.loop(0, self.height // ROWS)
+        return lambda rows, start: stage[rows]
+
+    def sweep(self, step):
+        @pl.loop(0, self.height // STEP_ROWS)
         def _(i):
-            start = pl.multiple_of(i * ROWS, ROWS)
-            step(m, pl.ds(start, ROWS), start)
-
-    def forward(self):
+            start = pl.multiple_of(i * STEP_ROWS, STEP_ROWS)
+            step(pl.ds(start, STEP_ROWS), start)
+
+    def forward(self, m, stages=(None, None)):
         n = self.at.n_f
-        own = self.reader(1, 0, 0)
-
-        def add_y(m, rows, start):
-            value = own(m, rows, start).astype(F32)
+        for copy in self.raw(0, m):
+            copy.wait_recv()
+        if stages[0] is not None:
+            self.load(1, 0, 0, m, stages[0], 0).wait()
+        own = self.reader(1, 0, 0, m, stages[0])
+
+        def add_y(rows, start):
+            value = own(rows, start).astype(F32)
             for s in range(n - 1):
                 value = value + self.pass_x[s, m, rows].astype(F32)
             self.pass_x[0, m, rows] = value.astype(BF)
 
-        for m in range(self.matrices):
-            for copy in self.raw(0, m):
-                copy.wait_recv()
-            self.sweep(add_y, m)
-            self.added(0, m).start()
+        self.sweep(add_y)
+        self.added(0, m).start()
         for s in range(1, n):
-            own_x = self.reader(0, s, 1)
-
-            def add_x(m, rows, start, s=s, own_x=own_x):
-                value = own_x(m, rows, start).astype(F32) + self.pass_y[s - 1, m, rows].astype(F32)
+            if stages[1] is not None:
+                load = self.load(0, s, 1, m, stages[1], 1)
+                if s > 1:
+                    load.start()
+                load.wait()
+            own_x = self.reader(0, s, 1, m, stages[1])
+            self.raw(1, m)[s - 1].wait_recv()
+
+            def add_x(rows, start, s=s, own_x=own_x):
+                value = own_x(rows, start).astype(F32) + self.pass_y[s - 1, m, rows].astype(F32)
                 self.pass_y[s - 1, m, rows] = value.astype(BF)
 
-            for m in range(self.matrices):
-                self.raw(1, m)[s - 1].wait_recv()
-                self.sweep(add_x, m)
-                self.added(s, m).start()
-
-    def finish_sums(self, stage):
-        self.stage = stage
-        self.total()
-
-    def total(self):
+            self.sweep(add_x)
+            self.added(s, m).start()
+
+    def total(self, m, stages=(None, None)):
         n = self.at.n_f
+        for copy in self.raw(2, m):
+            copy.wait_recv()
+        for s in range(n):
+            self.added(s, m).wait_recv()
         for half in range(2):
-            own = self.reader(0, 0, half)
-
-            def add(m, rows, start, half=half, own=own):
-                here = pl.ds(pl.multiple_of(half * self.height + start, ROWS), ROWS)
-                value = own(m, rows, start).astype(F32) + self.by_y[m, here].astype(F32)
+            if stages[half] is not None:
+                self.load(0, 0, half, m, stages[half], 2 + 2 * m + half).wait()
+            own = self.reader(0, 0, half, m, stages[half])
+
+            def add(rows, start, half=half, own=own):
+                here = pl.ds(pl.multiple_of(half * self.height + start, STEP_ROWS), STEP_ROWS)
+                value = own(rows, start).astype(F32) + self.by_y[m, here].astype(F32)
                 for s in range(n - 1):
                     value = value + self.by_x[s, m, here].astype(F32)
                 self.by_y[m, here] = value.astype(BF)
 
-            for m in range(self.matrices):
-                if half == 0:
-                    for copy in self.raw(2, m):
-                        copy.wait_recv()
-                    for s in range(n):
-                        self.added(s, m).wait_recv()
-                self.sweep(add, m)
+            self.sweep(add)
 
     def finish(self):
         for m in range(self.matrices):
@@ -574,7 +576,7 @@
         rows, sheets = shard.shape[1], summed.shape[0]
         beside = shard.shape[0] // sheets
         width = summed.shape[2] // beside
-        self.local, self.far = [], []
+        self.copies = []
         for m in range(shard.shape[0]):
             target = shard.at[m, :, pl.ds(pl.multiple_of(at.c * width, 128), width)]
             first = m % beside * width
@@ -583,18 +585,21 @@
                 here = pl.ds(pl.multiple_of(c * rows, rows), rows)
                 return summed.at[m // beside, here, first : first + width]
 
-            self.local.append(pltpu.make_async_copy(part(at.c), target, local.at[m]))
+            copies = []
             for s in range(1, at.n_c):
                 k = m * at.n_c + s
-                self.far.append(remote(part(at.ctx(s)), target, send.at[k], recv.at[k], at.z(s)))
-
-    def start(self):
-        for copy in (*self.far, *self.local):
+                copies.append(remote(part(at.ctx(s)), target, send.at[k], recv.at[k], at.z(s)))
+            copies.append(pltpu.make_async_copy(part(at.c), target, local.at[m]))
+            self.copies.append(copies)
+
+    def start(self, m):
+        for copy in self.copies[m]:
             copy.start()
 
     def wait(self):
-        for copy in (*self.far, *self.local):
-            copy.wait()
+        for copies in self.copies:
+            for copy in copies:
+                copy.wait()
 
 
 def pack_weights(w, packed):
@@ -688,16 +693,22 @@
         at.greet([at.core, *at.all_z(), *at.all_xy()])
         gather.start()
         swap_att.start()
+        spread_att.start(swap_att.arrived(0))
         for copy in loads[3:]:
             copy.wait()
         recast(ff_wide, ff_low)
         gather.forward(range(1, 2))
-        swap_att.wait()
-        spread_att.start()
+        behind = [s for pair in zip(range(1, n_c), range(n_c - 1, 0, -1)) for s in pair][: n_c - 1]
+        spread_att.start(swap_att.arrived(behind[0]))
+        spread_att.start(swap_att.arrived(behind[1]))
         gather.forward(range(2, n_c - 1))
         swap_ff.start()
+        for s in behind[2:]:
+            spread_att.start(swap_att.arrived(s))
         gather.forward(range(n_c - 1, n_c))
-        spread_att.forward()
+        for piece in range(n_c):
+            spread_att.forward(piece)
+        spread_ff.start(swap_ff.arrived(0))
         gather.finish()
         take = [pltpu.make_async_copy(rows_ref.at[b], a1.at[pl.ds(b * half, half)], lp.at[b]) for b in range(2 * n_c)]
         for copy in take:
@@ -719,11 +730,17 @@
             copy.wait()
         attend(a1, packed, place, key_place, first, cos, sine, qkv, attended, mass, part)
         scatter.start()
-        scatter.pass_on(range(n_c - 1, 1, -1))
-        swap_ff.wait()
-        spread_ff.start()
+        cots.start()
+        scatter.pass_on(range(n_c - 1, n_c - 2, -1))
+        spread_ff.start(swap_ff.arrived(behind[0]))
+        spread_ff.start(swap_ff.arrived(behind[1]))
+        cots.forward(range(1, 2))
+        scatter.pass_on(range(n_c - 2, 1, -1))
+        for s in behind[2:]:
+            spread_ff.start(swap_ff.arrived(s))
+        cots.forward(range(2, 3))
         scatter.pass_on(range(1, 2))
-        cots.start()
+        spread_ff.forward(0)
         scatter.arrive()
 
         def norm_two(rows):
@@ -733,24 +750,27 @@
 
         by_rows(half, norm_two)
         a2.start()
-        cots.forward(range(1, 2))
         a2.forward(range(1, 2))
-        spread_ff.forward()
-        for hop in range(2, n_c):
-            a2.forward(range(hop, hop + 1))
-            cots.forward(range(hop, hop + 1))
+        spread_ff.forward(n_c - 1)
+        a2.forward(range(2, 3))
+        for piece in range(1, n_c - 1):
+            spread_ff.forward(piece)
+        a2.forward(range(3, n_c))
+        cots.forward(range(3, n_c))
         cots.finish()
         a2.finish()
         scatter.finish()
+        swap_att.finish()
+        swap_ff.finish()
         spread_ff.wait()
 
     def back_kernel(
-        a2_ref, cots_ref, joined_ref, d_a2_ref, branch_ref, mid_ref, tok_ref, cot_ref, a1_ref, attw_ref,
+        a2_ref, cots_ref, joined_ref, d_a2_ref, ffw_ref, mid_ref, tok_ref, cot_ref, a1_ref, attw_ref,
         place, key_place, first, cos, sine, qkv, attended, mass,
         input_ref, out_ref, attg_ref, ffg_ref, norm_ref, grad_ref, rows_ref,
         rows_one, rows_two, wide, sheets, d_v, d_k, own, block, low, x_ref, own_cot, lk, lg, credit,
         part, near, sent, got, ss, sr, g1, h1, l1, lf, s4, r4, l4, s5, r5, l5, s6, r6, l6,
-        total, got_t, got_c, got_f, s7, r7, *collected,
+        total, got_p, got_c, s7, r7, *collected,
     ):
         at = Place(sizes)
         half = own.shape[0]
@@ -771,16 +791,16 @@
         gather = Gather(at, low, rows_ref, g1, h1, l1)
         columns = sheets.shape[3]
         high = tall // n_f // 2
-        collect_ff = Collect(
-            at, grad_ref, lambda m: sheets.at[0, 0, pl.ds(m * high, high)], lf, *collected[:6]
-        )
-        collect_att = Collect(at, sheets, None, None, *collected[6:])
+        early = [wide.at[1, pl.ds(length, high), pl.ds(i * columns, columns)] for i in range(2)]
+        late = [
+            [sheets.at[m % 2, 0, pl.ds((m // 2 * 2 + i) * high, high)] for i in range(2)] for m in range(3)
+        ]
+        collect_ff = Collect(at, grad_ref, lf, *collected[:6])
+        collect_att = Collect(at, sheets, None, *collected[6:])
         give_ff = Return(at, collected[1], ffg_ref, s5, r5, l5)
         give_att = Return(at, collected[7], attg_ref, s4, r4, l4)
-        tps = [(at.f, at.c, lax.rem(at.t + s, n_t)) for s in range(1, n_t)]
-        fs = [at.xy(s, 0) for s in range(1, n_f)]
         load((d_a2_ref, part))
-        at.greet([*tps, *at.all_z(), *fs])
+        at.greet([*plane(at), *at.all_z()])
         scatter.start()
         load(
             (a2_ref, rows_one),
@@ -811,14 +831,19 @@
                 sheets[y, 0, cols] = dot(rows[:, cols], side, ((0,), (0,))).astype(BF)
 
             keep(k).start()
-            if y == 0 and m > 0:
-                collect_ff.start(m - 1)
-            if k in (0, 3, 5):
-                hop = {0: n_c - 1, 3: n_c - 2, 5: n_c - 3}[k]
-                scatter.pass_on(range(hop, hop + 1))
+            if k == 0:
+                scatter.pass_on(range(n_c - 1, n_c - 2, -1))
+            if k == 2:
+                collect_ff.start(0)
+            if k == 3:
+                scatter.pass_on(range(n_c - 2, 1, -1))
+            if k == 4:
+                collect_ff.start(1)
         keep(4).wait()
         keep(5).wait()
         collect_ff.start(2)
+        collect_ff.fetch(0, early)
+        scatter.pass_on(range(1, 2))
         scatter.arrive()
 
         def norm_two(rows):
@@ -829,14 +854,29 @@
 
         by_rows(half, norm_two)
         gather.start()
+        heads = attw_ref.shape[0]
+        load(*((ffw_ref.at[y, 2], wide.at[0, :, pl.ds(y * columns, columns)]) for y in range(heads)))
         scatter.finish()
         scatter.free(credit.at[0])
-        load((branch_ref, part))
-        gather.forward(range(1, n_c - 1))
+        width = part.shape[2] // 4
+
+        @pl.loop(0, 4)
+        def _(c):
+            cols = pl.ds(pl.multiple_of(c * width, width), width)
+            value = dot(wide[1, :length], wide[0, cols], ((1,), (1,))).astype(BF)
+            part[:, :, cols] = value.reshape(part.shape[0], part.shape[1], width)
+
+        gather.forward(range(1, 2))
+        collect_ff.forward(0, early)
+        collect_ff.fetch(1, early)
+        gather.forward(range(2, n_c - 1))
         scatter.start()
-        collect_ff.forward()
+        collect_ff.forward(1, early)
+        collect_ff.fetch(2, early)
+        for m in range(3):
+            collect_ff.fetch_own(m, late[m])
+        collect_ff.forward(2, early)
         gather.forward(range(n_c - 1, n_c))
-        heads = attw_ref.shape[0]
         load(
             *in_blocks(a1_ref, rows_two),
             *(
@@ -855,8 +895,14 @@
             attend_back(y, packed, joint, place, key_place, first, cos, sine, qkv, mass, d_v, d_k, heads)
             if y == 0:
                 scatter.pass_on(range(n_c - 2, 1, -1))
+                collect_ff.total(0, late[0])
         scatter.pass_on(range(1, 2))
+        give_ff.start(0)
+        collect_ff.total(1, late[1])
         scatter.arrive()
+        give_ff.start(1)
+        collect_ff.total(2, late[2])
+        give_ff.start(2)
 
         def add(rows):
             block[rows] = (mid_ref[rows] + scatter.total(rows)).astype(BF)
@@ -864,7 +910,6 @@
         by_rows(half, add)
         scatter.finish()
         scatter.free(credit.at[1])
-        width = part.shape[2] // 4
 
         @pl.loop(0, 4)
         def _(c):
@@ -894,13 +939,13 @@
         share_block = Share(at, block, out_ref, s6.at[0], r6.at[0], l6.at[0])
         share_input = Share(at, low, input_ref, s6.at[1], r6.at[1], l6.at[1])
         share_block.start()
-        collect_ff.finish_sums(lambda m: rows_one.at[pl.ds(0, high), pl.ds(m * columns, columns)])
-        give_ff.start()
-        collect_att.forward()
-        scatter.pass_on(range(n_c - 2, 0, -1))
+        collect_att.forward(0)
+        scatter.pass_on(range(n_c - 2, 1, -1))
         share_block.forward()
-        collect_att.total()
-        give_att.start()
+        collect_att.total(0)
+        for m in range(4):
+            give_att.start(m)
+        scatter.pass_on(range(1, 2))
         scatter.arrive()
 
         def norm_one(rows):
@@ -924,13 +969,17 @@
             *((ffg_ref.at[m], ff_low[m]) for m in range(3)),
             *((attg_ref.at[m], att_low[m]) for m in range(4)),
         )
-        sum_norm(at, (*ff_low, *att_low), norm_ref, total, got_t, got_c, got_f, s7, r7)
+        sum_norm(at, (*ff_low, *att_low), norm_ref, total, got_p, got_c, s7, r7)
         share_block.finish()
         share_input.finish()
 
-    def sum_norm(at, grads, norm_ref, total, got_t, got_c, got_f, send, recv):
-        tps = [(at.f, at.c, lax.rem(at.t + s, n_t)) for s in range(1, n_t)]
-        fs = [at.xy(s, 0) for s in range(1, n_f)]
+    def plane(at):
+        count = n_f * n_t
+        here = at.f * n_t + at.t
+        others = [lax.rem(here + i, count) for i in range(1, count)]
+        return [(i // n_t, at.c, lax.rem(i, n_t)) for i in others]
+
+    def sum_norm(at, grads, norm_ref, total, got_p, got_c, send, recv):
         total[0] = jnp.zeros(total.shape[1:], F32)
         for low in grads:
 
@@ -945,7 +994,7 @@
 
             by_rows(low.shape[0], square)
         base = 0
-        stages = ((tps, got_t, at.t), (at.all_z(), got_c, at.c), (fs, got_f, at.f))
+        stages = ((plane(at), got_p, at.f * n_t + at.t), (at.all_z(), got_c, at.c))
         for stage, (peers, got, place) in enumerate(stages):
             copies = [
                 remote(total.at[stage], got.at[place], send.at[base + i], recv.at[base + i], peer)
@@ -961,7 +1010,7 @@
             for i in range(1, got.shape[0]):
                 value = value + got[i]
             total[stage + 1] = value
-        norm = jnp.sqrt(jnp.sum(total[3], axis=(0, 1), keepdims=True))
+        norm = jnp.sqrt(jnp.sum(total[2], axis=(0, 1), keepdims=True))
         norm_ref[...] = jnp.broadcast_to(norm, norm_ref.shape)
 
     def finish_kernel(norm_ref, block_in, input_in, attg_ref, ffg_ref, *refs):
@@ -1112,7 +1161,7 @@
         ).astype(BF)
         joint[:, 2 * wide + y * HEAD_DIM : 2 * wide + (y + 1) * HEAD_DIM] = d_v[...].astype(BF)
 
-    def hidden_kernel(a2, cot, w, d_a2, branch, joined, kept):
+    def hidden_kernel(a2, cot, w, d_a2, joined, kept):
         d_up, d_gate, hidden = joined.at[0], joined.at[1], joined.at[2]
         step, steps = pl.program_id(0), pl.num_programs(0)
         tile = w.shape[3]
@@ -1132,7 +1181,7 @@
             d_up[rows, here] = (d_hid * act).astype(BF)
             d_gate[rows, here] = (d_hid * up * sigma * (1.0 + gate * (1.0 - sigma))).astype(BF)
 
-        for m in range(3):
+        for m in range(2):
             kept[m, :, here] = w[0, m]
 
         @pl.when(step == steps - 1)
@@ -1144,7 +1193,6 @@
                     dot(d_up[...], kept[0, cols], ((1,), (1,)))
                     + dot(d_gate[...], kept[1, cols], ((1,), (1,)))
                 ).astype(BF)
-                branch[:, cols] = dot(hidden[...], kept[2, cols], ((1,), (1,))).astype(BF)
 
     def shards(
         tokens,
@@ -1231,7 +1279,7 @@
             + scatter_scratch(n_c, half, width)
             + gather_sems(n_c) * 3
             + [dma(n_c), dma(n_c), pltpu.SemaphoreType.DMA] * 2
-            + [dma(5 * n_f)] * 4,
+            + [dma(2 * n_f * n_c)] * 4,
             vmem=56,
         )(tokens, cotangent, *tables, att_proj, attn_out, ff_proj, ff_out)
         act_two = act_two.reshape(pack_len, width)
@@ -1242,22 +1290,21 @@
         kept = pl.BlockSpec((pack_len, width), lambda i: (0, 0), pipeline_mode=pl.Buffered(1))
         moved = pl.BlockSpec((1, 3, width, tile), lambda i: (i // tiles, 0, 0, i % tiles))
         rows_flat = jax.ShapeDtypeStruct((pack_len, width), BF)
-        act_two_part, branch_part, joined = pl.pallas_call(
+        act_two_part, joined = pl.pallas_call(
             hidden_kernel,
             grid=(2 * tiles,),
-            out_shape=(rows_flat, rows_flat, jax.ShapeDtypeStruct((3, pack_len, 2 * ff_cols), BF)),
+            out_shape=(rows_flat, jax.ShapeDtypeStruct((3, pack_len, 2 * ff_cols), BF)),
             in_specs=[kept, kept, moved],
             out_specs=(
                 kept,
-                kept,
                 pl.BlockSpec((3, pack_len, 2 * ff_cols), lambda i: (0, 0, 0), pipeline_mode=pl.Buffered(1)),
             ),
-            scratch_shapes=[pltpu.VMEM((3, width, 2 * ff_cols), BF)],
+            scratch_shapes=[pltpu.VMEM((2, width, 2 * ff_cols), BF)],
             compiler_params=pltpu.CompilerParams(vmem_limit_bytes=60 << 20),
             name="hidden",
         )(act_two, cot_rows, ff_w)
         height = width // n_f
-        count = n_f + n_c + n_t
+        count = n_f * n_t + n_c
         input_grad, block_out, att_total, ff_total, norm_value, *_ = call(
             back_kernel,
             "back",
@@ -1291,20 +1338,20 @@
             ]
             + scatter_scratch(n_c, half, width)
             + gather_sems(n_c)
-            + [dma(3)]
+            + [dma(8)]
             + [dma(4 * n_c), dma(4 * n_c), dma(4), dma(3 * n_c), dma(3 * n_c), dma(3)]
             + [
                 pltpu.SemaphoreType.DMA((2, 3)),
                 pltpu.SemaphoreType.DMA((2, 3)),
                 dma(2),
             ]
-            + [pltpu.VMEM((k, 8, 128), F32) for k in (4, n_t, n_c, n_f)]
+            + [pltpu.VMEM((k, 8, 128), F32) for k in (3, n_f * n_t, n_c)]
             + [dma(count), dma(count)]
             + collect_scratch(n_f, 3, height, ff_cols)
             + collect_scratch(n_f, 1, height, 4 * att_cols),
             vmem=62,
         )(
-            act_two, cot_rows, joined, act_two_part.reshape(rows_bf.shape), branch_part.reshape(rows_bf.shape),
+            act_two, cot_rows, joined, act_two_part.reshape(rows_bf.shape), ff_w,
             resid_mid, tokens, cotangent, act_one, att_w, *tables, qkv, attended, mass,
         )
         weights = (att_proj, attn_out, ff_proj, ff_out)

time: 624 us -> 576 us (0.923)
  Pallas kernels: 614 us -> 567 us
    pallas_call x1, Pallas kernels: 260 us -> 239 us  [shards(): call(front_kernel, 'front', 0, (rows_bf, att_full, ff_full, rows_bf, rows...]
    pallas_call x1, Pallas kernels: 284 us -> 264 us  [shards(): call(back_kernel, 'back', 1, (jax.ShapeDtypeStruct((n_t, half, width), BF...]
where the time goes in v6:
time: 576 us
  Pallas kernels  567 us (98%)
    pallas_call x1, Pallas kernels, shards(): call(back_kernel, 'back', 1, (jax.ShapeDtypeStruct((n_t, half, width), BF...  264 us
    pallas_call x1, Pallas kernels, shards(): call(front_kernel, 'front', 0, (rows_bf, att_full, ff_full, rows_bf, rows...  239 us
    pallas_call x1, Pallas kernels, shards(): pl.pallas_call(hidden_kernel, grid=(2 * tiles,), out_shape=(rows_flat, ja...  35.2 us
    pallas_call x1, Pallas kernels, shards(): pl.pallas_call(finish_kernel, out_shape=(*(jax.ShapeDtypeStruct(w.shape,...  28.6 us

profile of v6, /device:TPU:0, one launch (start us, length us, event | category | flops | bytes accessed | tf_op | source)
XLA Modules:
  0.0 575.7 jit_solution(5935799223899962291)
XLA Ops:
  0.7 0.0 copy-start
  0.7 0.7 fusion.4
  1.4 0.1 fusion.2
  1.5 0.7 fusion.3
  2.2 0.0 copy-done
  2.2 0.0 copy-start.2
  2.2 0.1 fusion.1
  2.4 1.0 copy.43.place
  3.4 1.0 copy.44.first
  4.4 1.9 fusion
  6.3 1.3 pad_maximum_fusion
  7.6 0.0 copy-done.2
  7.6 239.1 %front.1 = (bf16[8,128,2048]{2,1,0:T(8,128)(2,1)}, bf16[2,4,2048,128]{3,2,1,0:T(8,128)(2,1)}, bf16[2,3,2048,512]{3,2,1,0:T(8,128)(2,1)}, bf16[8,128,2048]{2,1,0:...) custom-call(bf16[2,256,2048]{2,1,0:T(8,128)(2,1)} %tok_ref.3, ...), custom_call_target="tpu_custom_call" | custom-call | tf_op jit(solution)/shard_map/front/pallas_call | solution.py:1249
  246.8 35.2 %hidden.1 = (bf16[1024,2048]{1,0:T(8,128)(2,1)}, bf16[3,1024,1024]{2,1,0:T(8,128)(2,1)}) custom-call(bf16[1024,2048]{1,0:T(8,128)(2,1)} %bitcast.18, bf16[1024,2048]{1,0:T(8,128)(2,1)} %bitcast.20, bf16[2,3,2048,512]{3,2,1,0:T(8,128)(2,1)} %get-tuple-element.63.w.ffw_ref), custom_call_target="tpu_custom_call" | custom-call | tf_op jit(solution)/shard_map/hidden/pallas_call | solution.py:1293
  282.0 263.7 %back.1 = (bf16[4,128,2048]{2,1,0:T(8,128)(2,1)}, bf16[4,128,2048]{2,1,0:T(8,128)(2,1)}, bf16[4,256,512]{2,1,0:T(8,128)(2,1)}, bf16[3,256,2048]{2,1,0:T(8,128)(2...) custom-call(bf16[1024,2048]{1,0:T(8,128)(2,1)} %bitcast.19, ...), custom_call_target="tpu_custom_call" | custom-call | tf_op jit(solution)/shard_map/back/pallas_call | solution.py:1308
  545.7 1.2 slice.3
  546.9 0.0 copy-start.1
  546.9 28.6 %finish.1 = (f32[3,256,512]{2,1,0:T(8,128)}, f32[256,512]{1,0:T(8,128)}, f32[2,256,2048]{2,1,0:T(8,128)}, f32[256,2048]{1,0:T(8,128)}, f32[3,256,512]{2,1,0:T(8,...) custom-call(f32[8,128]{1,0:T(8,128)} %get-tuple-element.72.norm_ref,, ...), custom_call_target="tpu_custom_call" | custom-call | tf_op jit(solution)/shard_map/finish/pallas_call | solution.py:1360
  575.5 0.0 copy-done.1
  (4 shorter events, 0.0 us)
Async XLA Ops:
  0.7 1.5 copy-start
  2.2 5.4 copy-start.2
  546.9 28.6 %copy-start.1 = (s32[2,1024]{1,0:T(2,128)S(1)}, s32[2,1024]{1,0:T(2,128)}, u32[]{:S(2)}) copy-start(s32[2,1024]{1,0:T(2,128)} %param.19) | copy-start | bytes 24580

commit v7 on v6

--- a/solution.py
+++ b/solution.py
@@ -196,11 +196,14 @@
     def far(self, way, hop, slot):
         at = self.at
         k = at.n_c + hop + (0 if way > 0 else at.n_c)
-        sent = self.sent.at[jnp.clip(at.c + way * hop, 0, at.n_c - 1)]
+        sent = self.sent.at[self.slot(jnp.clip(at.c + way * hop, 0, at.n_c - 1))]
         return remote(sent, self.got.at[slot], self.send.at[k], self.recv.at[k], at.z(way))
 
+    def slot(self, c):
+        return jnp.minimum(jnp.where(c > self.at.c, c - 1, c), self.at.n_c - 2)
+
     def end(self, way):
-        return self.at.n_c + (0 if way > 0 else 1)
+        return self.at.c if way > 0 else self.at.n_c
 
     there = Gather.there
 
@@ -232,16 +235,16 @@
 
                     else:
                         self.add(c, False)
-                    self.far(way, hop, self.end(way) if hop == 1 else c).start()
+                    self.far(way, hop, at.n_c if hop == 1 and way < 0 else c).start()
 
     def add(self, c, more):
-        at = self.at
+        at, slot = self.at, self.slot(c)
 
         def rows_of(rows):
             value = self.part[c * 2 + at.lo, rows].astype(F32) + self.near[c, rows].astype(F32)
             if more:
                 value = value + self.got[c, rows].astype(F32)
-            self.sent[c, rows] = value.astype(BF)
+            self.sent[slot, rows] = value.astype(BF)
 
         by_rows(self.near.shape[1], rows_of)
 
@@ -302,8 +305,8 @@
     return [
         pltpu.VMEM((2 * n_c, half, width), BF),
         pltpu.VMEM((n_c, half, width), BF),
-        pltpu.VMEM((n_c, half, width), BF),
-        pltpu.VMEM((n_c + 2, half, width), BF),
+        pltpu.VMEM((n_c - 1, half, width), BF),
+        pltpu.VMEM((n_c + 1, half, width), BF),
         pltpu.SemaphoreType.DMA((3 * n_c,)),
         pltpu.SemaphoreType.DMA((3 * n_c,)),
     ]
@@ -505,7 +508,7 @@
             self.sweep(add_x)
             self.added(s, m).start()
 
-    def total(self, m, stages=(None, None)):
+    def total(self, m, squares, stages=(None, None)):
         n = self.at.n_f
         for copy in self.raw(2, m):
             copy.wait_recv()
@@ -521,7 +524,19 @@
                 value = own(rows, start).astype(F32) + self.by_y[m, here].astype(F32)
                 for s in range(n - 1):
                     value = value + self.by_x[s, m, here].astype(F32)
-                self.by_y[m, here] = value.astype(BF)
+                rounded = value.astype(BF)
+                self.by_y[m, here] = rounded
+                value = rounded.astype(F32)
+                value = value * value
+                tall = squares.shape[1]
+                rows = value[:tall]
+                for r in range(tall, value.shape[0], tall):
+                    rows = rows + value[r : r + tall]
+                wide = squares.shape[2]
+                lanes = rows[:, :wide]
+                for c in range(wide, value.shape[1], wide):
+                    lanes = lanes + rows[:, c : c + wide]
+                squares[0] += lanes
 
             self.sweep(add)
 
@@ -655,7 +670,7 @@
         )
 
     def front_kernel(
-        tok_ref, cot_ref, place, key_place, first, cos, sine, att_ref, out_ref, ffp_ref, ffo_ref,
+        tok_ref, cot_ref, spots, key_place, cos, sine, att_ref, out_ref, ffp_ref, ffo_ref,
         rows_ref, attw_ref, ffw_ref, a2_ref, cots_ref, qkv, attended, mass, mid_ref,
         x_ref, own_cot, att_wide, ff_wide, att_low, ff_low, low, a1, packed, lk, lp,
         part, near, sent, got, ss, sr, g1, h1, l1, g2, h2, l2, g3, h3, l3, s4, r4, l4, s5, r5, l5, s6, r6, s7, r7,
@@ -691,8 +706,8 @@
         loads[2].wait()
         recast(att_wide, att_low)
         at.greet([at.core, *at.all_z(), *at.all_xy()])
+        swap_att.start()
         gather.start()
-        swap_att.start()
         spread_att.start(swap_att.arrived(0))
         for copy in loads[3:]:
             copy.wait()
@@ -728,7 +743,7 @@
             copy.start()
         for copy in (*take, *packs):
             copy.wait()
-        attend(a1, packed, place, key_place, first, cos, sine, qkv, attended, mass, part)
+        attend(a1, packed, spots, key_place, cos, sine, qkv, attended, mass, part)
         scatter.start()
         cots.start()
         scatter.pass_on(range(n_c - 1, n_c - 2, -1))
@@ -766,15 +781,15 @@
 
     def back_kernel(
         a2_ref, cots_ref, joined_ref, d_a2_ref, ffw_ref, mid_ref, tok_ref, cot_ref, a1_ref, attw_ref,
-        place, key_place, first, cos, sine, qkv, attended, mass,
+        spots, key_place, cos, sine, qkv, attended, mass,
         input_ref, out_ref, attg_ref, ffg_ref, norm_ref, grad_ref, rows_ref,
-        rows_one, rows_two, wide, sheets, d_v, d_k, own, block, low, x_ref, own_cot, lk, lg, credit,
-        part, near, sent, got, ss, sr, g1, h1, l1, lf, s4, r4, l4, s5, r5, l5, s6, r6, l6,
+        rows_one, rows_two, wide, sheets, d_v, d_k, own, block, low, lk, lg, credit,
+        part, near, sent, got, ss, sr, near2, sent2, got2, ss2, sr2, g1, h1, l1, lf, s4, r4, l4, s5, r5, l5, s6, r6, l6,
         total, got_p, got_c, s7, r7, *collected,
     ):
         at = Place(sizes)
         half = own.shape[0]
-        length, tall = rows_one.shape[0], wide.shape[1]
+        length, tall = 2 * n_c * half, wide.shape[1]
         mine = pl.ds(pl.multiple_of(at.lo * half, half), half)
 
         def load(*pairs):
@@ -784,10 +799,12 @@
             for copy in copies:
                 copy.wait()
 
-        def in_blocks(src, dst):
-            return [(src.at[b], dst.at[pl.ds(b * half, half)]) for b in range(2 * n_c)]
+        def flat(ref, cols=slice(None)):
+            value = ref[:, :, cols]
+            return value.reshape(length, value.shape[2])
 
         scatter = Scatter(at, part, near, sent, got, ss, sr)
+        branch = Scatter(at, rows_one, near2, sent2, got2, ss2, sr2)
         gather = Gather(at, low, rows_ref, g1, h1, l1)
         columns = sheets.shape[3]
         high = tall // n_f // 2
@@ -799,8 +816,9 @@
         collect_att = Collect(at, sheets, None, *collected[6:])
         give_ff = Return(at, collected[1], ffg_ref, s5, r5, l5)
         give_att = Return(at, collected[7], attg_ref, s4, r4, l4)
+        total[0] = jnp.zeros(total.shape[1:], F32)
+        at.greet([*plane(at), *at.all_z()])
         load((d_a2_ref, part))
-        at.greet([*plane(at), *at.all_z()])
         scatter.start()
         load(
             (a2_ref, rows_one),
@@ -808,8 +826,7 @@
             (joined_ref.at[0], wide.at[0, pl.ds(0, length)]),
             (joined_ref.at[1], wide.at[0, pl.ds(length, length)]),
             (joined_ref.at[2], wide.at[1, pl.ds(0, length)]),
-            (tok_ref.at[at.hi, mine], x_ref),
-            (cot_ref.at[at.hi, mine], own_cot),
+            (cot_ref.at[at.hi, mine], block),
         )
 
         def keep(k):
@@ -828,7 +845,7 @@
             def _(i, y=y, rows=rows, slot=slot, start=start):
                 cols = pl.ds(pl.multiple_of(i * (tall // 2), tall // 2), tall // 2)
                 side = wide[slot, start : start + length, y * columns : (y + 1) * columns]
-                sheets[y, 0, cols] = dot(rows[:, cols], side, ((0,), (0,))).astype(BF)
+                sheets[y, 0, cols] = dot(flat(rows, cols), side, ((0,), (0,))).astype(BF)
 
             keep(k).start()
             if k == 0:
@@ -848,29 +865,20 @@
 
         def norm_two(rows):
             normed, scale = mean_spread(mid_ref[rows])
-            grad = own_cot[rows].astype(F32) + norm_back(scatter.total(rows), normed, scale)
+            grad = block[rows].astype(F32) + norm_back(scatter.total(rows), normed, scale)
             own[rows] = grad
             low[rows] = grad.astype(BF)
 
         by_rows(half, norm_two)
         gather.start()
         heads = attw_ref.shape[0]
-        load(*((ffw_ref.at[y, 2], wide.at[0, :, pl.ds(y * columns, columns)]) for y in range(heads)))
         scatter.finish()
         scatter.free(credit.at[0])
         width = part.shape[2] // 4
-
-        @pl.loop(0, 4)
-        def _(c):
-            cols = pl.ds(pl.multiple_of(c * width, width), width)
-            value = dot(wide[1, :length], wide[0, cols], ((1,), (1,))).astype(BF)
-            part[:, :, cols] = value.reshape(part.shape[0], part.shape[1], width)
-
         gather.forward(range(1, 2))
         collect_ff.forward(0, early)
         collect_ff.fetch(1, early)
         gather.forward(range(2, n_c - 1))
-        scatter.start()
         collect_ff.forward(1, early)
         collect_ff.fetch(2, early)
         for m in range(3):
@@ -878,38 +886,25 @@
         collect_ff.forward(2, early)
         gather.forward(range(n_c - 1, n_c))
         load(
-            *in_blocks(a1_ref, rows_two),
+            (a1_ref, rows_two),
             *(
                 (attw_ref.at[y, i], wide.at[0, :, pl.ds((i * heads + y) * HEAD_DIM, HEAD_DIM)])
                 for i in range(4)
                 for y in range(heads)
             ),
         )
-        scatter.pass_on(range(n_c - 1, n_c - 2, -1))
         gather.finish()
-        load(*in_blocks(rows_ref, rows_one))
+        load((rows_ref, rows_one), (tok_ref.at[at.hi, mine], low))
         packed, joint = wide.at[0], wide.at[1, pl.ds(length, length)]
         wide_heads = heads * HEAD_DIM
-        joint[:, :wide_heads] = dot(rows_one[...], packed[:, 3 * wide_heads :], ((1,), (0,))).astype(BF)
+        joint[:, :wide_heads] = dot(flat(rows_one), packed[:, 3 * wide_heads :], ((1,), (0,))).astype(BF)
+        collect_ff.total(0, total, late[0])
+        give_ff.start(0)
         for y in range(heads):
-            attend_back(y, packed, joint, place, key_place, first, cos, sine, qkv, mass, d_v, d_k, heads)
+            attend_back(y, packed, joint, spots, key_place, cos, sine, qkv, mass, d_v, d_k, heads)
             if y == 0:
-                scatter.pass_on(range(n_c - 2, 1, -1))
-                collect_ff.total(0, late[0])
-        scatter.pass_on(range(1, 2))
-        give_ff.start(0)
-        collect_ff.total(1, late[1])
-        scatter.arrive()
-        give_ff.start(1)
-        collect_ff.total(2, late[2])
-        give_ff.start(2)
-
-        def add(rows):
-            block[rows] = (mid_ref[rows] + scatter.total(rows)).astype(BF)
-
-        by_rows(half, add)
-        scatter.finish()
-        scatter.free(credit.at[1])
+                collect_ff.total(1, total, late[1])
+                give_ff.start(1)
 
         @pl.loop(0, 4)
         def _(c):
@@ -918,6 +913,7 @@
             part[:, :, cols] = value.reshape(part.shape[0], part.shape[1], width)
 
         scatter.start()
+        collect_ff.total(2, total, late[2])
 
         @pl.loop(0, 2)
         def _(c):
@@ -925,10 +921,10 @@
             for i in range(4):
                 if i < 3:
                     value = dot(
-                        rows_two[:, cols], joint[:, i * wide_heads : (i + 1) * wide_heads], ((0,), (0,))
+                        flat(rows_two, cols), joint[:, i * wide_heads : (i + 1) * wide_heads], ((0,), (0,))
                     )
                 else:
-                    value = dot(rows_one[:, cols], attended[...], ((0,), (0,)))
+                    value = dot(flat(rows_one, cols), attended[...], ((0,), (0,)))
                 for y in range(heads):
                     sheets[y, 0, cols, i * HEAD_DIM : (i + 1) * HEAD_DIM] = value[
                         :, y * HEAD_DIM : (y + 1) * HEAD_DIM
@@ -936,40 +932,51 @@
 
         collect_att.start(0)
         scatter.pass_on(range(n_c - 1, n_c - 2, -1))
+        give_ff.start(2)
+        load(*((ffw_ref.at[y, 2], wide.at[0, :, pl.ds(y * columns, columns)]) for y in range(heads)))
+
+        @pl.loop(0, 4)
+        def _(c):
+            cols = pl.ds(pl.multiple_of(c * width, width), width)
+            value = dot(wide[1, :length], wide[0, cols], ((1,), (1,))).astype(BF)
+            rows_one[:, :, cols] = value.reshape(rows_one.shape[0], rows_one.shape[1], width)
+
+        branch.start()
         share_block = Share(at, block, out_ref, s6.at[0], r6.at[0], l6.at[0])
         share_input = Share(at, low, input_ref, s6.at[1], r6.at[1], l6.at[1])
-        share_block.start()
+        scatter.pass_on(range(n_c - 2, 1, -1))
+        branch.pass_on(range(n_c - 1, n_c - 2, -1))
         collect_att.forward(0)
-        scatter.pass_on(range(n_c - 2, 1, -1))
-        share_block.forward()
-        collect_att.total(0)
+        scatter.pass_on(range(1, 2))
+        branch.pass_on(range(n_c - 2, 1, -1))
+        collect_att.total(0, total)
         for m in range(4):
             give_att.start(m)
-        scatter.pass_on(range(1, 2))
+        branch.pass_on(range(1, 2))
         scatter.arrive()
 
         def norm_one(rows):
-            normed, scale = mean_spread(x_ref[rows].astype(F32))
+            normed, scale = mean_spread(low[rows].astype(F32))
             low[rows] = (own[rows] + norm_back(scatter.total(rows), normed, scale)).astype(BF)
 
         by_rows(half, norm_one)
         share_input.start()
+        branch.arrive()
+
+        def add(rows):
+            block[rows] = (mid_ref[rows] + branch.total(rows)).astype(BF)
+
+        by_rows(half, add)
+        share_block.start()
         scatter.finish()
+        branch.finish()
         collect_ff.finish()
         collect_att.finish()
         share_input.forward()
+        share_block.forward()
+        sum_norm(at, norm_ref, total, got_p, got_c, s7, r7)
         give_ff.wait()
         give_att.wait()
-        own_rows, own_cols = ffg_ref.shape[1], attg_ref.shape[2]
-        ff_low = [rows_one.at[pl.ds(m * own_rows, own_rows)] for m in range(3)]
-        att_low = [
-            rows_two.at[pl.ds(0, own_rows), pl.ds(m * own_cols, own_cols)] for m in range(4)
-        ]
-        load(
-            *((ffg_ref.at[m], ff_low[m]) for m in range(3)),
-            *((attg_ref.at[m], att_low[m]) for m in range(4)),
-        )
-        sum_norm(at, (*ff_low, *att_low), norm_ref, total, got_p, got_c, s7, r7)
         share_block.finish()
         share_input.finish()
 
@@ -979,20 +986,7 @@
         others = [lax.rem(here + i, count) for i in range(1, count)]
         return [(i // n_t, at.c, lax.rem(i, n_t)) for i in others]
 
-    def sum_norm(at, grads, norm_ref, total, got_p, got_c, send, recv):
-        total[0] = jnp.zeros(total.shape[1:], F32)
-        for low in grads:
-
-            def square(rows, low=low):
-                value = low[rows].astype(F32)
-                value = value * value
-                value = value[: ROWS // 2] + value[ROWS // 2 :]
-                lanes = value[:, :128]
-                for c in range(1, value.shape[1] // 128):
-                    lanes = lanes + value[:, c * 128 : (c + 1) * 128]
-                total[0] += lanes
-
-            by_rows(low.shape[0], square)
+    def sum_norm(at, norm_ref, total, got_p, got_c, send, recv):
         base = 0
         stages = ((plane(at), got_p, at.f * n_t + at.t), (at.all_z(), got_c, at.c))
         for stage, (peers, got, place) in enumerate(stages):
@@ -1090,7 +1084,7 @@
         for store in stores:
             store.wait()
 
-    def attend(a1, packed, place, key_place, first, cos, sine, qkv, attended, mass, part):
+    def attend(a1, packed, spots, key_place, cos, sine, qkv, attended, mass, part):
         wide = attended.shape[1]
         heads = wide // HEAD_DIM
         for i in range(3):
@@ -1108,7 +1102,7 @@
             def _(c, y=y, cols=cols):
                 rows = pl.ds(pl.multiple_of(c * QUERIES, QUERIES), QUERIES)
                 scores = dot(qkv[0, rows, cols], qkv[1, :, cols], ((1,), (1,))) * SCORE_SCALE
-                allowed = (key_place[...] <= place[rows]) & (key_place[...] >= first[rows])
+                allowed = (key_place[...] <= spots[rows, 0:1]) & (key_place[...] >= spots[rows, 1:2])
                 scores = jnp.where(allowed, scores, NEG_FILL)
                 peak = jnp.max(scores, axis=1, keepdims=True)
                 exp_scores = jnp.exp(scores - peak)
@@ -1125,7 +1119,7 @@
             value = dot(attended[...], packed[cols, 3 * wide :], ((1,), (1,))).astype(BF)
             part[:, :, cols] = value.reshape(part.shape[0], part.shape[1], width)
 
-    def attend_back(y, packed, joint, place, key_place, first, cos, sine, qkv, mass, d_v, d_k, heads):
+    def attend_back(y, packed, joint, spots, key_place, cos, sine, qkv, mass, d_v, d_k, heads):
         wide = heads * HEAD_DIM
         cols = slice(y * HEAD_DIM, (y + 1) * HEAD_DIM)
 
@@ -1135,7 +1129,7 @@
             query, key, value = qkv[0, rows, cols], qkv[1, :, cols], qkv[2, :, cols]
             d_att = joint[rows, cols]
             scores = dot(query, key, ((1,), (1,))) * SCORE_SCALE
-            allowed = (key_place[...] <= place[rows]) & (key_place[...] >= first[rows])
+            allowed = (key_place[...] <= spots[rows, 0:1]) & (key_place[...] >= spots[rows, 1:2])
             probs = jnp.exp(jnp.where(allowed, scores, NEG_FILL) - mass[rows, y : y + 1])
             d_prob = dot(d_att, value, ((1,), (1,)))
             delta = jnp.sum(probs * d_prob, axis=1, keepdims=True)
@@ -1239,9 +1233,8 @@
         angles = (places - firsts).astype(F32)[:, None] * inverse[None, :]
         cos_table, sine_table = jnp.cos(angles), jnp.sin(angles)
         tables = (
-            places[:, None],
+            jnp.stack([places, firsts], axis=1),
             places[None, :],
-            firsts[:, None],
             jnp.concatenate([cos_table, cos_table], axis=1),
             jnp.concatenate([-sine_table, sine_table], axis=1),
         )
@@ -1261,7 +1254,7 @@
                 jax.ShapeDtypeStruct((pack_len, 2), F32),
                 own_f32,
             ),
-            [ANY, ANY] + [VMEM] * 5 + [ANY] * 4,
+            [ANY, ANY] + [VMEM] * 4 + [ANY] * 4,
             (ANY,) * 5 + (VMEM,) * 4,
             [
                 pltpu.VMEM((half, width), BF),
@@ -1318,11 +1311,11 @@
                 ff_full,
                 rows_bf,
             ),
-            [ANY] * 5 + [VMEM] + [ANY] * 4 + [VMEM] * 8,
+            [ANY] * 5 + [VMEM] + [ANY] * 4 + [VMEM] * 7,
             (ANY,) * 4 + (VMEM,) + (ANY,) * 2,
             [
-                pltpu.VMEM((pack_len, width), BF),
-                pltpu.VMEM((pack_len, width), BF),
+                pltpu.VMEM((2 * n_c, half, width), BF),
+                pltpu.VMEM((2 * n_c, half, width), BF),
                 pltpu.VMEM((2, width, 4 * rank_width), BF),
                 pltpu.VMEM((2, 1, width, 4 * att_cols), BF),
                 pltpu.VMEM((pack_len, HEAD_DIM), F32),
@@ -1330,13 +1323,12 @@
                 pltpu.VMEM((half, width), F32),
                 pltpu.VMEM((half, width), BF),
                 pltpu.VMEM((half, width), BF),
-                pltpu.VMEM((half, width), BF),
-                pltpu.VMEM((half, width), BF),
-                dma(2 * n_c + 8),
+                dma(12),
                 dma(2),
-                pltpu.SemaphoreType.REGULAR((2, 3)),
+                pltpu.SemaphoreType.REGULAR((1, 3)),
             ]
             + scatter_scratch(n_c, half, width)
+            + scatter_scratch(n_c, half, width)[1:]
             + gather_sems(n_c)
             + [dma(8)]
             + [dma(4 * n_c), dma(4 * n_c), dma(4), dma(3 * n_c), dma(3 * n_c), dma(3)]
@@ -1351,7 +1343,7 @@
             + collect_scratch(n_f, 1, height, 4 * att_cols),
             vmem=62,
         )(
-            act_two, cot_rows, joined, act_two_part.reshape(rows_bf.shape), ff_w,
+            act_two.reshape(rows_bf.shape), cot_rows.reshape(rows_bf.shape), joined, act_two_part.reshape(rows_bf.shape), ff_w,
             resid_mid, tokens, cotangent, act_one, att_w, *tables, qkv, attended, mass,
         )
         weights = (att_proj, attn_out, ff_proj, ff_out)

time: 576 us -> 566 us (0.983)
  Pallas kernels: 567 us -> 557 us
    pallas_call x1, Pallas kernels: 239 us -> 231 us  [shards(): call(front_kernel, 'front', 0, (rows_bf, att_full, ff_full, rows_bf, rows...]
where the time goes in v7:
time: 566 us; the launch traced here: 565 us
  Pallas kernels  557 us (98%)
    pallas_call x1, Pallas kernels, shards(): call(back_kernel, 'back', 1, (jax.ShapeDtypeStruct((n_t, half, width), BF...  263 us
    pallas_call x1, Pallas kernels, shards(): call(front_kernel, 'front', 0, (rows_bf, att_full, ff_full, rows_bf, rows...  231 us
    pallas_call x1, Pallas kernels, shards(): pl.pallas_call(hidden_kernel, grid=(2 * tiles,), out_shape=(rows_flat, ja...  35.2 us
    pallas_call x1, Pallas kernels, shards(): pl.pallas_call(finish_kernel, out_shape=(*(jax.ShapeDtypeStruct(w.shape,...  28.6 us

profile of v7, /device:TPU:0, one launch (start us, length us, event | category | flops | bytes accessed | tf_op | source)
XLA Modules:
  0.0 565.4 jit_solution(2308689573376151125)
XLA Ops:
  0.7 0.0 copy-start
  0.7 0.7 fusion.4
  1.4 0.1 fusion.2
  1.5 0.7 fusion.3
  2.2 0.0 copy-done
  2.2 0.0 copy-start.2
  2.2 0.1 fusion.1
  2.4 1.0 copy.43.spots
  3.4 1.9 fusion
  5.3 1.3 pad_maximum_fusion
  6.6 0.0 copy-done.2
  6.6 230.7 %front.1 = (bf16[8,128,2048]{2,1,0:T(8,128)(2,1)}, bf16[2,4,2048,128]{3,2,1,0:T(8,128)(2,1)}, bf16[2,3,2048,512]{3,2,1,0:T(8,128)(2,1)}, bf16[8,128,2048]{2,1,0:...) custom-call(bf16[2,256,2048]{2,1,0:T(8,128)(2,1)} %tok_ref.3, ...), custom_call_target="tpu_custom_call" | custom-call | tf_op jit(solution)/shard_map/front/pallas_call | solution.py:1242
  237.3 35.2 %hidden.1 = (bf16[1024,2048]{1,0:T(8,128)(2,1)}, bf16[3,1024,1024]{2,1,0:T(8,128)(2,1)}) custom-call(bf16[1024,2048]{1,0:T(8,128)(2,1)} %bitcast.18, bf16[1024,2048]{1,0:T(8,128)(2,1)} %bitcast.19, bf16[2,3,2048,512]{3,2,1,0:T(8,128)(2,1)} %get-tuple-element.63.w.ffw_ref), custom_call_target="tpu_custom_call" | custom-call | tf_op jit(solution)/shard_map/hidden/pallas_call | solution.py:1286
  272.5 262.9 %back.1 = (bf16[4,128,2048]{2,1,0:T(8,128)(2,1)}, bf16[4,128,2048]{2,1,0:T(8,128)(2,1)}, bf16[4,256,512]{2,1,0:T(8,128)(2,1)}, bf16[3,256,2048]{2,1,0:T(8,128)(2...) custom-call(bf16[8,128,2048]{2,1,0:T(8,128)(2,1)} %get-tuple-element.61.a2_ref, ...), custom_call_target="tpu_custom_call" | custom-call | tf_op jit(solution)/shard_map/back/pallas_call | solution.py:1301
  535.4 1.2 slice.3
  536.6 0.0 copy-start.1
  536.6 28.6 %finish.1 = (f32[3,256,512]{2,1,0:T(8,128)}, f32[256,512]{1,0:T(8,128)}, f32[2,256,2048]{2,1,0:T(8,128)}, f32[256,2048]{1,0:T(8,128)}, f32[3,256,512]{2,1,0:T(8,...) custom-call(f32[8,128]{1,0:T(8,128)} %get-tuple-element.72.norm_ref,, ...), custom_call_target="tpu_custom_call" | custom-call | tf_op jit(solution)/shard_map/finish/pallas_call | solution.py:1352
  565.2 0.0 copy-done.1
  (5 shorter events, 0.1 us)
Async XLA Ops:
  0.7 1.5 copy-start
  2.2 4.4 copy-start.2
  536.6 28.6 %copy-start.1 = (s32[2,1024]{1,0:T(2,128)S(1)}, s32[2,1024]{1,0:T(2,128)}, u32[]{:S(2)}) copy-start(s32[2,1024]{1,0:T(2,128)} %param.19) | copy-start | bytes 24580

commit v8 on v7

--- a/solution.py
+++ b/solution.py
@@ -696,6 +696,7 @@
         swap_ff = Swap(at, ff_low, ffw_ref, s5, r5, l5)
         spread_att = Spread(at, attw_ref, s6, r6)
         spread_ff = Spread(at, ffw_ref, s7, r7)
+        at.greet([at.core, *at.all_z(), *at.all_xy()])
         loads[0].wait()
 
         def norm_one(rows):
@@ -705,7 +706,6 @@
         loads[1].wait()
         loads[2].wait()
         recast(att_wide, att_low)
-        at.greet([at.core, *at.all_z(), *at.all_xy()])
         swap_att.start()
         gather.start()
         spread_att.start(swap_att.arrived(0))
@@ -932,7 +932,6 @@
 
         collect_att.start(0)
         scatter.pass_on(range(n_c - 1, n_c - 2, -1))
-        give_ff.start(2)
         load(*((ffw_ref.at[y, 2], wide.at[0, :, pl.ds(y * columns, columns)]) for y in range(heads)))
 
         @pl.loop(0, 4)
@@ -942,6 +941,7 @@
             rows_one[:, :, cols] = value.reshape(rows_one.shape[0], rows_one.shape[1], width)
 
         branch.start()
+        give_ff.start(2)
         share_block = Share(at, block, out_ref, s6.at[0], r6.at[0], l6.at[0])
         share_input = Share(at, low, input_ref, s6.at[1], r6.at[1], l6.at[1])
         scatter.pass_on(range(n_c - 2, 1, -1))

time: 566 us -> 564 us (level)
  no operation moved by 1% of the time
where the time goes in v8:
time: 564 us
  Pallas kernels  556 us (99%)
    pallas_call x1, Pallas kernels, shards(): call(back_kernel, 'back', 1, (jax.ShapeDtypeStruct((n_t, half, width), BF...  263 us
    pallas_call x1, Pallas kernels, shards(): call(front_kernel, 'front', 0, (rows_bf, att_full, ff_full, rows_bf, rows...  230 us
    pallas_call x1, Pallas kernels, shards(): pl.pallas_call(hidden_kernel, grid=(2 * tiles,), out_shape=(rows_flat, ja...  35.2 us
    pallas_call x1, Pallas kernels, shards(): pl.pallas_call(finish_kernel, out_shape=(*(jax.ShapeDtypeStruct(w.shape,...  28.6 us

profile of v8, /device:TPU:0, one launch (start us, length us, event | category | flops | bytes accessed | tf_op | source)
XLA Modules:
  0.0 564.1 jit_solution(3109841527069959730)
XLA Ops:
  0.7 0.0 copy-start
  0.7 0.7 fusion.4
  1.4 0.1 fusion.2
  1.5 0.7 fusion.3
  2.2 0.0 copy-done
  2.2 0.0 copy-start.2
  2.2 0.1 fusion.1
  2.4 1.0 copy.43.spots
  3.4 1.9 fusion
  5.3 1.3 pad_maximum_fusion
  6.6 0.0 copy-done.2
  6.6 229.6 %front.1 = (bf16[8,128,2048]{2,1,0:T(8,128)(2,1)}, bf16[2,4,2048,128]{3,2,1,0:T(8,128)(2,1)}, bf16[2,3,2048,512]{3,2,1,0:T(8,128)(2,1)}, bf16[8,128,2048]{2,1,0:...) custom-call(bf16[2,256,2048]{2,1,0:T(8,128)(2,1)} %tok_ref.3, ...), custom_call_target="tpu_custom_call" | custom-call | tf_op jit(solution)/shard_map/front/pallas_call | solution.py:1242
  236.2 35.2 %hidden.1 = (bf16[1024,2048]{1,0:T(8,128)(2,1)}, bf16[3,1024,1024]{2,1,0:T(8,128)(2,1)}) custom-call(bf16[1024,2048]{1,0:T(8,128)(2,1)} %bitcast.18, bf16[1024,2048]{1,0:T(8,128)(2,1)} %bitcast.19, bf16[2,3,2048,512]{3,2,1,0:T(8,128)(2,1)} %get-tuple-element.63.w.ffw_ref), custom_call_target="tpu_custom_call" | custom-call | tf_op jit(solution)/shard_map/hidden/pallas_call | solution.py:1286
  271.5 262.6 %back.1 = (bf16[4,128,2048]{2,1,0:T(8,128)(2,1)}, bf16[4,128,2048]{2,1,0:T(8,128)(2,1)}, bf16[4,256,512]{2,1,0:T(8,128)(2,1)}, bf16[3,256,2048]{2,1,0:T(8,128)(2...) custom-call(bf16[8,128,2048]{2,1,0:T(8,128)(2,1)} %get-tuple-element.61.a2_ref, ...), custom_call_target="tpu_custom_call" | custom-call | tf_op jit(solution)/shard_map/back/pallas_call | solution.py:1301
  534.1 1.2 slice.3
  535.3 0.0 copy-start.1
  535.3 28.6 %finish.1 = (f32[3,256,512]{2,1,0:T(8,128)}, f32[256,512]{1,0:T(8,128)}, f32[2,256,2048]{2,1,0:T(8,128)}, f32[256,2048]{1,0:T(8,128)}, f32[3,256,512]{2,1,0:T(8,...) custom-call(f32[8,128]{1,0:T(8,128)} %get-tuple-element.72.norm_ref,, ...), custom_call_target="tpu_custom_call" | custom-call | tf_op jit(solution)/shard_map/finish/pallas_call | solution.py:1352
  563.9 0.0 copy-done.1
  (5 shorter events, 0.1 us)
Async XLA Ops:
  0.7 1.5 copy-start
  2.2 4.4 copy-start.2
  535.3 28.6 %copy-start.1 = (s32[2,1024]{1,0:T(2,128)S(1)}, s32[2,1024]{1,0:T(2,128)}, u32[]{:S(2)}) copy-start(s32[2,1024]{1,0:T(2,128)} %param.19) | copy-start | bytes 24580
